TPU v7x, 32 devices: a whole 2x2x4 slice. The times are simulated.
32 devices in a mesh: ctx: 4 (over z), dp: 4 (over x, core), adv: 2 (over y).
Axes of the slice: x: 2, y: 2, z: 4, core: 2. Of those that a mesh axis runs over, the one named last changes fastest.
Arguments:
- hidden: bfloat16 [2, 4, 512, 4096], P('adv', 'dp', 'ctx'), may hold values from -6 to 6
- queries: bfloat16 [2, 4, 512, 4096], P('adv', 'dp', 'ctx'), may hold values from -48 to 48
- keys: bfloat16 [2, 4, 512, 1024], P('adv', 'dp', 'ctx'), may hold values from -4.5 to 4.5
- targets: bfloat16 [2, 4, 512, 4096], P('adv', 'dp', None, 'ctx'), may hold values from -6 to 6
- lengths: int32 [2, 4, 8], P('adv', 'dp'), may hold values from 1 to 128, 512 in all within a row
- value_matrix: bfloat16 [4096, 1024], replicated, may hold values from -0.09375 to 0.09375
- attacker_down_factor: bfloat16 [4096, 16], replicated, may hold values from -0.09375 to 0.09375
- attacker_up_factor: bfloat16 [16, 1024], replicated, may hold values from -1.5 to 1.5
Outputs:
- outer_grad: float32 [4096, 1024], P('ctx', 'dp')
Inputs may be any that keep to these rules, and one draw needn't show every extreme that they name: The 8 lengths of a sequence sum to 512, and the longest is exactly a quarter of 512.
All inputs are finite; a program needn't handle non-finite values.
Results may differ from a plain program's by a relative error of at most 0.008.
Values may be sent and summed in bfloat16 or wider, within the bound.
No kernel may reach another device: no remote copies, remote signals or barrier semaphores. Data moves between devices by JAX's collectives and lax.ppermute only.
A program may use at most 128 MiB of HBM per device.

v0:
```python
import jax
import jax.numpy as jnp
from jax import lax
from jax.sharding import PartitionSpec as P

HD = 128
GROUP = 4


ATTACK_STEP = 0.01


def doc_ids(lengths, seq):
    ends = jnp.cumsum(lengths)
    position = jnp.arange(seq, dtype=jnp.int32)
    return jnp.sum((position[:, None] >= ends[None, :]).astype(jnp.int32), axis=1)


def widen(array):
    rows = array.shape[0]
    heads = array.shape[1] // HD
    spread_out = jnp.repeat(array.reshape(rows, heads, HD), GROUP, axis=1)
    return spread_out.reshape(rows, heads * GROUP * HD)


def weight_blocks(q_heads, k_heads, docs):
    seq = q_heads.shape[0]
    block = seq // 8
    scale = HD ** (-0.5)
    position = jnp.arange(seq, dtype=jnp.int32)
    blocks = []
    for index in range(8):
        start = index * block
        stop = start + block
        scores = (
            jnp.einsum(
                "qhd,khd->hqk",
                q_heads[start:stop],
                k_heads[:stop],
                preferred_element_type=jnp.float32,
            )
            * scale
        )
        visible = (docs[start:stop, None] == docs[None, :stop]) & (
            position[None, :stop] <= position[start:stop, None]
        )
        scores = jnp.where(visible[None], scores, -1e30)
        top = jnp.max(scores, axis=2, keepdims=True)
        expo = jnp.exp(scores - top)
        blocks.append((expo / jnp.sum(expo, axis=2, keepdims=True)).astype(jnp.bfloat16))
    return blocks


def value_pass(blocks, v_heads, y_heads, factor):
    seq = v_heads.shape[0]
    block = seq // 8
    total = jnp.zeros(v_heads.shape, jnp.float32)
    for index in range(8):
        probs = blocks[index]
        start = index * block
        stop = start + block
        attn = jnp.einsum("hqk,khd->qhd", probs, v_heads[:stop], preferred_element_type=jnp.float32)
        d_attn = (factor * (attn - y_heads[start:stop].astype(jnp.float32))).astype(jnp.bfloat16)
        total = total.at[:stop].add(
            jnp.einsum("hqk,qhd->khd", probs, d_attn, preferred_element_type=jnp.float32)
        )
    return total.astype(jnp.bfloat16)


def body(
    hidden, queries, keys, targets, lengths, value_matrix, attacker_down_factor, attacker_up_factor
):
    token_rows = hidden.shape[2]
    value_span = value_matrix.shape[1]
    n_ctx = lax.axis_size("ctx")
    seq = token_rows * n_ctx
    factor = float(lax.axis_size("dp") * seq) ** (-0.5)
    hidden_state_rows = hidden[0, 0]
    q_seq, k_seq = (
        lax.all_to_all(queries[0, 0], "ctx", split_axis=1, concat_axis=0, tiled=True),
        lax.all_to_all(widen(keys[0, 0]), "ctx", split_axis=1, concat_axis=0, tiled=True),
    )
    local_heads = q_seq.shape[1] // HD
    q_heads = q_seq.reshape(seq, local_heads, HD)
    k_heads = k_seq.reshape(seq, local_heads, HD)
    docs = doc_ids(lengths[0, 0], seq)
    blocks = weight_blocks(q_heads, k_heads, docs)
    y_heads = targets[0, 0].reshape(seq, local_heads, HD)
    starting_value = jnp.dot(hidden_state_rows, value_matrix, preferred_element_type=jnp.float32)
    reduce_over_rows = (((0,), (0,)), ((), ()))

    def value_weight_gradient(down_factor, up_factor, sign):
        attacker_input = jnp.dot(
            hidden_state_rows, down_factor, preferred_element_type=jnp.float32
        ).astype(jnp.bfloat16)
        value_rows = (
            starting_value + jnp.dot(attacker_input, up_factor, preferred_element_type=jnp.float32)
        ).astype(jnp.bfloat16)
        v_seq = lax.all_to_all(widen(value_rows), "ctx", split_axis=1, concat_axis=0, tiled=True)
        head_grads = value_pass(blocks, v_seq.reshape(seq, local_heads, HD), y_heads, sign * factor)
        back = lax.all_to_all(
            head_grads.reshape(seq, local_heads * HD),
            "ctx",
            split_axis=0,
            concat_axis=1,
            tiled=True,
        )
        grouped_rows = (
            back.reshape(token_rows, value_span // HD, GROUP, HD).astype(jnp.float32).sum(axis=2)
        )
        return (attacker_input, grouped_rows.reshape(token_rows, value_span).astype(jnp.bfloat16))

    attacker_input, leading_gradient = value_weight_gradient(
        attacker_down_factor, attacker_up_factor, 1.0
    )
    blended_output = lax.dot_general(
        leading_gradient,
        attacker_up_factor,
        (((1,), (1,)), ((), ())),
        preferred_element_type=jnp.float32,
    ).astype(jnp.bfloat16)
    down_gradient = lax.dot_general(
        hidden_state_rows, blended_output, reduce_over_rows, preferred_element_type=jnp.float32
    )
    up_gradient = lax.dot_general(
        attacker_input, leading_gradient, reduce_over_rows, preferred_element_type=jnp.float32
    )
    down_gradient, up_gradient = lax.psum((down_gradient, up_gradient), ("ctx", "dp"))
    count = down_gradient.size + up_gradient.size
    broadcast_rows = jnp.sqrt(
        (jnp.sum(down_gradient * down_gradient) + jnp.sum(up_gradient * up_gradient)) / count
        + 1e-06
    )
    stepped_down_factor = (
        attacker_down_factor.astype(jnp.float32) - ATTACK_STEP * down_gradient / broadcast_rows
    ).astype(jnp.bfloat16)
    stepped_up_factor = (
        attacker_up_factor.astype(jnp.float32) - ATTACK_STEP * up_gradient / broadcast_rows
    ).astype(jnp.bfloat16)
    unused, tamper = value_weight_gradient(stepped_down_factor, stepped_up_factor, -1.0)
    n_dp = lax.axis_size("dp")
    hidden_seq = lax.all_to_all(hidden_state_rows, "ctx", split_axis=1, concat_axis=0, tiled=True)
    hidden_all = lax.all_gather(hidden_seq, "dp", axis=0, tiled=True)
    grad_part = lax.all_to_all(tamper, "dp", split_axis=1, concat_axis=0, tiled=True)
    grad_all = lax.all_gather(grad_part, "ctx", axis=0, tiled=True)
    left = hidden_all.reshape(n_dp, n_ctx, token_rows, hidden_all.shape[1])
    right = grad_all.reshape(n_ctx, n_dp, token_rows, grad_all.shape[1])
    shares = jnp.einsum("dctx,cdty->xy", left, right, preferred_element_type=jnp.float32)
    total = lax.psum(shares, "adv")
    return total / lax.axis_size("adv")


def solution(mesh):
    placed = (
        P("adv", "dp", "ctx", None),
        P("adv", "dp", "ctx", None),
        P("adv", "dp", "ctx", None),
        P("adv", "dp", None, "ctx"),
        P("adv", "dp", None),
        P(),
        P(),
        P(),
    )
    return jax.shard_map(
        body, mesh=mesh, in_specs=placed, out_specs=P("ctx", "dp"), check_vma=False
    )
```

profile of v0, /device:TPU:0, one launch (start us, length us, event | category | flops | bytes accessed | tf_op | source)
XLA Modules:
  0.0 510.5 jit_solution(11649998353570647107)
XLA Ops:
  9.8 6.3 %all-to-all-start.2 = ((bf16[128,4,1024]{0,2,1:T(8,128)(2,1)}), bf16[128,4,1024]{0,2,1:T(8,128)(2,1)S(1)}, u32[]{:S(2)}, u32[]{:S(2)}) async-start(bf16[128,4,1024]{0,2,1:T(8,128)(2,1)} %bitcast.8), calls=%async_computation.2 | async-start | bytes 2097152 | tf_op jit(solution)/shard_map/all_to_all | solution.py:81
  16.5 4.7 fusion.113
  22.4 19.4 %all-to-all-done.2 = bf16[128,4,1024]{0,2,1:T(8,128)(2,1)S(1)} async-done(((bf16[128,4,1024]{0,2,1:T(8,128)(2,1)}), bf16[128,4,1024]{0,2,1:T(8,128)(2,1)S(1)}, u32[]{:S(2)}, u32[]{:S(2)}) %all-to-all-start.2) | async-done | bytes 1048608 | tf_op jit(solution)/shard_map/all_to_all | solution.py:81
  43.1 3.5 all-to-all-start
  59.7 12.2 %all-to-all-done = bf16[128,4,1024]{0,2,1:T(8,128)(2,1)S(1)} async-done(((bf16[128,4,1024]{0,2,1:T(8,128)(2,1)}), bf16[128,4,1024]{0,2,1:T(8,128)(2,1)S(1)}, u32[]{:S(2)}, u32[]{:S(2)}) %all-to-all-start) | async-done | bytes 1048608 | tf_op jit(solution)/shard_map/all_to_all | solution.py:99
  71.9 4.3 all-to-all-start.1
  87.7 13.7 %all-to-all-done.1 = bf16[128,4,1024]{2,0,1:T(8,128)(2,1)} async-done(((bf16[128,4,1024]{2,0,1:T(8,128)(2,1)}), bf16[128,4,1024]{2,0,1:T(8,128)(2,1)}, u32[]{:S(2)}, u32[]{:S(2)}) %all-to-all-start.1) | async-done | bytes 1048608 | tf_op jit(solution)/shard_map/all_to_all | solution.py:80
  157.5 3.7 fusion.21
  161.2 4.1 fusion.15
  165.3 4.3 fusion.13
  174.7 3.5 all-to-all-start.3
  179.6 23.9 %all-to-all-done.3 = bf16[4,128,1024]{2,1,0:T(8,128)(2,1)S(1)} async-done(((bf16[4,128,1024]{2,1,0:T(8,128)(2,1)}), bf16[4,128,1024]{2,1,0:T(8,128)(2,1)S(1)}, u32[]{:S(2)}, u32[]{:S(2)}) %all-to-all-start.3) | async-done | bytes 1048608 | tf_op jit(solution)/shard_map/all_to_all | solution.py:101
  204.5 3.5 all-to-all-start.7
  213.7 20.8 %all-to-all-done.7 = bf16[128,4,1024]{0,2,1:T(8,128)(2,1)S(1)} async-done(((bf16[128,4,1024]{0,2,1:T(8,128)(2,1)}), bf16[128,4,1024]{0,2,1:T(8,128)(2,1)S(1)}, u32[]{:S(2)}, u32[]{:S(2)}) %all-to-all-start.7) | async-done | bytes 1048608 | tf_op jit(solution)/shard_map/all_to_all | solution.py:142
  235.9 86.6 %all-reduce.8.cloned.1.call-done = (f32[4096,16]{0,1:T(8,128)}, f32[16,1024]{1,0:T(8,128)}) async-done(((f32[4096,16]{0,1:T(8,128)}, f32[16,1024]{1,0:T(8,128)}), (f32[4096,16]{0,1:T(8,128)}, f32[16,1024]{1,0:T(8,128)})) %all-reduce.8.cloned.1.call-update) | async-done | bytes 327696 | tf_op jit(solution)/shard_map/psum | solution.py:128
  329.0 29.4 %all_to_all.125 = bf16[128,4,1024]{0,2,1:T(8,128)(2,1)S(1)} all-to-all(bf16[128,4,1024]{0,2,1:T(8,128)(2,1)S(1)} %bitcast.377), channel_id=1, replica_groups=mesh['ctx'=4,'dp'=4,'adv'=2] {'ctx'}, dimensions={1} | all-to-all | bytes 2097152 | tf_op jit(solution)/shard_map/all_to_all | solution.py:99
  375.8 3.7 fusion.19
  379.6 3.8 fusion.14
  383.4 4.2 fusion.12
  391.9 27.2 %all_to_all.126 = bf16[4,128,1024]{2,1,0:T(8,128)(2,1)S(1)} all-to-all(bf16[4,128,1024]{2,1,0:T(8,128)(2,1)S(1)} %all_to_all.108), channel_id=1, replica_groups=mesh['ctx'=4,'dp'=4,'adv'=2] {'ctx'}, dimensions={0} | all-to-all | bytes 2097152 | tf_op jit(solution)/shard_map/all_to_all | solution.py:101
  420.0 9.1 %all_to_all.127 = bf16[128,4,256]{0,2,1:T(8,128)(2,1)S(1)} all-to-all(bf16[128,4,256]{0,2,1:T(8,128)(2,1)S(1)} %bitcast.403), channel_id=1, replica_groups=mesh['ctx'=4,'dp'=4,'adv'=2] {'dp'}, dimensions={1} | all-to-all | bytes 524288 | tf_op jit(solution)/shard_map/all_to_all | solution.py:144
  430.0 26.1 %all-gather.3.cloned.1.call-done = bf16[2048,256]{1,0:T(8,128)(2,1)} async-done(((bf16[512,256]{1,0:T(8,128)(2,1)}), bf16[2048,256]{1,0:T(8,128)(2,1)}) %all-gather.3.cloned.1.call-update) | async-done | bytes 1048592 | tf_op jit(solution)/shard_map/all_gather | solution.py:145
  456.1 4.8 fusion.26
  460.9 39.6 %all-reduce.6.cloned.1.call-done = f32[1024,256]{0,1:T(8,128)} async-done(((f32[1024,256]{0,1:T(8,128)}), f32[1024,256]{0,1:T(8,128)}) %all-reduce.6.cloned.1.call-update) | async-done | bytes 1048592 | tf_op jit(solution)/shard_map/psum | solution.py:149
  (196 shorter events, 131.5 us)
Async XLA Ops:
  7.4 8.8 %copy-start = (bf16[1,1,128,4096]{3,2,1,0:T(8,128)(2,1)S(1)}, bf16[1,1,128,4096]{3,2,1,0:T(8,128)(2,1)}, u32[]{:S(2)}) copy-start(bf16[1,1,128,4096]{3,2,1,0:T(8,128)(2,1)} %param.44) | copy-start | bytes 3145732
  7.4 8.8 %copy-start.11 = (bf16[4096,16]{0,1:T(8,128)(2,1)S(1)}, bf16[4096,16]{0,1:T(8,128)(2,1)}, u32[]{:S(2)}) copy-start(bf16[4096,16]{0,1:T(8,128)(2,1)} %param.50) | copy-start | bytes 393220
  9.8 32.1 %all-to-all-start.2 = ((bf16[128,4,1024]{0,2,1:T(8,128)(2,1)}), bf16[128,4,1024]{0,2,1:T(8,128)(2,1)S(1)}, u32[]{:S(2)}, u32[]{:S(2)}) async-start(bf16[128,4,1024]{0,2,1:T(8,128)(2,1)} %bitcast.8), calls=%async_computation.2 | async-start | bytes 2097152 | tf_op jit(solution)/shard_map/all_to_all | solution.py:81
  16.5 5.5 %copy-start.12 = (bf16[16,1024]{1,0:T(8,128)(2,1)S(1)}, bf16[16,1024]{1,0:T(8,128)(2,1)}, u32[]{:S(2)}) copy-start(bf16[16,1024]{1,0:T(8,128)(2,1)} %param.51) | copy-start | bytes 98308
  22.3 24.5 %copy-start.25 = (s32[1,1,8]{2,1,0:T(1,128)S(1)}, s32[1,1,8]{2,1,0:T(1,128)}, u32[]{:S(2)}) copy-start(s32[1,1,8]{2,1,0:T(1,128)} %param.48) | copy-start | bytes 100
  43.1 28.8 %all-to-all-start = ((bf16[128,4,1024]{0,2,1:T(8,128)(2,1)}), bf16[128,4,1024]{0,2,1:T(8,128)(2,1)S(1)}, u32[]{:S(2)}, u32[]{:S(2)}) async-start(bf16[128,4,1024]{0,2,1:T(8,128)(2,1)} %bitcast.376), calls=%async_computation | async-start | bytes 2097152 | tf_op jit(solution)/shard_map/all_to_all | solution.py:99
  46.6 5.7 %copy-start.24 = (s32[512]{0:T(512)}, s32[512]{0:T(512)S(1)}, u32[]{:S(2)}) copy-start(s32[512]{0:T(512)S(1)} %iota.29) | copy-start | bytes 6148
  47.0 11.9 %copy-start.18 = (s32[512]{0:T(512)}, s32[512]{0:T(512)S(1)}, u32[]{:S(2)}) copy-start(s32[512]{0:T(512)S(1)} %convert_reduce_fusion) | copy-start | bytes 6148
  52.6 6.3 %slice-start.5 = ((s32[512]{0:T(512)}), s32[64]{0:T(128)S(1)}, s32[]{:S(2)}) async-start(s32[512]{0:T(512)} %copy-done.23), calls=%async_computation.17 | async-start | bytes 1024 | tf_op jit(solution)/shard_map/slice | solution.py:45
  55.6 20.5 %slice-start.6 = ((s32[512]{0:T(512)}), s32[128]{0:T(128)S(1)}, s32[]{:S(2)}) async-start(s32[512]{0:T(512)} %copy-done.24), calls=%async_computation.18 | async-start | bytes 1024 | tf_op jit(solution)/shard_map/slice | solution.py:45
  55.6 21.2 %slice-start.3 = ((s32[512]{0:T(512)}), s32[192]{0:T(256)S(1)}, s32[]{:S(2)}) async-start(s32[512]{0:T(512)} %copy-done.21), calls=%async_computation.15 | async-start | bytes 2048 | tf_op jit(solution)/shard_map/slice | solution.py:45
  55.6 21.9 %slice-start.4 = ((s32[512]{0:T(512)}), s32[256]{0:T(256)S(1)}, s32[]{:S(2)}) async-start(s32[512]{0:T(512)} %copy-done.22), calls=%async_computation.16 | async-start | bytes 2048 | tf_op jit(solution)/shard_map/slice | solution.py:45
  58.9 17.2 %slice-start = ((s32[512]{0:T(512)}), s32[128]{0:T(128)S(1)}, s32[]{:S(2)}) async-start(s32[512]{0:T(512)} %copy-done.18), calls=%async_computation.12 | async-start | bytes 1024 | tf_op jit(solution)/shard_map/slice | solution.py:44
  58.9 17.9 %slice-start.1 = ((s32[512]{0:T(512)}), s32[192]{0:T(256)S(1)}, s32[]{:S(2)}) async-start(s32[512]{0:T(512)} %copy-done.18), calls=%async_computation.13 | async-start | bytes 2048 | tf_op jit(solution)/shard_map/slice | solution.py:44
  58.9 18.6 %slice-start.2 = ((s32[512]{0:T(512)}), s32[256]{0:T(256)S(1)}, s32[]{:S(2)}) async-start(s32[512]{0:T(512)} %copy-done.18), calls=%async_computation.14 | async-start | bytes 2048 | tf_op jit(solution)/shard_map/slice | solution.py:44
  59.0 18.7 %copy-start.19 = (s32[512]{0:T(512)S(1)}, s32[512]{0:T(512)}, u32[]{:S(2)}) copy-start(s32[512]{0:T(512)} %copy-done.18) | copy-start | bytes 6148
  71.9 29.6 %all-to-all-start.1 = ((bf16[128,4,1024]{2,0,1:T(8,128)(2,1)}), bf16[128,4,1024]{2,0,1:T(8,128)(2,1)}, u32[]{:S(2)}, u32[]{:S(2)}) async-start(bf16[128,4,1024]{2,0,1:T(8,128)(2,1)} %copy.314), calls=%async_computation.1 | async-start | bytes 2097152 | tf_op jit(solution)/shard_map/all_to_all | solution.py:80
  174.7 28.8 %all-to-all-start.3 = ((bf16[4,128,1024]{2,1,0:T(8,128)(2,1)}), bf16[4,128,1024]{2,1,0:T(8,128)(2,1)S(1)}, u32[]{:S(2)}, u32[]{:S(2)}) async-start(bf16[4,128,1024]{2,1,0:T(8,128)(2,1)} %all_to_all.103), calls=%async_computation.3 | async-start | bytes 2097152 | tf_op jit(solution)/shard_map/all_to_all | solution.py:101
  204.5 30.0 %all-to-all-start.7 = ((bf16[128,4,1024]{0,2,1:T(8,128)(2,1)}), bf16[128,4,1024]{0,2,1:T(8,128)(2,1)S(1)}, u32[]{:S(2)}, u32[]{:S(2)}) async-start(bf16[128,4,1024]{0,2,1:T(8,128)(2,1)} %bitcast.58), calls=%async_computation.7 | async-start | bytes 2097152 | tf_op jit(solution)/shard_map/all_to_all | solution.py:142
  208.0 114.5 %all-reduce.8.cloned.1.call-start = ((), (), s32[]{:S(2)}) async-start(), calls=%async_computation.11 | async-start | bytes 655360 | tf_op jit(solution)/shard_map/psum | solution.py:128
  213.6 113.3 %copy-start.2 = (f32[128,1024]{1,0:T(8,128)S(1)}, f32[128,1024]{1,0:T(8,128)}, u32[]{:S(2)}) copy-start(f32[128,1024]{1,0:T(8,128)} %copy-done.1) | copy-start | bytes 1572868
  213.6 216.3 %all-gather.5.cloned.1.call-start = ((), (), s32[]{:S(2)}) async-start(), calls=%async_computation.9 | async-start | bytes 5242880 | tf_op jit(solution)/shard_map/all_gather | solution.py:143
  235.8 220.2 %all-gather.3.cloned.1.call-start = ((), (), s32[]{:S(2)}) async-start(), calls=%async_computation.8 | async-start | bytes 1310720 | tf_op jit(solution)/shard_map/all_gather | solution.py:145
  429.9 70.5 %all-reduce.6.cloned.1.call-start = ((), (), s32[]{:S(2)}) async-start(), calls=%async_computation.10 | async-start | bytes 2097152 | tf_op jit(solution)/shard_map/psum | solution.py:149
  (21 other events, 74.1 us)
Sparse Core Ops, SparseCore 0:
  213.8 108.6 all-reduce.7
  461.0 39.4 all-reduce.5
Sparse Core Ops, SparseCore 1:
  235.9 33.3 all-gather.4
  430.0 26.0 all-gather.2
where the time goes:
time: 512 us; the launch traced here: 510 us
  waiting for transfers between devices  242 us (47%)
  matrix products  87.7 us (17%)
  local copies, waits for them, and re-layouts  67.1 us (13%)
  blocking collectives  65.7 us (13%)
  starting transfers between devices  21.3 us (4%)
  between operations  16.7 us (3%)
  other arithmetic  9.65 us (2%)
    psum x1, waiting for transfers between devices, body(): lax.psum((down_gradient, up_gradient), ('ctx', 'dp'))  86.6 us
    dot_general x16, matrix products, value_pass(): jnp.einsum('hqk,qhd->khd', probs, d_attn, preferred_element_type=jnp.floa...  53 us
    psum x1, waiting for transfers between devices, body(): total = lax.psum(shares, 'adv')  39.6 us
    all_to_all x1, blocking collectives, value_weight_gradient(): lax.all_to_all(widen(value_rows), 'ctx', split_axis=1, concat_axis=0, til...  29.4 us
    all_to_all x1, blocking collectives, value_weight_gradient(): lax.all_to_all(head_grads.reshape(seq, local_heads * HD), 'ctx', split_ax...  27.2 us
    all_gather x1, waiting for transfers between devices, body(): grad_all = lax.all_gather(grad_part, 'ctx', axis=0, tiled=True)  26.1 us
    all_to_all x1, waiting for transfers between devices, value_weight_gradient(): lax.all_to_all(head_grads.reshape(seq, local_heads * HD), 'ctx', split_ax...  23.9 us
    unnamed x77, local copies, waits for them, and re-layouts  21.1 us
  transfers between devices with their start and end apart: 9, of which 8 were waited for; matrix products, arithmetic and copies ran while one was open for 15% of the time, Pallas kernels for 0%

commit v1 on v0

--- a/solution.py
+++ b/solution.py
@@ -1,6 +1,9 @@
+import functools
 import jax
 import jax.numpy as jnp
 from jax import lax
+from jax.experimental import pallas as pl
+from jax.experimental.pallas import tpu as pltpu
 from jax.sharding import PartitionSpec as P
 
 HD = 128
@@ -8,6 +11,232 @@
 
 
 ATTACK_STEP = 0.01
+
+BF16 = jnp.bfloat16
+F32 = jnp.float32
+
+
+def dot(a, b, da, db):
+    return lax.dot_general(a, b, (((da,), (db,)), ((), ())), preferred_element_type=F32)
+
+
+def whole(shape):
+    return pl.BlockSpec(shape, lambda *_: (0,) * len(shape))
+
+
+def gram_kernel(len_ref, q_ref, k_ref, y_ref, g_ref, z_ref, g_acc, z_acc, *, docs, block, reach):
+    seq = k_ref.shape[0]
+    scale = HD ** (-0.5)
+    ends, total = [], jnp.int32(0)
+    for j in range(docs):
+        total = total + len_ref[j]
+        ends.append(total)
+    g_acc[...] = jnp.zeros_like(g_acc)
+    z_acc[...] = jnp.zeros_like(z_acc)
+    for i in range(seq // block):
+        at, hi = i * block, (i + 1) * block
+        lo = max(0, at - reach)
+        heads = [slice(h * HD, (h + 1) * HD) for h in range(GROUP)]
+        q = jnp.concatenate([q_ref[at:hi, h] for h in heads], axis=0)
+        y = jnp.concatenate([y_ref[at:hi, h] for h in heads], axis=0)
+        scores = dot(q, k_ref[lo:hi, :], 1, 1) * scale
+        row = lax.broadcasted_iota(jnp.int32, (block, 1), 0) + at
+        first = jnp.zeros((block, 1), jnp.int32)
+        for end in ends:
+            first = jnp.where(row >= end, end, first)
+        col = lax.broadcasted_iota(jnp.int32, (block, hi - lo), 1) + lo
+        visible = (col >= first) & (col <= row)
+        scores = scores.reshape(GROUP, block, hi - lo)
+        scores = jnp.where(visible[None], scores, -1e30)
+        top = jnp.max(scores, axis=2, keepdims=True)
+        expo = jnp.exp(scores - top)
+        probs = expo * (1.0 / jnp.sum(expo, axis=2, keepdims=True))
+        probs = probs.reshape(GROUP * block, hi - lo).astype(BF16)
+        g_acc[lo:hi, lo:hi] += dot(probs, probs, 0, 0)
+        z_acc[lo:hi, :] += dot(probs, y, 0, 0)
+    g_ref[0] = g_acc[...].astype(BF16)
+    z_ref[...] = z_acc[...]
+
+
+def gram(lengths, qk, targets):
+    seq, width = targets.shape
+    groups = width // (GROUP * HD)
+    span = GROUP * HD
+    return pl.pallas_call(
+        functools.partial(gram_kernel, docs=lengths.shape[0], block=seq // 4, reach=seq // 4),
+        grid=(groups,),
+        in_specs=[
+            pl.BlockSpec(memory_space=pltpu.SMEM),
+            pl.BlockSpec((seq, span), lambda g: (0, g)),
+            pl.BlockSpec((seq, HD), lambda g: (0, groups * GROUP + g)),
+            pl.BlockSpec((seq, span), lambda g: (0, g)),
+        ],
+        out_specs=[
+            pl.BlockSpec((1, seq, seq), lambda g: (g, 0, 0)),
+            pl.BlockSpec((seq, HD), lambda g: (0, g)),
+        ],
+        out_shape=[
+            jax.ShapeDtypeStruct((groups, seq, seq), BF16),
+            jax.ShapeDtypeStruct((seq, groups * HD), F32),
+        ],
+        scratch_shapes=[pltpu.VMEM((seq, seq), F32), pltpu.VMEM((seq, HD), F32)],
+        cost_estimate=pl.CostEstimate(
+            flops=600_000_000, bytes_accessed=5_000_000, transcendentals=1_100_000
+        ),
+        name="gram",
+    )(lengths, qk, qk, targets)
+
+
+def first_kernel(g_ref, z_ref, v_ref, low_ref, up_ref, grad_ref, mixed_ref, up_grad_ref, *, factor):
+    for g in range(g_ref.shape[0]):
+        cols = slice(g * HD, (g + 1) * HD)
+        total = dot(g_ref[g], v_ref[:, cols], 1, 0) - z_ref[:, cols]
+        grad_ref[:, cols] = (factor * total).astype(BF16)
+    grad = grad_ref[...]
+    mixed_ref[...] = dot(up_ref[...], grad, 1, 1)
+    up_grad_ref[...] = dot(low_ref[...], grad, 1, 0)
+
+
+def first_pass(g, z, values, low_t, up, factor):
+    seq, width = values.shape
+    rank = up.shape[0]
+    return pl.pallas_call(
+        functools.partial(first_kernel, factor=factor),
+        out_shape=[
+            jax.ShapeDtypeStruct((seq, width), BF16),
+            jax.ShapeDtypeStruct((rank, seq), F32),
+            jax.ShapeDtypeStruct((rank, width), F32),
+        ],
+        cost_estimate=pl.CostEstimate(
+            flops=150_000_000, bytes_accessed=2_000_000, transcendentals=0
+        ),
+        name="first_pass",
+    )(g, z, values, low_t, up)
+
+
+def second_kernel(g_ref, grad_ref, low_ref, new_low_ref, up_ref, new_up_ref, out_ref, *, factor):
+    delta = dot(new_low_ref[...], new_up_ref[...], 0, 0) - dot(low_ref[...], up_ref[...], 0, 0)
+    delta = delta.astype(BF16)
+    for g in range(g_ref.shape[0]):
+        cols = slice(g * HD, (g + 1) * HD)
+        moved = factor * dot(g_ref[g], delta[:, cols], 1, 0)
+        out_ref[:, cols] = (-(grad_ref[:, cols].astype(F32) + moved)).astype(BF16)
+
+
+def second_pass(g, grad, low_t, new_low_t, up, new_up, factor):
+    return pl.pallas_call(
+        functools.partial(second_kernel, factor=factor),
+        out_shape=jax.ShapeDtypeStruct(grad.shape, BF16),
+        cost_estimate=pl.CostEstimate(
+            flops=150_000_000, bytes_accessed=2_000_000, transcendentals=0
+        ),
+        name="second_pass",
+    )(g, grad, low_t, new_low_t, up, new_up)
+
+
+def exchange(array, axis):
+    return lax.all_to_all(array, axis, split_axis=0, concat_axis=0, tiled=True)
+
+
+def everyone(array, axis):
+    count = lax.axis_size(axis)
+    return exchange(jnp.broadcast_to(array[None], (count,) + array.shape), axis)
+
+
+def by_columns(array, parts):
+    rows, width = array.shape
+    return array.reshape(rows, parts, width // parts).transpose(1, 0, 2)
+
+
+def swap(array, axis, bit):
+    count = lax.axis_size(axis)
+    return lax.ppermute(array, axis, [(i, i ^ bit) for i in range(count)])
+
+
+def sum_over(array, axis):
+    bit = 1
+    while bit < lax.axis_size(axis):
+        array = array + swap(array, axis, bit)
+        bit *= 2
+    return array
+
+
+def body(
+    hidden, queries, keys, targets, lengths, value_matrix, attacker_down_factor, attacker_up_factor
+):
+    n_ctx, n_dp = lax.axis_size("ctx"), lax.axis_size("dp")
+    rows, width = hidden.shape[2:]
+    seq = rows * n_ctx
+    value_span = value_matrix.shape[1]
+    rank = attacker_up_factor.shape[0]
+    factor = float(n_dp * seq) ** (-0.5)
+    own = value_span // n_ctx
+    ctx, dp = lax.axis_index("ctx"), lax.axis_index("dp")
+    h = hidden[0, 0]
+    up_own = lax.dynamic_slice_in_dim(attacker_up_factor, ctx * own, own, axis=1)
+
+    qk = exchange(
+        jnp.concatenate([by_columns(queries[0, 0], n_ctx), by_columns(keys[0, 0], n_ctx)], axis=2),
+        "ctx",
+    ).reshape(seq, -1)
+    base = dot(h, value_matrix, 1, 0)
+    low_t = dot(attacker_down_factor, h, 0, 1).astype(BF16)
+    values = (base + dot(low_t, attacker_up_factor, 0, 0)).astype(BF16)
+    carried = jnp.concatenate(
+        [
+            by_columns(values, n_ctx),
+            jnp.broadcast_to(
+                jnp.pad(low_t, ((0, 0), (0, own - rows)))[None], (n_ctx, rank, own)
+            ),
+        ],
+        axis=1,
+    )
+    carried = exchange(carried, "ctx")
+    v_seq = carried[:, :rows].reshape(seq, own)
+    low_all = carried[:, rows:, :rows].transpose(1, 0, 2).reshape(rank, seq)
+    h_cols = exchange(by_columns(h, n_ctx), "ctx").reshape(seq, width // n_ctx)
+
+    g, z = gram(lengths[0, 0], qk, targets[0, 0])
+    grad, mixed_t, up_grad = first_pass(g, z, v_seq, low_all, up_own, factor)
+    mixed_t = everyone(mixed_t, "ctx").sum(axis=0).astype(BF16)
+    down_grad = dot(mixed_t, h_cols, 1, 0)
+    low_rank = sum_over(jnp.concatenate([down_grad, up_grad], axis=1), "dp")
+    down_grad, up_grad = low_rank[:, : width // n_ctx], low_rank[:, width // n_ctx :]
+    squares = jnp.sum(low_rank * low_rank)
+    moved_t = dot(down_grad.astype(BF16), h_cols, 1, 1)
+    both = jnp.concatenate([moved_t, jnp.full((8, seq), squares)], axis=0)
+    both = everyone(both, "ctx").sum(axis=0)
+    moved_t, squares = both[:rank], both[rank, 0]
+    spread = jnp.sqrt(squares / (rank * (width + value_span)) + 1e-06)
+    step = ATTACK_STEP / spread
+    new_low = (low_all.astype(F32) - step * moved_t).astype(BF16)
+    new_up = (up_own.astype(F32) - step * up_grad).astype(BF16)
+    tamper = second_pass(g, grad, low_all, new_low, up_own, new_up, factor)
+
+    tampers = everyone(tamper, "ctx")
+    shares = lax.dot_general(
+        tampers, h_cols, (((1,), (0,)), ((), ())), preferred_element_type=F32
+    )
+    return finish(shares, dp, n_dp, value_span)
+
+
+def finish(shares, dp, n_dp, value_span):
+    rows = shares.shape[2]
+    blocks = shares.reshape(n_dp, value_span // n_dp, rows)
+    bit = n_dp // 2
+    low = 1
+    while low < n_dp:
+        pairs = blocks.reshape(blocks.shape[0] // 2, 2, *blocks.shape[1:])
+        mine = (dp // low) % 2
+        keep = lax.dynamic_index_in_dim(pairs, mine, 1, keepdims=False)
+        send = lax.dynamic_index_in_dim(pairs, 1 - mine, 1, keepdims=False)
+        blocks = keep + swap(send.astype(BF16), "dp", low).astype(F32)
+        low *= 2
+    total = blocks[0].astype(BF16)
+    n_adv = lax.axis_size("adv")
+    other = swap(total, "adv", 1)
+    out = (total.astype(F32) + other.astype(F32)) / n_adv
+    return out.T
 
 
 def doc_ids(lengths, seq):
@@ -67,7 +296,7 @@
     return total.astype(jnp.bfloat16)
 
 
-def body(
+def plain_body(
     hidden, queries, keys, targets, lengths, value_matrix, attacker_down_factor, attacker_up_factor
 ):
     token_rows = hidden.shape[2]
@@ -151,6 +380,7 @@
 
 
 def solution(mesh):
+    split = 8 % mesh.shape['ctx'] == 0 and mesh.shape['adv'] == 2
     placed = (
         P("adv", "dp", "ctx", None),
         P("adv", "dp", "ctx", None),
@@ -162,5 +392,5 @@
         P(),
     )
     return jax.shard_map(
-        body, mesh=mesh, in_specs=placed, out_specs=P("ctx", "dp"), check_vma=False
-    )
+        body if split else plain_body, mesh=mesh, in_specs=placed, out_specs=P("ctx", "dp"), check_vma=False
+    )

time: 512 us -> 197 us (0.38)
  waiting for transfers between devices: 242 us -> 118 us
  matrix products: 87.7 us -> 8.7 us
  blocking collectives: 65.7 us -> 9.78 us
  local copies, waits for them, and re-layouts: 67.1 us -> 15.5 us
  between operations: 16.7 us -> 0.96 us
  Pallas kernels: 0 us -> 12.3 us
    psum x2 -> x0, waiting for transfers between devices: 126 us -> none  [the longest x1 86.6 us: body(): lax.psum((down_gradient, up_gradient), ('ctx', 'dp'))]
    dot_general x23 -> x6, matrix products: 66.7 us -> 8.7 us  [the longest x5 7.45 us: dot(): lax.dot_general(a, b, (((da,), (db,)), ((), ())), preferred_element_type=...]
    all_to_all x3 -> x1, blocking collectives: 65.7 us -> 9.78 us  [exchange(): return lax.all_to_all(array, axis, split_axis=0, concat_axis=0, tiled=True)]
    ppermute x0 -> x5, waiting for transfers between devices: none -> 30.9 us  [swap(): return lax.ppermute(array, axis, [(i, i ^ bit) for i in range(count)])]
    all_gather x2 -> x0, waiting for transfers between devices: 26.1 us -> none  [the longest x1 26.1 us: body(): grad_all = lax.all_gather(grad_part, 'ctx', axis=0, tiled=True)]
    sub x8 -> x0, matrix products: 21 us -> none  [weight_blocks(): expo = jnp.exp(scores - top)]
    unnamed x77 -> x16, local copies, waits for them, and re-layouts: 21.1 us -> 3.96 us
    slice x38 -> x2, local copies, waits for them, and re-layouts: 16.4 us -> 1.26 us  [the longest x1 0.75 us: body(): v_seq = carried[:, :rows].reshape(seq, own)]
  transfers between devices with their start and end apart: 9 -> 10, of which waited for: 8 -> 10; matrix products, arithmetic and copies ran while one was open for 15% -> 3% of each run, Pallas kernels for 0% -> 0%
where the time goes in v1:
time: 197 us; the launch traced here: 196 us
  waiting for transfers between devices  118 us (60%)
  starting transfers between devices  25.1 us (13%)
  local copies, waits for them, and re-layouts  15.5 us (8%)
  Pallas kernels  12.3 us (6%)
  blocking collectives  9.78 us (5%)
  matrix products  8.7 us (4%)
  other arithmetic  5.98 us (3%)
    all_to_all x5, waiting for transfers between devices, exchange(): return lax.all_to_all(array, axis, split_axis=0, concat_axis=0, tiled=True)  87.1 us
    ppermute x5, waiting for transfers between devices, swap(): return lax.ppermute(array, axis, [(i, i ^ bit) for i in range(count)])  30.9 us
    all_to_all x5, starting transfers between devices, exchange(): return lax.all_to_all(array, axis, split_axis=0, concat_axis=0, tiled=True)  20.2 us
    all_to_all x1, blocking collectives, exchange(): return lax.all_to_all(array, axis, split_axis=0, concat_axis=0, tiled=True)  9.78 us
    dot_general x5, matrix products, dot(): lax.dot_general(a, b, (((da,), (db,)), ((), ())), preferred_element_type=...  7.45 us
    pallas_call x1, Pallas kernels, gram(): pl.pallas_call(functools.partial(gram_kernel, docs=lengths.shape[0], bloc...  6.85 us
    ppermute x5, starting transfers between devices, swap(): return lax.ppermute(array, axis, [(i, i ^ bit) for i in range(count)])  4.84 us
    unnamed x16, local copies, waits for them, and re-layouts  3.96 us
  transfers between devices with their start and end apart: 10, of which 10 were waited for; matrix products, arithmetic and copies ran while one was open for 3% of the time, Pallas kernels for 0%

profile of v1, /device:TPU:0, one launch (start us, length us, event | category | flops | bytes accessed | tf_op | source)
XLA Modules:
  0.0 196.4 jit_solution(16387583221635431071)
XLA Ops:
  0.9 1.6 convolution_convert_fusion
  2.5 5.0 %fusion.3 = f32[128,1024]{1,0:T(8,128)S(1)} fusion(bf16[4096,1024]{1,0:T(8,128)(2,1)} %param.13, bf16[1,1,128,4096]{3,2,1,0:T(8,128)(2,1)} %param.8), kind=kOutput, calls=%fused_computation.8 | convolution fusion | flops 1073741824 | bytes 9961472 | tf_op jit(solution)/shard_map/dot_general | solution.py:20
  8.6 6.3 %all-to-all-start.1 = ((bf16[4,144,256]{2,1,0:T(8,128)(2,1)}), bf16[4,144,256]{2,1,0:T(8,128)(2,1)S(1)}, u32[]{:S(2)}, u32[]{:S(2)}) async-start(bf16[4,144,256]{2,1,0:T(8,128)(2,1)} %pad_maximum_fusion.1), calls=%async_computation.1 | async-start | bytes 589824 | tf_op jit(solution)/shard_map/all_to_all | solution.py:138
  17.5 7.1 %all-to-all-done.1 = bf16[4,144,256]{2,1,0:T(8,128)(2,1)S(1)} async-done(((bf16[4,144,256]{2,1,0:T(8,128)(2,1)}), bf16[4,144,256]{2,1,0:T(8,128)(2,1)S(1)}, u32[]{:S(2)}, u32[]{:S(2)}) %all-to-all-start.1) | async-done | bytes 294944 | tf_op jit(solution)/shard_map/all_to_all | solution.py:138
  24.5 3.5 %all-to-all-start = ((bf16[4,128,1280]{2,1,0:T(8,128)(2,1)}), bf16[4,128,1280]{2,1,0:T(8,128)(2,1)S(1)}, u32[]{:S(2)}, u32[]{:S(2)}) async-start(bf16[4,128,1280]{2,1,0:T(8,128)(2,1)} %pad_maximum_fusion), calls=%async_computation | async-start | bytes 2621440 | tf_op jit(solution)/shard_map/all_to_all | solution.py:138
  30.0 27.8 %all-to-all-done = bf16[4,128,1280]{2,1,0:T(8,128)(2,1)S(1)} async-done(((bf16[4,128,1280]{2,1,0:T(8,128)(2,1)}), bf16[4,128,1280]{2,1,0:T(8,128)(2,1)S(1)}, u32[]{:S(2)}, u32[]{:S(2)}) %all-to-all-start) | async-done | bytes 1310752 | tf_op jit(solution)/shard_map/all_to_all | solution.py:138
  59.0 6.9 %gram.1 = (bf16[2,512,512]{2,1,0:T(8,128)(2,1)}, f32[512,256]{1,0:T(8,128)}) custom-call(s32[8]{0:T(128)} %bitcast.78, bf16[512,1280]{1,0:T(8,128)(2,1)} %bitcast.69, bf16[512,1280]{1,0:T(8,128)(2,1)} %bitcast.70, bf16[512,1024]{1,0:T(8,128)(2,1)} %bitcast.77), custom_call_target="tpu_custom_call" | custom-call | flops 600000000 | bytes 5000000 | tf_op jit(solution)/shard_map/gram/pallas_call | solution.py:65
  65.8 2.7 %first_pass.1 = (bf16[512,256]{1,0:T(8,128)(2,1)}, f32[16,512]{1,0:T(8,128)}, f32[16,256]{1,0:T(8,128)}) custom-call(bf16[2,512,512]{2,1,0:T(8,128)(2,1)} %get-tuple-element.10.g_ref, f32[512,256]{1,0:T(8,128)} %get-tuple-element.11.z_ref, bf16[512,256]{1,0:T(8,128)(2,1)} %bitcast.73, bf16[16,512]{1,0:T(8,128)(2,1)} %copy_bitcast_fusion.3.low_ref, ...), custom_call_target="tpu_custom_call" | custom-call | flops 150000000 | bytes 2000000 | tf_op jit(solution)/shard_map/first_pass/pallas_call | solution.py:103
  69.9 3.3 %all-to-all-start.2 = ((f32[4,16,512]{2,1,0:T(8,128)}), f32[4,16,512]{2,1,0:T(8,128)S(1)}, u32[]{:S(2)}, u32[]{:S(2)}) async-start(f32[4,16,512]{2,1,0:T(8,128)} %broadcast_in_dim.9), calls=%async_computation.2 | async-start | bytes 262144 | tf_op jit(solution)/shard_map/all_to_all | solution.py:138
  75.4 3.8 %all-to-all-done.2 = f32[4,16,512]{2,1,0:T(8,128)S(1)} async-done(((f32[4,16,512]{2,1,0:T(8,128)}), f32[4,16,512]{2,1,0:T(8,128)S(1)}, u32[]{:S(2)}, u32[]{:S(2)}) %all-to-all-start.2) | async-done | bytes 131104 | tf_op jit(solution)/shard_map/all_to_all | solution.py:138
  79.2 3.5 %all-to-all-start.3 = ((bf16[4,128,1024]{2,1,0:T(8,128)(2,1)}), bf16[4,128,1024]{2,1,0:T(8,128)(2,1)S(1)}, u32[]{:S(2)}, u32[]{:S(2)}) async-start(bf16[4,128,1024]{2,1,0:T(8,128)(2,1)} %bitcast.61), calls=%async_computation.3 | async-start | bytes 2097152 | tf_op jit(solution)/shard_map/all_to_all | solution.py:138
  82.7 24.1 %all-to-all-done.3 = bf16[4,128,1024]{2,1,0:T(8,128)(2,1)S(1)} async-done(((bf16[4,128,1024]{2,1,0:T(8,128)(2,1)}), bf16[4,128,1024]{2,1,0:T(8,128)(2,1)S(1)}, u32[]{:S(2)}, u32[]{:S(2)}) %all-to-all-start.3) | async-done | bytes 1048608 | tf_op jit(solution)/shard_map/all_to_all | solution.py:138
  110.0 3.0 %collective-permute-done.1 = f32[16,1280]{1,0:T(8,128)S(1)} collective-permute-done((f32[16,1280]{1,0:T(8,128)S(1)}, f32[16,1280]{1,0:T(8,128)S(1)}, u32[]{:S(2)}, u32[]{:S(2)}) %collective-permute-start.1) | collective-permute-done | bytes 81952 | tf_op jit(solution)/shard_map/ppermute | solution.py:153
  114.6 9.8 %all_to_all.30 = f32[4,24,512]{2,1,0:T(8,128)S(1)} all-to-all(f32[4,24,512]{2,1,0:T(8,128)S(1)} %broadcast_in_dim.10), channel_id=1, replica_groups=mesh['ctx'=4,'dp'=4,'adv'=2] {'ctx'}, dimensions={0} | all-to-all | bytes 393216 | tf_op jit(solution)/shard_map/all_to_all | solution.py:138
  126.7 2.7 %second_pass.1 = bf16[512,256]{1,0:T(8,128)(2,1)} custom-call(bf16[2,512,512]{2,1,0:T(8,128)(2,1)} %get-tuple-element.10.g_ref, bf16[512,256]{1,0:T(8,128)(2,1)} %get-tuple-element.12.grad_ref, bf16[16,512]{1,0:T(8,128)(2,1)} %copy_bitcast_fusion.3.low_ref, bf16[16,512]{1,0:T(8,128)(2,1)} %fusion.8.new_low_ref, ...), custom_call_target="tpu_custom_call" | custom-call | flops 150000000 | bytes 2000000 | tf_op jit(solution)/shard_map/second_pass/pallas_call | solution.py:127
  131.6 3.5 %all-to-all-start.5 = ((bf16[4,512,256]{1,2,0:T(8,128)(2,1)}), bf16[4,512,256]{1,2,0:T(8,128)(2,1)S(1)}, u32[]{:S(2)}, u32[]{:S(2)}) async-start(bf16[4,512,256]{1,2,0:T(8,128)(2,1)} %broadcast_in_dim.11), calls=%async_computation.5 | async-start | bytes 2097152 | tf_op jit(solution)/shard_map/all_to_all | solution.py:138
  135.1 24.4 %all-to-all-done.5 = bf16[4,512,256]{1,2,0:T(8,128)(2,1)S(1)} async-done(((bf16[4,512,256]{1,2,0:T(8,128)(2,1)}), bf16[4,512,256]{1,2,0:T(8,128)(2,1)S(1)}, u32[]{:S(2)}, u32[]{:S(2)}) %all-to-all-start.5) | async-done | bytes 1048608 | tf_op jit(solution)/shard_map/all_to_all | solution.py:138
  160.7 2.0 copy-done.2
  163.0 2.6 %collective-permute-done.2 = bf16[2,256,1024]{2,1,0:T(8,128)(2,1)S(1)} collective-permute-done((bf16[2,256,1024]{2,1,0:T(8,128)(2,1)S(1)}, bf16[2,256,1024]{2,1,0:T(8,128)(2,1)S(1)}, u32[]{:S(2)}, u32[]{:S(2)}) %collective-permute-start.2) | collective-permute-done | bytes 1048608 | tf_op jit(solution)/shard_map/ppermute | solution.py:153
  165.6 1.9 bitcast_add_fusion
  167.5 1.6 collective-permute-start.3
  169.1 12.5 %collective-permute-done.3 = bf16[1,256,1024]{2,1,0:T(8,128)(2,1)S(1)} collective-permute-done((bf16[1,256,1024]{2,1,0:T(8,128)(2,1)S(1)}, bf16[1,256,1024]{2,1,0:T(8,128)(2,1)S(1)}, u32[]{:S(2)}, u32[]{:S(2)}) %collective-permute-start.3) | collective-permute-done | bytes 524320 | tf_op jit(solution)/shard_map/ppermute | solution.py:153
  181.7 1.6 collective-permute-start.4
  183.3 11.6 %collective-permute-done.4 = bf16[256,1024]{1,0:T(8,128)(2,1)S(1)} collective-permute-done((bf16[256,1024]{1,0:T(8,128)(2,1)S(1)}, bf16[256,1024]{1,0:T(8,128)(2,1)S(1)}, u32[]{:S(2)}, u32[]{:S(2)}) %collective-permute-start.4) | collective-permute-done | bytes 524320 | tf_op jit(solution)/shard_map/ppermute | solution.py:153
  (55 shorter events, 22.8 us)
Async XLA Ops:
  0.0 0.9 copy-start
  2.5 5.0 %copy-start.6 = (bf16[16,1024]{1,0:T(8,128)(2,1)S(1)}, bf16[16,1024]{1,0:T(8,128)(2,1)}, u32[]{:S(2)}) copy-start(bf16[16,1024]{1,0:T(8,128)(2,1)} %param.15) | copy-start | bytes 98308
  7.5 7.4 %copy-start.5 = (bf16[1,1,128,1024]{3,2,1,0:T(8,128)(2,1)S(1)}, bf16[1,1,128,1024]{3,2,1,0:T(8,128)(2,1)}, u32[]{:S(2)}) copy-start(bf16[1,1,128,1024]{3,2,1,0:T(8,128)(2,1)} %param.10) | copy-start | bytes 786436
  7.5 7.6 %copy-start.4 = (bf16[1,1,128,4096]{3,2,1,0:T(8,128)(2,1)S(1)}, bf16[1,1,128,4096]{3,2,1,0:T(8,128)(2,1)}, u32[]{:S(2)}) copy-start(bf16[1,1,128,4096]{3,2,1,0:T(8,128)(2,1)} %param.9) | copy-start | bytes 3145732
  8.6 16.0 %all-to-all-start.1 = ((bf16[4,144,256]{2,1,0:T(8,128)(2,1)}), bf16[4,144,256]{2,1,0:T(8,128)(2,1)S(1)}, u32[]{:S(2)}, u32[]{:S(2)}) async-start(bf16[4,144,256]{2,1,0:T(8,128)(2,1)} %pad_maximum_fusion.1), calls=%async_computation.1 | async-start | bytes 589824 | tf_op jit(solution)/shard_map/all_to_all | solution.py:138
  24.5 33.3 %all-to-all-start = ((bf16[4,128,1280]{2,1,0:T(8,128)(2,1)}), bf16[4,128,1280]{2,1,0:T(8,128)(2,1)S(1)}, u32[]{:S(2)}, u32[]{:S(2)}) async-start(bf16[4,128,1280]{2,1,0:T(8,128)(2,1)} %pad_maximum_fusion), calls=%async_computation | async-start | bytes 2621440 | tf_op jit(solution)/shard_map/all_to_all | solution.py:138
  57.9 1.1 copy-start.3
  58.9 14.3 %copy-start.1 = (bf16[1,1,128,4096]{3,2,1,0:T(8,128)(2,1)S(1)}, bf16[1,1,128,4096]{3,2,1,0:T(8,128)(2,1)}, u32[]{:S(2)}) copy-start(bf16[1,1,128,4096]{3,2,1,0:T(8,128)(2,1)} %param.8) | copy-start | bytes 3145732
  69.9 9.2 %all-to-all-start.2 = ((f32[4,16,512]{2,1,0:T(8,128)}), f32[4,16,512]{2,1,0:T(8,128)S(1)}, u32[]{:S(2)}, u32[]{:S(2)}) async-start(f32[4,16,512]{2,1,0:T(8,128)} %broadcast_in_dim.9), calls=%async_computation.2 | async-start | bytes 262144 | tf_op jit(solution)/shard_map/all_to_all | solution.py:138
  74.1 33.0 %copy-start.7 = (f32[16,256]{1,0:T(8,128)S(1)}, f32[16,256]{1,0:T(8,128)}, u32[]{:S(2)}) copy-start(f32[16,256]{1,0:T(8,128)} %get-tuple-element.14) | copy-start | bytes 49156
  79.2 27.6 %all-to-all-start.3 = ((bf16[4,128,1024]{2,1,0:T(8,128)(2,1)}), bf16[4,128,1024]{2,1,0:T(8,128)(2,1)S(1)}, u32[]{:S(2)}, u32[]{:S(2)}) async-start(bf16[4,128,1024]{2,1,0:T(8,128)(2,1)} %bitcast.61), calls=%async_computation.3 | async-start | bytes 2097152 | tf_op jit(solution)/shard_map/all_to_all | solution.py:138
  107.1 1.3 collective-permute-start
  108.4 4.6 %collective-permute-start.1 = (f32[16,1280]{1,0:T(8,128)S(1)}, f32[16,1280]{1,0:T(8,128)S(1)}, u32[]{:S(2)}, u32[]{:S(2)}) collective-permute-start(f32[16,1280]{1,0:T(8,128)S(1)} %fusion.13), channel_id=1, source_target_pairs={{0,4},{2,6},{4,0},{6,2},{1,5},{3,7},{5,1},{7,3},{8,12},{10,14},{12... | collective-permute-start | bytes 245768 | tf_op jit(solution)/shard_map/ppermute | solution.py:153
  131.6 27.9 %all-to-all-start.5 = ((bf16[4,512,256]{1,2,0:T(8,128)(2,1)}), bf16[4,512,256]{1,2,0:T(8,128)(2,1)S(1)}, u32[]{:S(2)}, u32[]{:S(2)}) async-start(bf16[4,512,256]{1,2,0:T(8,128)(2,1)} %broadcast_in_dim.11), calls=%async_computation.5 | async-start | bytes 2097152 | tf_op jit(solution)/shard_map/all_to_all | solution.py:138
  160.7 2.0 copy-start.2
  162.8 2.7 %collective-permute-start.2 = (bf16[2,256,1024]{2,1,0:T(8,128)(2,1)S(1)}, bf16[2,256,1024]{2,1,0:T(8,128)(2,1)S(1)}, u32[]{:S(2)}, u32[]{:S(2)}) collective-permute-start(bf16[2,256,1024]{2,1,0:T(8,128)(2,1)S(1)} %fusion.1), channel_id=1, source_target_pairs={{0,2},{2,0},{4,6},{6,4},{1,3},{3,1},{5,7},{7,5},{8,10},{10,8},{12,... | collective-permute-start | bytes 3145736 | tf_op jit(solution)/shard_map/ppermute | solution.py:153
  167.5 14.0 %collective-permute-start.3 = (bf16[1,256,1024]{2,1,0:T(8,128)(2,1)S(1)}, bf16[1,256,1024]{2,1,0:T(8,128)(2,1)S(1)}, u32[]{:S(2)}, u32[]{:S(2)}) collective-permute-start(bf16[1,256,1024]{2,1,0:T(8,128)(2,1)S(1)} %dynamic-slice_convert_fusion.1), channel_id=1, source_target_pairs={{0,4},{2,6},{4,0},{6,2},{1,5},{3,7},{5,1},{7,3},{8,12},{10,14},{12... | collective-permute-start | bytes 1572872 | tf_op jit(solution)/shard_map/ppermute | solution.py:153
  181.7 13.2 %collective-permute-start.4 = (bf16[256,1024]{1,0:T(8,128)(2,1)S(1)}, bf16[256,1024]{1,0:T(8,128)(2,1)S(1)}, u32[]{:S(2)}, u32[]{:S(2)}) collective-permute-start(bf16[256,1024]{1,0:T(8,128)(2,1)S(1)} %fusion.5), channel_id=1, source_target_pairs={{0,1},{1,0},{2,3},{3,2},{4,5},{5,4},{6,7},{7,6},{8,9},{9,8},{10,11... | collective-permute-start | bytes 1572872 | tf_op jit(solution)/shard_map/ppermute | solution.py:153

commit v2 on v1

--- a/solution.py
+++ b/solution.py
@@ -14,14 +14,20 @@
 
 BF16 = jnp.bfloat16
 F32 = jnp.float32
+SMEM = pl.BlockSpec(memory_space=pltpu.SMEM)
+VMEM = pl.BlockSpec(memory_space=pltpu.VMEM)
 
 
 def dot(a, b, da, db):
     return lax.dot_general(a, b, (((da,), (db,)), ((), ())), preferred_element_type=F32)
 
 
-def whole(shape):
-    return pl.BlockSpec(shape, lambda *_: (0,) * len(shape))
+def cost(flops, size):
+    return pl.CostEstimate(flops=flops, bytes_accessed=size, transcendentals=0)
+
+
+def struct(shape, dtype):
+    return jax.ShapeDtypeStruct(shape, dtype)
 
 
 def gram_kernel(len_ref, q_ref, k_ref, y_ref, g_ref, z_ref, g_acc, z_acc, *, docs, block, reach):
@@ -66,7 +72,7 @@
         functools.partial(gram_kernel, docs=lengths.shape[0], block=seq // 4, reach=seq // 4),
         grid=(groups,),
         in_specs=[
-            pl.BlockSpec(memory_space=pltpu.SMEM),
+            SMEM,
             pl.BlockSpec((seq, span), lambda g: (0, g)),
             pl.BlockSpec((seq, HD), lambda g: (0, groups * GROUP + g)),
             pl.BlockSpec((seq, span), lambda g: (0, g)),
@@ -75,72 +81,267 @@
             pl.BlockSpec((1, seq, seq), lambda g: (g, 0, 0)),
             pl.BlockSpec((seq, HD), lambda g: (0, g)),
         ],
-        out_shape=[
-            jax.ShapeDtypeStruct((groups, seq, seq), BF16),
-            jax.ShapeDtypeStruct((seq, groups * HD), F32),
-        ],
+        out_shape=[struct((groups, seq, seq), BF16), struct((seq, groups * HD), F32)],
         scratch_shapes=[pltpu.VMEM((seq, seq), F32), pltpu.VMEM((seq, HD), F32)],
-        cost_estimate=pl.CostEstimate(
-            flops=600_000_000, bytes_accessed=5_000_000, transcendentals=1_100_000
-        ),
+        cost_estimate=cost(4_000_000_000, 5_000_000),
         name="gram",
     )(lengths, qk, qk, targets)
 
 
-def first_kernel(g_ref, z_ref, v_ref, low_ref, up_ref, grad_ref, mixed_ref, up_grad_ref, *, factor):
+def first_kernel(
+    at_ref, g_ref, z_ref, c0, c1, c2, c3, up_ref,
+    packed_ref, mixed_ref, up_grad_ref, v_ref, low_ref, *, rows, factor,
+):
+    rank = up_ref.shape[0]
+    seq, own = v_ref.shape
+    for k, ref in enumerate((c0, c1, c2, c3)):
+        at = pl.multiple_of((at_ref[0] ^ k) * rows, rows)
+        v_ref[pl.ds(at, rows), :] = ref[:rows, :]
+        low_ref[:, pl.ds(at, rows)] = ref[rows:, :rows]
+    low = low_ref[...]
     for g in range(g_ref.shape[0]):
         cols = slice(g * HD, (g + 1) * HD)
         total = dot(g_ref[g], v_ref[:, cols], 1, 0) - z_ref[:, cols]
-        grad_ref[:, cols] = (factor * total).astype(BF16)
-    grad = grad_ref[...]
+        packed_ref[:seq, cols] = (factor * total).astype(BF16)
+        x0 = (factor * dot(low, g_ref[g], 1, 0)).astype(BF16)
+        for part in range(seq // own):
+            to = seq + part * g_ref.shape[0] * rank + g * rank
+            packed_ref[to : to + rank, :] = x0[:, part * own : (part + 1) * own]
+    grad = packed_ref[:seq, :]
     mixed_ref[...] = dot(up_ref[...], grad, 1, 1)
-    up_grad_ref[...] = dot(low_ref[...], grad, 1, 0)
-
-
-def first_pass(g, z, values, low_t, up, factor):
-    seq, width = values.shape
+    up_grad_ref[...] = dot(low, grad, 1, 0)
+
+
+def first_pass(at, g, z, carried, up, rows, factor):
+    seq, own = z.shape
     rank = up.shape[0]
-    return pl.pallas_call(
-        functools.partial(first_kernel, factor=factor),
+    extra = g.shape[0] * rank * seq // own
+    return pl.pallas_call(
+        functools.partial(first_kernel, rows=rows, factor=factor),
+        in_specs=[SMEM] + [VMEM] * 7,
         out_shape=[
-            jax.ShapeDtypeStruct((seq, width), BF16),
-            jax.ShapeDtypeStruct((rank, seq), F32),
-            jax.ShapeDtypeStruct((rank, width), F32),
+            struct((seq + extra, own), BF16),
+            struct((rank, seq), F32),
+            struct((rank, own), F32),
         ],
-        cost_estimate=pl.CostEstimate(
-            flops=150_000_000, bytes_accessed=2_000_000, transcendentals=0
-        ),
+        scratch_shapes=[pltpu.VMEM((seq, own), BF16), pltpu.VMEM((rank, seq), BF16)],
+        cost_estimate=cost(1_000_000_000, 2_000_000),
         name="first_pass",
-    )(g, z, values, low_t, up)
-
-
-def second_kernel(g_ref, grad_ref, low_ref, new_low_ref, up_ref, new_up_ref, out_ref, *, factor):
-    delta = dot(new_low_ref[...], new_up_ref[...], 0, 0) - dot(low_ref[...], up_ref[...], 0, 0)
-    delta = delta.astype(BF16)
-    for g in range(g_ref.shape[0]):
+    )(at, g, z, *carried, up)
+
+
+def down_kernel(m0, m1, m2, m3, h_ref, up_grad_ref, out_ref):
+    width = h_ref.shape[1]
+    mixed = ((m0[...] + m1[...]) + (m2[...] + m3[...])).astype(BF16)
+    out_ref[:, :width] = dot(mixed, h_ref[...], 1, 0)
+    out_ref[:, width:] = up_grad_ref[...]
+
+
+def down_pass(mixed, h_cols, up_grad):
+    rank, own = up_grad.shape
+    return pl.pallas_call(
+        down_kernel,
+        in_specs=[VMEM] * 6,
+        out_shape=struct((rank, h_cols.shape[1] + own), F32),
+        cost_estimate=cost(500_000_000, 1_200_000),
+        name="down_pass",
+    )(*mixed, h_cols, up_grad)
+
+
+def moved_kernel(l0, l1, l2, l3, h_ref, out_ref, up_grad_ref):
+    rank, own = up_grad_ref.shape
+    width = h_ref.shape[1]
+    low_rank = (l0[...] + l1[...]) + (l2[...] + l3[...])
+    out_ref[:rank, :] = dot(low_rank[:, :width].astype(BF16), h_ref[...], 1, 1)
+    squares = jnp.sum(jnp.sum(low_rank * low_rank, axis=1, keepdims=True), axis=0, keepdims=True)
+    out_ref[rank:, :] = jnp.broadcast_to(squares, (out_ref.shape[0] - rank, out_ref.shape[1]))
+    up_grad_ref[...] = low_rank[:, width:]
+
+
+def moved_pass(low_rank, h_cols):
+    rank, total = low_rank[0].shape
+    seq, width = h_cols.shape
+    return pl.pallas_call(
+        moved_kernel,
+        in_specs=[VMEM] * 5,
+        out_shape=[struct((rank + 8, seq), F32), struct((rank, total - width), F32)],
+        cost_estimate=cost(500_000_000, 1_200_000),
+        name="moved_pass",
+    )(*low_rank, h_cols)
+
+
+def step_kernel(s0, s1, s2, s3, g_ref, up_ref, up_grad_ref, out_ref, *, count, factor):
+    rank, own = up_ref.shape
+    both = (s0[...] + s1[...]) + (s2[...] + s3[...])
+    moved = both[:rank, :].astype(BF16)
+    spread = jnp.sqrt(both[rank : rank + 1, :1] / count + 1e-06)
+    step = ATTACK_STEP / spread
+    groups = g_ref.shape[0]
+    for g in range(groups):
+        out_ref[g * rank : (g + 1) * rank, :] = (factor * dot(moved, g_ref[g], 1, 0)).astype(BF16)
+    up = up_ref[...].astype(F32)
+    new_up = (up - step * up_grad_ref[...]).astype(BF16).astype(F32)
+    out_ref[groups * rank :, :own] = (new_up - up).astype(BF16)
+    out_ref[groups * rank :, own:] = (-step * new_up).astype(BF16)
+
+
+def step_pass(sums, g, up, up_grad, count, factor):
+    rank, own = up.shape
+    groups, seq = g.shape[:2]
+    return pl.pallas_call(
+        functools.partial(step_kernel, count=count, factor=factor),
+        in_specs=[VMEM] * 7,
+        out_shape=struct(((groups + 1) * rank, seq), BF16),
+        cost_estimate=cost(500_000_000, 1_200_000),
+        name="step_pass",
+    )(*sums, g, up, up_grad)
+
+
+def main_kernel(at_ref, h_ref, p0, p1, p2, p3, send_ref, keep_ref):
+    seq, width = h_ref.shape
+    own = p0.shape[1]
+    parts = seq // own
+    wide = (p0.shape[0] - seq) // parts
+    turned = h_ref[...].T
+    for k, ref in enumerate((p0, p1, p2, p3)):
+        slot = at_ref[0] ^ at_ref[1] ^ k
+        x0 = jnp.concatenate(
+            [ref[seq + part * wide : seq + (part + 1) * wide, :] for part in range(parts)], axis=1
+        )
+        block = dot(turned, ref[:seq, :], 1, 0)
+        small = dot(x0, h_ref[...], 1, 0)
+
+        def put(out, dtype):
+            out[slot // 2, :width, :] = block.astype(dtype)
+            for part in range(width // own):
+                at = width + part * wide
+                out[slot // 2, at : at + wide, :] = small[
+                    :, part * own : (part + 1) * own
+                ].astype(dtype)
+
+        pl.when(slot % 2 == 1)(functools.partial(put, send_ref, BF16))
+        pl.when(slot % 2 == 0)(functools.partial(put, keep_ref, F32))
+
+
+def main_pass(at, h_cols, packed):
+    seq, width = h_cols.shape
+    own = packed[0].shape[1]
+    wide = (packed[0].shape[0] - seq) // (seq // own)
+    tall = width + wide * (width // own)
+    return pl.pallas_call(
+        main_kernel,
+        in_specs=[SMEM] + [VMEM] * 5,
+        out_shape=[struct((2, tall, own), BF16), struct((2, tall, own), F32)],
+        cost_estimate=cost(2_000_000_000, 6_000_000),
+        name="main_pass",
+    )(at, h_cols, *packed)
+
+
+def late_kernel(at_ref, h_ref, x0, x1, x2, x3, keep_ref, s1, s2, s3, up_ref, *, rank):
+    seq = h_ref.shape[0]
+    own = up_ref.shape[1]
+    wide = keep_ref.shape[0]
+    where = at_ref[0] ^ at_ref[1]
+    for k, ref in enumerate((x0, x1, x2, x3)):
+        slot = where ^ k
+        block = dot(ref[:wide, :], h_ref[...], 1, 0)
+
+        def keep(ref=ref, block=block):
+            keep_ref[...] = block
+            for part in range(seq // own):
+                up_ref[part * rank : (part + 1) * rank, :] = ref[
+                    wide:, part * own : (part + 1) * own
+                ]
+
+        pl.when(slot == 0)(keep)
+        for m, out in ((1, s1), (2, s2), (3, s3)):
+
+            def put(out=out, block=block):
+                out[...] = block.astype(BF16)
+
+            pl.when(slot == m)(put)
+
+
+def late_pass(at, h_cols, moved, rank, own):
+    seq, width = h_cols.shape
+    wide = moved[0].shape[0] - rank
+    block = struct((wide, width), BF16)
+    return pl.pallas_call(
+        functools.partial(late_kernel, rank=rank),
+        in_specs=[SMEM] + [VMEM] * 5,
+        out_shape=[
+            struct((wide, width), F32), block, block, block, struct((rank * seq // own, own), BF16)
+        ],
+        cost_estimate=cost(500_000_000, 1_500_000),
+        name="late_pass",
+    )(at, h_cols, *moved)
+
+
+def pack_kernel(r0, r1, r2, r3, up_ref, out_ref):
+    wide, width = r0.shape
+    total = (r0[...] + r1[...].astype(F32)) + (r2[...].astype(F32) + r3[...].astype(F32))
+    out_ref[:wide, :] = total.astype(BF16)
+    own = up_ref.shape[1]
+    deep = up_ref.shape[0] * own // width
+    for part in range(width // own):
+        out_ref[wide:, part * own : (part + 1) * own] = up_ref[part * deep : (part + 1) * deep, :]
+
+
+def pack_pass(late, up):
+    wide, width = late[0].shape
+    deep = up.shape[0] * up.shape[1] // width
+    return pl.pallas_call(
+        pack_kernel,
+        in_specs=[VMEM] * 5,
+        out_shape=struct((wide + deep, width), BF16),
+        cost_estimate=cost(500_000, 400_000),
+        name="pack_pass",
+    )(*late, up)
+
+
+def last_kernel(m0, m1, l0, l1, out_ref, *, rank, scale):
+    width, own = out_ref.shape
+    wide = own // HD * rank
+    deep = l0.shape[0] - wide
+
+    def correction(main, late, g):
+        x0 = jnp.concatenate(
+            [
+                main[width + part * wide + g * rank : width + part * wide + (g + 1) * rank, :]
+                for part in range(width // own)
+            ],
+            axis=1,
+        )
+        left = jnp.concatenate([x0, late[g * rank : (g + 1) * rank, :]], axis=0)
+        right = jnp.concatenate(
+            [
+                late[wide:, part * own + g * HD : part * own + (g + 1) * HD]
+                for part in range(width // own)
+            ],
+            axis=0,
+        )
+        return dot(left, right, 0, 0)
+
+    for g in range(own // HD):
         cols = slice(g * HD, (g + 1) * HD)
-        moved = factor * dot(g_ref[g], delta[:, cols], 1, 0)
-        out_ref[:, cols] = (-(grad_ref[:, cols].astype(F32) + moved)).astype(BF16)
-
-
-def second_pass(g, grad, low_t, new_low_t, up, new_up, factor):
-    return pl.pallas_call(
-        functools.partial(second_kernel, factor=factor),
-        out_shape=jax.ShapeDtypeStruct(grad.shape, BF16),
-        cost_estimate=pl.CostEstimate(
-            flops=150_000_000, bytes_accessed=2_000_000, transcendentals=0
-        ),
-        name="second_pass",
-    )(g, grad, low_t, new_low_t, up, new_up)
+        main = m0[:width, cols].astype(F32) + m1[:width, cols].astype(F32)
+        moved = correction(m0, l0, g) + correction(m1, l1, g)
+        out_ref[:, cols] = scale * (main + moved)
+
+
+def last_pass(mains, lates, width, rank, scale):
+    own = mains[0].shape[1]
+    return pl.pallas_call(
+        functools.partial(last_kernel, rank=rank, scale=scale),
+        in_specs=[VMEM] * 4,
+        out_shape=struct((width, own), F32),
+        cost_estimate=cost(100_000_000, 2_500_000),
+        name="last_pass",
+    )(*mains, *lates)
 
 
 def exchange(array, axis):
     return lax.all_to_all(array, axis, split_axis=0, concat_axis=0, tiled=True)
-
-
-def everyone(array, axis):
-    count = lax.axis_size(axis)
-    return exchange(jnp.broadcast_to(array[None], (count,) + array.shape), axis)
 
 
 def by_columns(array, parts):
@@ -148,17 +349,13 @@
     return array.reshape(rows, parts, width // parts).transpose(1, 0, 2)
 
 
-def swap(array, axis, bit):
+def swap(array, axis, bits):
     count = lax.axis_size(axis)
-    return lax.ppermute(array, axis, [(i, i ^ bit) for i in range(count)])
-
-
-def sum_over(array, axis):
-    bit = 1
-    while bit < lax.axis_size(axis):
-        array = array + swap(array, axis, bit)
-        bit *= 2
-    return array
+    return lax.ppermute(array, axis, [(i, i ^ bits) for i in range(count)])
+
+
+def everyone(array, axis):
+    return [array] + [swap(array, axis, bits) for bits in (1, 2, 3)]
 
 
 def body(
@@ -172,71 +369,56 @@
     factor = float(n_dp * seq) ** (-0.5)
     own = value_span // n_ctx
     ctx, dp = lax.axis_index("ctx"), lax.axis_index("dp")
+    at = jnp.stack([ctx, dp]).astype(jnp.int32)
     h = hidden[0, 0]
-    up_own = lax.dynamic_slice_in_dim(attacker_up_factor, ctx * own, own, axis=1)
+    up = lax.dynamic_slice_in_dim(attacker_up_factor, ctx * own, own, axis=1)
 
     qk = exchange(
         jnp.concatenate([by_columns(queries[0, 0], n_ctx), by_columns(keys[0, 0], n_ctx)], axis=2),
         "ctx",
     ).reshape(seq, -1)
-    base = dot(h, value_matrix, 1, 0)
     low_t = dot(attacker_down_factor, h, 0, 1).astype(BF16)
-    values = (base + dot(low_t, attacker_up_factor, 0, 0)).astype(BF16)
+    values = (dot(h, value_matrix, 1, 0) + dot(low_t, attacker_up_factor, 0, 0)).astype(BF16)
     carried = jnp.concatenate(
         [
             by_columns(values, n_ctx),
-            jnp.broadcast_to(
-                jnp.pad(low_t, ((0, 0), (0, own - rows)))[None], (n_ctx, rank, own)
-            ),
+            jnp.broadcast_to(jnp.pad(low_t, ((0, 0), (0, own - rows)))[None], (n_ctx, rank, own)),
         ],
         axis=1,
     )
-    carried = exchange(carried, "ctx")
-    v_seq = carried[:, :rows].reshape(seq, own)
-    low_all = carried[:, rows:, :rows].transpose(1, 0, 2).reshape(rank, seq)
-    h_cols = exchange(by_columns(h, n_ctx), "ctx").reshape(seq, width // n_ctx)
+    carried = [
+        lax.dynamic_index_in_dim(carried, ctx ^ bits, 0, keepdims=False) for bits in range(n_ctx)
+    ]
+    carried = carried[:1] + [swap(carried[bits], "ctx", bits) for bits in (1, 2, 3)]
+    h_later, qk = lax.optimization_barrier((h, qk))
+    h_cols = exchange(by_columns(h_later, n_ctx), "ctx").reshape(seq, width // n_ctx)
 
     g, z = gram(lengths[0, 0], qk, targets[0, 0])
-    grad, mixed_t, up_grad = first_pass(g, z, v_seq, low_all, up_own, factor)
-    mixed_t = everyone(mixed_t, "ctx").sum(axis=0).astype(BF16)
-    down_grad = dot(mixed_t, h_cols, 1, 0)
-    low_rank = sum_over(jnp.concatenate([down_grad, up_grad], axis=1), "dp")
-    down_grad, up_grad = low_rank[:, : width // n_ctx], low_rank[:, width // n_ctx :]
-    squares = jnp.sum(low_rank * low_rank)
-    moved_t = dot(down_grad.astype(BF16), h_cols, 1, 1)
-    both = jnp.concatenate([moved_t, jnp.full((8, seq), squares)], axis=0)
-    both = everyone(both, "ctx").sum(axis=0)
-    moved_t, squares = both[:rank], both[rank, 0]
-    spread = jnp.sqrt(squares / (rank * (width + value_span)) + 1e-06)
-    step = ATTACK_STEP / spread
-    new_low = (low_all.astype(F32) - step * moved_t).astype(BF16)
-    new_up = (up_own.astype(F32) - step * up_grad).astype(BF16)
-    tamper = second_pass(g, grad, low_all, new_low, up_own, new_up, factor)
-
-    tampers = everyone(tamper, "ctx")
-    shares = lax.dot_general(
-        tampers, h_cols, (((1,), (0,)), ((), ())), preferred_element_type=F32
-    )
-    return finish(shares, dp, n_dp, value_span)
-
-
-def finish(shares, dp, n_dp, value_span):
-    rows = shares.shape[2]
-    blocks = shares.reshape(n_dp, value_span // n_dp, rows)
-    bit = n_dp // 2
-    low = 1
-    while low < n_dp:
-        pairs = blocks.reshape(blocks.shape[0] // 2, 2, *blocks.shape[1:])
-        mine = (dp // low) % 2
-        keep = lax.dynamic_index_in_dim(pairs, mine, 1, keepdims=False)
-        send = lax.dynamic_index_in_dim(pairs, 1 - mine, 1, keepdims=False)
-        blocks = keep + swap(send.astype(BF16), "dp", low).astype(F32)
-        low *= 2
-    total = blocks[0].astype(BF16)
-    n_adv = lax.axis_size("adv")
-    other = swap(total, "adv", 1)
-    out = (total.astype(F32) + other.astype(F32)) / n_adv
-    return out.T
+    packed, mixed, up_grad = first_pass(at, g, z, carried, up, rows, factor)
+    mixed = everyone(mixed, "ctx")
+    packed, *mixed = lax.optimization_barrier((packed, *mixed))
+    packed = everyone(packed, "ctx")
+
+    low_rank = everyone(down_pass(mixed, h_cols, up_grad), "dp")
+    moved, up_grad = moved_pass(low_rank, h_cols)
+    stepped = step_pass(
+        everyone(moved, "ctx"), g, up, up_grad, rank * (width + value_span), factor
+    )
+    keep, *sent, rows_of_up = late_pass(at, h_cols, everyone(stepped, "ctx"), rank, own)
+    late = [keep] + [swap(part, "dp", bits) for bits, part in zip((1, 2, 3), sent)]
+    late = pack_pass(late, rows_of_up)
+    late = [late, swap(late, "adv", 1)]
+
+    send, kept = main_pass(at, h_cols, packed)
+    got = swap(send, "dp", 1).astype(F32)
+    cut = kept.shape[1] // 2
+    mains = []
+    for part in (slice(0, cut), slice(cut, None)):
+        passed = swap((kept[1, part] + got[1, part]).astype(BF16), "dp", 2).astype(F32)
+        mains.append(((kept[0, part] + got[0, part]) + passed).astype(BF16))
+    others = [swap(part, "adv", 1) for part in mains]
+    mains = [jnp.concatenate(mains, axis=0), jnp.concatenate(others, axis=0)]
+    return last_pass(mains, late, width // n_ctx, rank, -1.0 / lax.axis_size("adv"))
 
 
 def doc_ids(lengths, seq):
@@ -380,7 +562,8 @@
 
 
 def solution(mesh):
-    split = 8 % mesh.shape['ctx'] == 0 and mesh.shape['adv'] == 2
+    sizes = mesh.shape
+    fits = (sizes["ctx"], sizes["dp"], sizes["adv"]) == (4, 4, 2)
     placed = (
         P("adv", "dp", "ctx", None),
         P("adv", "dp", "ctx", None),
@@ -392,5 +575,9 @@
         P(),
     )
     return jax.shard_map(
-        body if split else plain_body, mesh=mesh, in_specs=placed, out_specs=P("ctx", "dp"), check_vma=False
-    )
+        body if fits else plain_body,
+        mesh=mesh,
+        in_specs=placed,
+        out_specs=P("ctx", "dp"),
+        check_vma=False,
+    )

time: 197 us -> 182 us (0.924)
  waiting for transfers between devices: 118 us -> 86.3 us
  Pallas kernels: 12.3 us -> 30.3 us
  starting transfers between devices: 25.1 us -> 42.2 us
  blocking collectives: 9.78 us -> 0 us
  local copies, waits for them, and re-layouts: 15.5 us -> 9.99 us
  matrix products: 8.7 us -> 5.25 us
    all_to_all x5 -> x2, waiting for transfers between devices: 87.1 us -> 26.7 us  [exchange(): return lax.all_to_all(array, axis, split_axis=0, concat_axis=0, tiled=True)]
    ppermute x5 -> x27, waiting for transfers between devices: 30.9 us -> 59.6 us  [swap(): return lax.ppermute(array, axis, [(i, i ^ bits) for i in range(count)])]
    ppermute x5 -> x27, starting transfers between devices: 4.84 us -> 31.6 us  [swap(): return lax.ppermute(array, axis, [(i, i ^ bits) for i in range(count)])]
    pallas_call x2 -> x8, Pallas kernels: 5.42 us -> 23.5 us  [the longest x1 6.37 us: main_pass(): pl.pallas_call(main_kernel, in_specs=[SMEM] + [VMEM] * 5, out_shape=[stru...]
    all_to_all x1 -> x0, blocking collectives: 9.78 us -> none  [exchange(): return lax.all_to_all(array, axis, split_axis=0, concat_axis=0, tiled=True)]
    all_to_all x5 -> x2, starting transfers between devices: 20.2 us -> 10.6 us  [exchange(): return lax.all_to_all(array, axis, split_axis=0, concat_axis=0, tiled=True)]
    broadcast_in_dim x3 -> x0, local copies, waits for them, and re-layouts: 2.48 us -> none  [everyone(): return exchange(jnp.broadcast_to(array[None], (count,) + array.shape), axis)]
    dot_general x5 -> x3, matrix products: 7.45 us -> 5.25 us  [dot(): lax.dot_general(a, b, (((da,), (db,)), ((), ())), preferred_element_type=...]
  transfers between devices with their start and end apart: 10 -> 29, of which waited for: 10 -> 17; matrix products, arithmetic and copies ran while one was open for 3% -> 7% of each run, Pallas kernels for 0% -> 12%
where the time goes in v2:
time: 182 us
  waiting for transfers between devices  86.3 us (47%)
  starting transfers between devices  42.2 us (23%)
  Pallas kernels  30.3 us (17%)
  local copies, waits for them, and re-layouts  9.99 us (5%)
  other arithmetic  7.34 us (4%)
  matrix products  5.25 us (3%)
    ppermute x27, waiting for transfers between devices, swap(): return lax.ppermute(array, axis, [(i, i ^ bits) for i in range(count)])  59.6 us
    ppermute x27, starting transfers between devices, swap(): return lax.ppermute(array, axis, [(i, i ^ bits) for i in range(count)])  31.6 us
    all_to_all x2, waiting for transfers between devices, exchange(): return lax.all_to_all(array, axis, split_axis=0, concat_axis=0, tiled=True)  26.7 us
    all_to_all x2, starting transfers between devices, exchange(): return lax.all_to_all(array, axis, split_axis=0, concat_axis=0, tiled=True)  10.6 us
    pallas_call x1, Pallas kernels, gram(): pl.pallas_call(functools.partial(gram_kernel, docs=lengths.shape[0], bloc...  6.79 us
    pallas_call x1, Pallas kernels, main_pass(): pl.pallas_call(main_kernel, in_specs=[SMEM] + [VMEM] * 5, out_shape=[stru...  6.37 us
    dot_general x3, matrix products, dot(): lax.dot_general(a, b, (((da,), (db,)), ((), ())), preferred_element_type=...  5.25 us
    unnamed x50, local copies, waits for them, and re-layouts  4.81 us
  transfers between devices with their start and end apart: 29, of which 17 were waited for; matrix products, arithmetic and copies ran while one was open for 7% of the time, Pallas kernels for 12%

profile of v2, /device:TPU:0, one launch (start us, length us, event | category | flops | bytes accessed | tf_op | source)
XLA Modules:
  0.0 181.7 jit_solution(354113316516251166)
XLA Ops:
  4.6 6.3 %all-to-all-start = ((bf16[4,128,1280]{2,1,0:T(8,128)(2,1)}), bf16[4,128,1280]{2,1,0:T(8,128)(2,1)S(1)}, u32[]{:S(2)}, u32[]{:S(2)}) async-start(bf16[4,128,1280]{2,1,0:T(8,128)(2,1)} %pad_maximum_fusion), calls=%async_computation | async-start | bytes 2621440 | tf_op jit(solution)/shard_map/all_to_all | solution.py:344
  10.9 4.6 %fusion.20 = f32[128,1024]{1,0:T(8,128)S(1)} fusion(bf16[4096,1024]{1,0:T(8,128)(2,1)} %param.13, bf16[1,1,128,4096]{3,2,1,0:T(8,128)(2,1)S(1)} %copy-done.1), kind=kOutput, calls=%fused_computation.43 | convolution fusion | flops 1073741824 | bytes 9961472 | tf_op jit(solution)/shard_map/dot_general | solution.py:22
  15.6 26.7 %all-to-all-done = bf16[4,128,1280]{2,1,0:T(8,128)(2,1)S(1)} async-done(((bf16[4,128,1280]{2,1,0:T(8,128)(2,1)}), bf16[4,128,1280]{2,1,0:T(8,128)(2,1)S(1)}, u32[]{:S(2)}, u32[]{:S(2)}) %all-to-all-start) | async-done | bytes 1310752 | tf_op jit(solution)/shard_map/all_to_all | solution.py:344
  43.5 4.3 %all-to-all-start.1 = ((bf16[4,128,1024]{2,1,0:T(8,128)(2,1)}), bf16[4,128,1024]{2,1,0:T(8,128)(2,1)}, u32[]{:S(2)}, u32[]{:S(2)}) async-start(bf16[4,128,1024]{2,1,0:T(8,128)(2,1)} %bitcast.58), calls=%async_computation.1 | async-start | bytes 2097152 | tf_op jit(solution)/shard_map/all_to_all | solution.py:344
  49.1 3.8 %collective-permute-start.2 = (bf16[144,256]{1,0:T(8,128)(2,1)S(1)}, bf16[144,256]{1,0:T(8,128)(2,1)S(1)}, u32[]{:S(2)}, u32[]{:S(2)}) collective-permute-start(bf16[144,256]{1,0:T(8,128)(2,1)S(1)} %get-tuple-element.51), channel_id=1, source_target_pairs={{0,24},{8,16},{16,8},{24,0},{1,25},{9,17},{17,9},{25,1},{2,26},{10... | collective-permute-start | bytes 221192 | tf_op jit(solution)/shard_map/ppermute | solution.py:354
  54.7 6.8 %gram.1 = (bf16[2,512,512]{2,1,0:T(8,128)(2,1)}, f32[512,256]{1,0:T(8,128)}) custom-call(s32[8]{0:T(128)} %bitcast.71, bf16[512,1280]{1,0:T(8,128)(2,1)} %bitcast.65, bf16[512,1280]{1,0:T(8,128)(2,1)} %bitcast.66, bf16[512,1024]{1,0:T(8,128)(2,1)} %bitcast.70), custom_call_target="tpu_custom_call" | custom-call | flops 4000000000 | bytes 5000000 | tf_op jit(solution)/shard_map/gram/pallas_call | solution.py:71
  61.5 10.0 %collective-permute-done.2.c3 = bf16[144,256]{1,0:T(8,128)(2,1)S(1)} collective-permute-done((bf16[144,256]{1,0:T(8,128)(2,1)S(1)}, bf16[144,256]{1,0:T(8,128)(2,1)S(1)}, u32[]{:S(2)}, u32[]{:S(2)}) %collective-permute-start.2) | collective-permute-done | bytes 73760 | tf_op jit(solution)/shard_map/ppermute | solution.py:354
  71.5 7.8 %collective-permute-done.1.c2 = bf16[144,256]{1,0:T(8,128)(2,1)S(1)} collective-permute-done((bf16[144,256]{1,0:T(8,128)(2,1)S(1)}, bf16[144,256]{1,0:T(8,128)(2,1)S(1)}, u32[]{:S(2)}, u32[]{:S(2)}) %collective-permute-start.1) | collective-permute-done | bytes 73760 | tf_op jit(solution)/shard_map/ppermute | solution.py:354
  79.9 2.8 %first_pass.1 = (bf16[576,256]{1,0:T(8,128)(2,1)}, f32[16,512]{1,0:T(8,128)}, f32[16,256]{1,0:T(8,128)}) custom-call(s32[2]{0:T(128)} %pad_add_fusion.at_ref, bf16[2,512,512]{2,1,0:T(8,128)(2,1)} %get-tuple-element.28.g_ref, f32[512,256]{1,0:T(8,128)} %get-tuple-element.29.z_ref, bf16[144,256]{1,0:T(8,128)(2,1)} %get-tuple-element.52.c0, ...), custom_call_target="tpu_custom_call" | custom-call | flops 1000000000 | bytes 2000000 | tf_op jit(solution)/shard_map/first_pass/pallas_call | solution.py:119
  84.2 2.9 %collective-permute-start.3 = (f32[16,512]{1,0:T(8,128)}, f32[16,512]{1,0:T(8,128)S(1)}, u32[]{:S(2)}, u32[]{:S(2)}) collective-permute-start(f32[16,512]{1,0:T(8,128)} %get-tuple-element.35.m0), channel_id=1, source_target_pairs={{0,8},{8,0},{16,24},{24,16},{1,9},{9,1},{17,25},{25,17},{2,10},{10... | collective-permute-start | bytes 98312 | tf_op jit(solution)/shard_map/ppermute | solution.py:354
  89.6 2.0 %collective-permute-start.8 = (bf16[576,256]{1,0:T(8,128)(2,1)}, bf16[576,256]{1,0:T(8,128)(2,1)S(1)}, u32[]{:S(2)}, u32[]{:S(2)}) collective-permute-start(bf16[576,256]{1,0:T(8,128)(2,1)} %get-tuple-element.32.p0), channel_id=1, source_target_pairs={{0,24},{8,16},{16,8},{24,0},{1,25},{9,17},{17,9},{25,1},{2,26},{10... | collective-permute-start | bytes 884744 | tf_op jit(solution)/shard_map/ppermute | solution.py:354
  94.0 7.5 %collective-permute-done.8.p3 = bf16[576,256]{1,0:T(8,128)(2,1)S(1)} collective-permute-done((bf16[576,256]{1,0:T(8,128)(2,1)}, bf16[576,256]{1,0:T(8,128)(2,1)S(1)}, u32[]{:S(2)}, u32[]{:S(2)}) %collective-permute-start.8) | collective-permute-done | bytes 294944 | tf_op jit(solution)/shard_map/ppermute | solution.py:354
  101.5 14.7 %collective-permute-done.7.p2 = bf16[576,256]{1,0:T(8,128)(2,1)S(1)} collective-permute-done((bf16[576,256]{1,0:T(8,128)(2,1)}, bf16[576,256]{1,0:T(8,128)(2,1)S(1)}, u32[]{:S(2)}, u32[]{:S(2)}) %collective-permute-start.7) | collective-permute-done | bytes 294944 | tf_op jit(solution)/shard_map/ppermute | solution.py:354
  117.0 6.4 %main_pass.1 = (bf16[2,1152,256]{2,1,0:T(8,128)(2,1)}, f32[2,1152,256]{2,1,0:T(8,128)}) custom-call(s32[2]{0:T(128)} %pad_add_fusion.at_ref, bf16[512,1024]{1,0:T(8,128)(2,1)} %bitcast.7.h_ref, bf16[576,256]{1,0:T(8,128)(2,1)} %get-tuple-element.32.p0, bf16[576,256]{1,0:T(8,128)(2,1)} %copy-done.10, bf16[576,256]{1,0:T(8,128)(2,1)} %copy-done.9, ...), custom_call_target="tpu_custom_call" | custom-call | flops 2000000000 | bytes 6000000 | tf_op jit(solution)/shard_map/main_pass/pallas_call | solution.py:231
  123.4 2.2 %down_pass.1.l0 = f32[16,1280]{1,0:T(8,128)} custom-call(f32[16,512]{1,0:T(8,128)} %get-tuple-element.35.m0, f32[16,512]{1,0:T(8,128)} %copy-done.24, f32[16,512]{1,0:T(8,128)} %copy-done.23, f32[16,512]{1,0:T(8,128)} %copy-done.22, bf16[512,1024]{1,0:T(8,128)(2,1)} %bitcast.7.h_ref, f32[16,256]{1,0:T(8,128)} %get-tuple-element.39.up_grad_ref), custom_call_target="tpu_custom_call" | custom-call | flops 500000000 | bytes 1200000 | tf_op jit(solution)/shard_map/down_pass/pallas_call | solution.py:142
  133.0 2.4 %moved_pass.1 = (f32[24,512]{1,0:T(8,128)}, f32[16,256]{1,0:T(8,128)}) custom-call(f32[16,1280]{1,0:T(8,128)} %down_pass.1.l0, f32[16,1280]{1,0:T(8,128)} %collective-permute-done.14.l1, f32[16,1280]{1,0:T(8,128)} %copy-done.12, f32[16,1280]{1,0:T(8,128)} %copy-done.11, bf16[512,1024]{1,0:T(8,128)(2,1)} %bitcast.7.h_ref), custom_call_target="tpu_custom_call" | custom-call | flops 500000000 | bytes 1200000 | tf_op jit(solution)/shard_map/moved_pass/pallas_call | solution.py:164
  136.6 3.2 %collective-permute-start.17 = (f32[24,512]{1,0:T(8,128)}, f32[24,512]{1,0:T(8,128)S(1)}, u32[]{:S(2)}, u32[]{:S(2)}) collective-permute-start(f32[24,512]{1,0:T(8,128)} %get-tuple-element.40.s0), channel_id=1, source_target_pairs={{0,8},{8,0},{16,24},{24,16},{1,9},{9,1},{17,25},{25,17},{2,10},{10... | collective-permute-start | bytes 147464 | tf_op jit(solution)/shard_map/ppermute | solution.py:354
  139.8 2.0 %collective-permute-done.19.s3 = f32[24,512]{1,0:T(8,128)S(1)} collective-permute-done((f32[24,512]{1,0:T(8,128)}, f32[24,512]{1,0:T(8,128)S(1)}, u32[]{:S(2)}, u32[]{:S(2)}) %collective-permute-start.19) | collective-permute-done | bytes 49184 | tf_op jit(solution)/shard_map/ppermute | solution.py:354
  143.3 2.2 %step_pass.1.x0 = bf16[48,512]{1,0:T(8,128)(2,1)} custom-call(f32[24,512]{1,0:T(8,128)} %get-tuple-element.40.s0, f32[24,512]{1,0:T(8,128)} %copy-done.21, f32[24,512]{1,0:T(8,128)} %copy-done.19, f32[24,512]{1,0:T(8,128)} %copy-done.17, bf16[2,512,512]{2,1,0:T(8,128)(2,1)} %get-tuple-element.28.g_ref, bf16[16,256]{1,0:T(8,128)(2,1)} %constant_dynamic-slice_fusion.up_ref, ...), custom_call_target="tpu_custom_call" | custom-call | flops 500000000 | bytes 1200000 | tf_op jit(solution)/shard_map/step_pass/pallas_call | solution.py:191
  150.0 2.3 %collective-permute-done.22.x3 = bf16[48,512]{1,0:T(8,128)(2,1)S(1)} collective-permute-done((bf16[48,512]{1,0:T(8,128)(2,1)}, bf16[48,512]{1,0:T(8,128)(2,1)S(1)}, u32[]{:S(2)}, u32[]{:S(2)}) %collective-permute-start.22) | collective-permute-done | bytes 49184 | tf_op jit(solution)/shard_map/ppermute | solution.py:354
  154.4 3.2 %late_pass.1 = (f32[32,1024]{1,0:T(8,128)}, bf16[32,1024]{1,0:T(8,128)(2,1)}, bf16[32,1024]{1,0:T(8,128)(2,1)}, bf16[32,1024]{1,0:T(8,128)(2,1)}, bf16[32,256]{1,0:T(8,128)(2,1)}) custom-call(s32[2]{0:T(128)} %pad_add_fusion.at_ref, bf16[512,1024]{1,0:T(8,128)(2,1)} %bitcast.7.h_ref, bf16[48,512]{1,0:T(8,128)(2,1)} %step_pass.1.x0, ...), custom_call_target="tpu_custom_call" | custom-call | flops 500000000 | bytes 1500000 | tf_op jit(solution)/shard_map/late_pass/pallas_call | solution.py:269
  167.7 3.2 %collective-permute-done.12 = bf16[576,256]{1,0:T(8,128)(2,1)S(1)} collective-permute-done((bf16[576,256]{1,0:T(8,128)(2,1)S(1)}, bf16[576,256]{1,0:T(8,128)(2,1)S(1)}, u32[]{:S(2)}, u32[]{:S(2)}) %collective-permute-start.12) | collective-permute-done | bytes 294944 | tf_op jit(solution)/shard_map/ppermute | solution.py:354
  170.9 6.3 %collective-permute-done.13 = bf16[576,256]{1,0:T(8,128)(2,1)S(1)} collective-permute-done((bf16[576,256]{1,0:T(8,128)(2,1)S(1)}, bf16[576,256]{1,0:T(8,128)(2,1)S(1)}, u32[]{:S(2)}, u32[]{:S(2)}) %collective-permute-start.13) | collective-permute-done | bytes 294944 | tf_op jit(solution)/shard_map/ppermute | solution.py:354
  179.0 2.7 %last_pass.1 = f32[1024,256]{1,0:T(8,128)} custom-call(bf16[1152,256]{1,0:T(8,128)(2,1)} %pad_maximum_fusion.1.m0, bf16[1152,256]{1,0:T(8,128)(2,1)} %pad_maximum_fusion.2.m1, bf16[40,1024]{1,0:T(8,128)(2,1)} %pack_pass.1.l0, bf16[40,1024]{1,0:T(8,128)(2,1)} %copy-done.4), custom_call_target="tpu_custom_call" | custom-call | flops 100000000 | bytes 2500000 | tf_op jit(solution)/shard_map/last_pass/pallas_call | solution.py:334
  (113 shorter events, 45.1 us)
Async XLA Ops:
  4.6 37.7 %all-to-all-start = ((bf16[4,128,1280]{2,1,0:T(8,128)(2,1)}), bf16[4,128,1280]{2,1,0:T(8,128)(2,1)S(1)}, u32[]{:S(2)}, u32[]{:S(2)}) async-start(bf16[4,128,1280]{2,1,0:T(8,128)(2,1)} %pad_maximum_fusion), calls=%async_computation | async-start | bytes 2621440 | tf_op jit(solution)/shard_map/all_to_all | solution.py:344
  43.5 72.8 %all-to-all-start.1 = ((bf16[4,128,1024]{2,1,0:T(8,128)(2,1)}), bf16[4,128,1024]{2,1,0:T(8,128)(2,1)}, u32[]{:S(2)}, u32[]{:S(2)}) async-start(bf16[4,128,1024]{2,1,0:T(8,128)(2,1)} %bitcast.58), calls=%async_computation.1 | async-start | bytes 2097152 | tf_op jit(solution)/shard_map/all_to_all | solution.py:344
  49.1 22.4 %collective-permute-start.2 = (bf16[144,256]{1,0:T(8,128)(2,1)S(1)}, bf16[144,256]{1,0:T(8,128)(2,1)S(1)}, u32[]{:S(2)}, u32[]{:S(2)}) collective-permute-start(bf16[144,256]{1,0:T(8,128)(2,1)S(1)} %get-tuple-element.51), channel_id=1, source_target_pairs={{0,24},{8,16},{16,8},{24,0},{1,25},{9,17},{17,9},{25,1},{2,26},{10... | collective-permute-start | bytes 221192 | tf_op jit(solution)/shard_map/ppermute | solution.py:354
  52.9 18.6 %collective-permute-start = (bf16[144,256]{1,0:T(8,128)(2,1)S(1)}, bf16[144,256]{1,0:T(8,128)(2,1)S(1)}, u32[]{:S(2)}, u32[]{:S(2)}) collective-permute-start(bf16[144,256]{1,0:T(8,128)(2,1)S(1)} %get-tuple-element.53), channel_id=1, source_target_pairs={{0,8},{8,0},{16,24},{24,16},{1,9},{9,1},{17,25},{25,17},{2,10},{10... | collective-permute-start | bytes 221192 | tf_op jit(solution)/shard_map/ppermute | solution.py:354
  52.9 26.4 %collective-permute-start.1 = (bf16[144,256]{1,0:T(8,128)(2,1)S(1)}, bf16[144,256]{1,0:T(8,128)(2,1)S(1)}, u32[]{:S(2)}, u32[]{:S(2)}) collective-permute-start(bf16[144,256]{1,0:T(8,128)(2,1)S(1)} %get-tuple-element.54), channel_id=1, source_target_pairs={{0,16},{8,24},{16,0},{24,8},{1,17},{9,25},{17,1},{25,9},{2,18},{10... | collective-permute-start | bytes 221192 | tf_op jit(solution)/shard_map/ppermute | solution.py:354
  82.7 5.9 %collective-permute-start.5 = (f32[16,512]{1,0:T(8,128)}, f32[16,512]{1,0:T(8,128)S(1)}, u32[]{:S(2)}, u32[]{:S(2)}) collective-permute-start(f32[16,512]{1,0:T(8,128)} %get-tuple-element.35.m0), channel_id=1, source_target_pairs={{0,24},{8,16},{16,8},{24,0},{1,25},{9,17},{17,9},{25,1},{2,26},{10... | collective-permute-start | bytes 98312 | tf_op jit(solution)/shard_map/ppermute | solution.py:354
  84.2 5.3 %collective-permute-start.4 = (f32[16,512]{1,0:T(8,128)}, f32[16,512]{1,0:T(8,128)S(1)}, u32[]{:S(2)}, u32[]{:S(2)}) collective-permute-start(f32[16,512]{1,0:T(8,128)} %get-tuple-element.35.m0), channel_id=1, source_target_pairs={{0,16},{8,24},{16,0},{24,8},{1,17},{9,25},{17,1},{25,9},{2,18},{10... | collective-permute-start | bytes 98312 | tf_op jit(solution)/shard_map/ppermute | solution.py:354
  84.2 5.4 %collective-permute-start.3 = (f32[16,512]{1,0:T(8,128)}, f32[16,512]{1,0:T(8,128)S(1)}, u32[]{:S(2)}, u32[]{:S(2)}) collective-permute-start(f32[16,512]{1,0:T(8,128)} %get-tuple-element.35.m0), channel_id=1, source_target_pairs={{0,8},{8,0},{16,24},{24,16},{1,9},{9,1},{17,25},{25,17},{2,10},{10... | collective-permute-start | bytes 98312 | tf_op jit(solution)/shard_map/ppermute | solution.py:354
  89.6 11.9 %collective-permute-start.8 = (bf16[576,256]{1,0:T(8,128)(2,1)}, bf16[576,256]{1,0:T(8,128)(2,1)S(1)}, u32[]{:S(2)}, u32[]{:S(2)}) collective-permute-start(bf16[576,256]{1,0:T(8,128)(2,1)} %get-tuple-element.32.p0), channel_id=1, source_target_pairs={{0,24},{8,16},{16,8},{24,0},{1,25},{9,17},{17,9},{25,1},{2,26},{10... | collective-permute-start | bytes 884744 | tf_op jit(solution)/shard_map/ppermute | solution.py:354
  91.6 24.6 %collective-permute-start.7 = (bf16[576,256]{1,0:T(8,128)(2,1)}, bf16[576,256]{1,0:T(8,128)(2,1)S(1)}, u32[]{:S(2)}, u32[]{:S(2)}) collective-permute-start(bf16[576,256]{1,0:T(8,128)(2,1)} %get-tuple-element.32.p0), channel_id=1, source_target_pairs={{0,16},{8,24},{16,0},{24,8},{1,17},{9,25},{17,1},{25,9},{2,18},{10... | collective-permute-start | bytes 884744 | tf_op jit(solution)/shard_map/ppermute | solution.py:354
  92.7 23.5 %collective-permute-start.6 = (bf16[576,256]{1,0:T(8,128)(2,1)}, bf16[576,256]{1,0:T(8,128)(2,1)S(1)}, u32[]{:S(2)}, u32[]{:S(2)}) collective-permute-start(bf16[576,256]{1,0:T(8,128)(2,1)} %get-tuple-element.32.p0), channel_id=1, source_target_pairs={{0,8},{8,0},{16,24},{24,16},{1,9},{9,1},{17,25},{25,17},{2,10},{10... | collective-permute-start | bytes 884744 | tf_op jit(solution)/shard_map/ppermute | solution.py:354
  125.6 5.9 %collective-permute-start.16 = (f32[16,1280]{1,0:T(8,128)}, f32[16,1280]{1,0:T(8,128)S(1)}, u32[]{:S(2)}, u32[]{:S(2)}) collective-permute-start(f32[16,1280]{1,0:T(8,128)} %down_pass.1.l0), channel_id=1, source_target_pairs={{0,6},{2,4},{4,2},{6,0},{1,7},{3,5},{5,3},{7,1},{8,14},{10,12},{12... | collective-permute-start | bytes 245768 | tf_op jit(solution)/shard_map/ppermute | solution.py:354
  129.4 30.0 %collective-permute-start.10 = (bf16[576,256]{1,0:T(8,128)(2,1)S(1)}, bf16[576,256]{1,0:T(8,128)(2,1)S(1)}, u32[]{:S(2)}, u32[]{:S(2)}) collective-permute-start(bf16[576,256]{1,0:T(8,128)(2,1)S(1)} %get-tuple-element.49), channel_id=1, source_target_pairs={{0,4},{2,6},{4,0},{6,2},{1,5},{3,7},{5,1},{7,3},{8,12},{10,14},{12... | collective-permute-start | bytes 884744 | tf_op jit(solution)/shard_map/ppermute | solution.py:354
  131.0 28.4 %collective-permute-start.11 = (bf16[576,256]{1,0:T(8,128)(2,1)S(1)}, bf16[576,256]{1,0:T(8,128)(2,1)}, u32[]{:S(2)}, u32[]{:S(2)}) collective-permute-start(bf16[576,256]{1,0:T(8,128)(2,1)S(1)} %get-tuple-element.50), channel_id=1, source_target_pairs={{0,4},{2,6},{4,0},{6,2},{1,5},{3,7},{5,1},{7,3},{8,12},{10,14},{12... | collective-permute-start | bytes 884744 | tf_op jit(solution)/shard_map/ppermute | solution.py:354
  135.4 6.4 %collective-permute-start.19 = (f32[24,512]{1,0:T(8,128)}, f32[24,512]{1,0:T(8,128)S(1)}, u32[]{:S(2)}, u32[]{:S(2)}) collective-permute-start(f32[24,512]{1,0:T(8,128)} %get-tuple-element.40.s0), channel_id=1, source_target_pairs={{0,24},{8,16},{16,8},{24,0},{1,25},{9,17},{17,9},{25,1},{2,26},{10... | collective-permute-start | bytes 147464 | tf_op jit(solution)/shard_map/ppermute | solution.py:354
  136.6 6.1 %collective-permute-start.18 = (f32[24,512]{1,0:T(8,128)}, f32[24,512]{1,0:T(8,128)S(1)}, u32[]{:S(2)}, u32[]{:S(2)}) collective-permute-start(f32[24,512]{1,0:T(8,128)} %get-tuple-element.40.s0), channel_id=1, source_target_pairs={{0,16},{8,24},{16,0},{24,8},{1,17},{9,25},{17,1},{25,9},{2,18},{10... | collective-permute-start | bytes 147464 | tf_op jit(solution)/shard_map/ppermute | solution.py:354
  136.6 6.2 %collective-permute-start.17 = (f32[24,512]{1,0:T(8,128)}, f32[24,512]{1,0:T(8,128)S(1)}, u32[]{:S(2)}, u32[]{:S(2)}) collective-permute-start(f32[24,512]{1,0:T(8,128)} %get-tuple-element.40.s0), channel_id=1, source_target_pairs={{0,8},{8,0},{16,24},{24,16},{1,9},{9,1},{17,25},{25,17},{2,10},{10... | collective-permute-start | bytes 147464 | tf_op jit(solution)/shard_map/ppermute | solution.py:354
  145.6 6.7 %collective-permute-start.22 = (bf16[48,512]{1,0:T(8,128)(2,1)}, bf16[48,512]{1,0:T(8,128)(2,1)S(1)}, u32[]{:S(2)}, u32[]{:S(2)}) collective-permute-start(bf16[48,512]{1,0:T(8,128)(2,1)} %step_pass.1.x0), channel_id=1, source_target_pairs={{0,24},{8,16},{16,8},{24,0},{1,25},{9,17},{17,9},{25,1},{2,26},{10... | collective-permute-start | bytes 147464 | tf_op jit(solution)/shard_map/ppermute | solution.py:354
  147.3 5.8 %collective-permute-start.21 = (bf16[48,512]{1,0:T(8,128)(2,1)}, bf16[48,512]{1,0:T(8,128)(2,1)S(1)}, u32[]{:S(2)}, u32[]{:S(2)}) collective-permute-start(bf16[48,512]{1,0:T(8,128)(2,1)} %step_pass.1.x0), channel_id=1, source_target_pairs={{0,16},{8,24},{16,0},{24,8},{1,17},{9,25},{17,1},{25,9},{2,18},{10... | collective-permute-start | bytes 147464 | tf_op jit(solution)/shard_map/ppermute | solution.py:354
  157.6 5.5 %collective-permute-start.23 = (bf16[32,1024]{1,0:T(8,128)(2,1)}, bf16[32,1024]{1,0:T(8,128)(2,1)S(1)}, u32[]{:S(2)}, u32[]{:S(2)}) collective-permute-start(bf16[32,1024]{1,0:T(8,128)(2,1)} %get-tuple-element.43), channel_id=1, source_target_pairs={{0,2},{2,0},{4,6},{6,4},{1,3},{3,1},{5,7},{7,5},{8,10},{10,8},{12,... | collective-permute-start | bytes 196616 | tf_op jit(solution)/shard_map/ppermute | solution.py:354
  157.6 5.5 %collective-permute-start.24 = (bf16[32,1024]{1,0:T(8,128)(2,1)}, bf16[32,1024]{1,0:T(8,128)(2,1)S(1)}, u32[]{:S(2)}, u32[]{:S(2)}) collective-permute-start(bf16[32,1024]{1,0:T(8,128)(2,1)} %get-tuple-element.44), channel_id=1, source_target_pairs={{0,4},{2,6},{4,0},{6,2},{1,5},{3,7},{5,1},{7,3},{8,12},{10,14},{12... | collective-permute-start | bytes 196616 | tf_op jit(solution)/shard_map/ppermute | solution.py:354
  160.9 9.9 %collective-permute-start.12 = (bf16[576,256]{1,0:T(8,128)(2,1)S(1)}, bf16[576,256]{1,0:T(8,128)(2,1)S(1)}, u32[]{:S(2)}, u32[]{:S(2)}) collective-permute-start(bf16[576,256]{1,0:T(8,128)(2,1)S(1)} %get-tuple-element.47), channel_id=1, source_target_pairs={{0,1},{1,0},{2,3},{3,2},{4,5},{5,4},{6,7},{7,6},{8,9},{9,8},{10,11... | collective-permute-start | bytes 884744 | tf_op jit(solution)/shard_map/ppermute | solution.py:354
  162.5 14.7 %collective-permute-start.13 = (bf16[576,256]{1,0:T(8,128)(2,1)S(1)}, bf16[576,256]{1,0:T(8,128)(2,1)S(1)}, u32[]{:S(2)}, u32[]{:S(2)}) collective-permute-start(bf16[576,256]{1,0:T(8,128)(2,1)S(1)} %get-tuple-element.48), channel_id=1, source_target_pairs={{0,1},{1,0},{2,3},{3,2},{4,5},{5,4},{6,7},{7,6},{8,9},{9,8},{10,11... | collective-permute-start | bytes 884744 | tf_op jit(solution)/shard_map/ppermute | solution.py:354
  165.3 13.0 %collective-permute-start.26 = (bf16[40,1024]{1,0:T(8,128)(2,1)}, bf16[40,1024]{1,0:T(8,128)(2,1)S(1)}, u32[]{:S(2)}, u32[]{:S(2)}) collective-permute-start(bf16[40,1024]{1,0:T(8,128)(2,1)} %pack_pass.1.l0), channel_id=1, source_target_pairs={{0,1},{1,0},{2,3},{3,2},{4,5},{5,4},{6,7},{7,6},{8,9},{9,8},{10,11... | collective-permute-start | bytes 245768 | tf_op jit(solution)/shard_map/ppermute | solution.py:354
  (30 other events, 236.5 us)

commit v3 on v2

v3 whole, which is shorter than its diff:
```python
import functools
import jax
import jax.numpy as jnp
from jax import lax
from jax.experimental import pallas as pl
from jax.experimental.pallas import tpu as pltpu
from jax.sharding import PartitionSpec as P

HD = 128
GROUP = 4


ATTACK_STEP = 0.01

BF16 = jnp.bfloat16
F32 = jnp.float32
SMEM = pl.BlockSpec(memory_space=pltpu.SMEM)
VMEM = pl.BlockSpec(memory_space=pltpu.VMEM)


def dot(a, b, da, db):
    return lax.dot_general(a, b, (((da,), (db,)), ((), ())), preferred_element_type=F32)


def cost(flops, size):
    return pl.CostEstimate(flops=flops, bytes_accessed=size, transcendentals=0)


def grant(mib):
    return pltpu.CompilerParams(vmem_limit_bytes=mib << 20)


def struct(shape, dtype):
    return jax.ShapeDtypeStruct(shape, dtype)


def pair_kernel(q_ref, k_ref, out_ref):
    parts = out_ref.shape[0]
    wide, narrow = q_ref.shape[1] // parts, k_ref.shape[1] // parts
    for p in range(parts):
        out_ref[p, :, :wide] = q_ref[:, p * wide : (p + 1) * wide]
        out_ref[p, :, wide:] = k_ref[:, p * narrow : (p + 1) * narrow]


def pair_columns(q, k, parts):
    return pl.pallas_call(
        pair_kernel,
        in_specs=[VMEM] * 2,
        out_shape=struct((parts, q.shape[0], (q.shape[1] + k.shape[1]) // parts), BF16),
        cost_estimate=cost(1000, 2_600_000),
        compiler_params=grant(12),
        name="pair_columns",
    )(q, k)


def gram_kernel(
    len_ref, q_all, y_ref, g_ref, z_ref, g_acc, z_acc, *, docs, reach
):
    seq = q_all.shape[0]
    block = seq // 4
    groups = g_ref.shape[0]
    scale = HD ** (-0.5)
    ends, total = [], jnp.int32(0)
    for j in range(docs):
        total = total + len_ref[j]
        ends.append(total)
    for g in range(groups):
        g_acc[...] = jnp.zeros_like(g_acc)
        z_acc[...] = jnp.zeros_like(z_acc)
        heads = [slice(h * HD, (h + 1) * HD) for h in range(g * GROUP, (g + 1) * GROUP)]
        key = slice((groups * GROUP + g) * HD, (groups * GROUP + g + 1) * HD)
        for i in range(seq // block):
            at, hi = i * block, (i + 1) * block
            lo = max(0, at - reach)
            q = jnp.concatenate([q_all[at:hi, h] for h in heads], axis=0)
            y = jnp.concatenate([y_ref[at:hi, h] for h in heads], axis=0)
            scores = dot(q, q_all[lo:hi, key], 1, 1) * scale
            row = lax.broadcasted_iota(jnp.int32, (block, 1), 0) + at
            first = jnp.zeros((block, 1), jnp.int32)
            for end in ends:
                first = jnp.where(row >= end, end, first)
            col = lax.broadcasted_iota(jnp.int32, (block, hi - lo), 1) + lo
            visible = (col >= first) & (col <= row)
            scores = scores.reshape(GROUP, block, hi - lo)
            scores = jnp.where(visible[None], scores, -1e30)
            top = jnp.max(scores, axis=2, keepdims=True)
            expo = jnp.exp(scores - top)
            probs = expo * (1.0 / jnp.sum(expo, axis=2, keepdims=True))
            probs = probs.reshape(GROUP * block, hi - lo).astype(BF16)
            g_acc[lo:hi, lo:hi] += dot(probs, probs, 0, 0)
            z_acc[:, lo:hi] += dot(y, probs, 0, 0)
        g_ref[g] = g_acc[...].astype(BF16)
        z_ref[g] = z_acc[...]


def gram(lengths, qk, targets):
    seq, width = targets.shape
    groups = width // (GROUP * HD)
    return pl.pallas_call(
        functools.partial(gram_kernel, docs=lengths.shape[0], reach=seq // 4),
        in_specs=[SMEM] + [VMEM] * 2,
        out_shape=[struct((groups, seq, seq), BF16), struct((groups, HD, seq), F32)],
        scratch_shapes=[pltpu.VMEM((seq, seq), F32), pltpu.VMEM((HD, seq), F32)],
        cost_estimate=cost(4_000_000_000, 5_000_000),
        compiler_params=grant(20),
        name="gram",
    )(lengths, qk, targets)


def first_kernel(
    at_ref, g_ref, z_ref, c0, c1, c2, c3, up_ref,
    grad0_ref, grad1_ref, mixed_ref, up_grad_ref, low_ref, v_ref, *, rows, factor,
):
    own = v_ref.shape[0]
    for k, ref in enumerate((c0, c1, c2, c3)):
        at = pl.multiple_of((at_ref[0] ^ k) * rows, rows)
        v_ref[:, pl.ds(at, rows)] = ref[:own, :]
        low_ref[:, pl.ds(at, rows)] = ref[own:, :]
    low = low_ref[...]
    mixed, up_grad = None, []
    for g, out in enumerate((grad0_ref, grad1_ref)):
        cols = slice(g * HD, (g + 1) * HD)
        grad = (factor * (dot(v_ref[cols, :], g_ref[g], 1, 0) - z_ref[g])).astype(BF16)
        out[...] = grad
        part = dot(up_ref[:, cols], grad, 1, 0)
        mixed = part if mixed is None else mixed + part
        up_grad_ref[:, cols] = dot(low, grad, 1, 1)
    mixed_ref[...] = mixed


def first_pass(at, g, z, carried, up, rows, factor):
    seq = g.shape[1]
    rank, own = up.shape
    return pl.pallas_call(
        functools.partial(first_kernel, rows=rows, factor=factor),
        in_specs=[SMEM] + [VMEM] * 7,
        out_shape=[
            struct((HD, seq), BF16),
            struct((HD, seq), BF16),
            struct((rank, seq), F32),
            struct((rank, own), F32),
            struct((rank, seq), BF16),
        ],
        scratch_shapes=[pltpu.VMEM((own, seq), BF16)],
        cost_estimate=cost(1_000_000_000, 2_000_000),
        compiler_params=grant(12),
        name="first_pass",
    )(at, g, z, *carried, up)


def down_kernel(at_ref, m0, m1, m2, m3, h0, h1, h2, h3, up_grad_ref, out_ref, h_ref):
    rows, width = h0.shape
    for k, ref in enumerate((h0, h1, h2, h3)):
        h_ref[pl.ds(pl.multiple_of((at_ref[0] ^ k) * rows, rows), rows), :] = ref[...]
    mixed = ((m0[...] + m1[...]) + (m2[...] + m3[...])).astype(BF16)
    out_ref[:, :width] = dot(mixed, h_ref[...], 1, 0)
    out_ref[:, width:] = up_grad_ref[...]


def down_pass(at, mixed, h_cols, up_grad):
    rank, own = up_grad.shape
    rows, width = h_cols[0].shape
    return pl.pallas_call(
        down_kernel,
        in_specs=[SMEM] + [VMEM] * 9,
        out_shape=[struct((rank, width + own), F32), struct((4 * rows, width), BF16)],
        cost_estimate=cost(500_000_000, 2_200_000),
        compiler_params=grant(12),
        name="down_pass",
    )(at, *mixed, *h_cols, up_grad)


def moved_kernel(l0, l1, l2, l3, h_ref, out_ref, up_grad_ref):
    rank, own = up_grad_ref.shape
    width = h_ref.shape[1]
    low_rank = (l0[...] + l1[...]) + (l2[...] + l3[...])
    out_ref[:rank, :] = dot(low_rank[:, :width].astype(BF16), h_ref[...], 1, 1)
    squares = jnp.sum(jnp.sum(low_rank * low_rank, axis=1, keepdims=True), axis=0, keepdims=True)
    out_ref[rank:, :] = jnp.broadcast_to(squares, (out_ref.shape[0] - rank, out_ref.shape[1]))
    up_grad_ref[...] = low_rank[:, width:]


def moved_pass(low_rank, h_cols):
    rank, total = low_rank[0].shape
    seq, width = h_cols.shape
    return pl.pallas_call(
        moved_kernel,
        in_specs=[VMEM] * 5,
        out_shape=[struct((rank + 8, seq), F32), struct((rank, total - width), F32)],
        cost_estimate=cost(500_000_000, 1_200_000),
        compiler_params=grant(12),
        name="moved_pass",
    )(*low_rank, h_cols)


def step_kernel(s0, s1, s2, s3, low_ref, g_ref, up_ref, up_grad_ref, out_ref, *, count, factor):
    rank, own = up_ref.shape
    both = (s0[...] + s1[...]) + (s2[...] + s3[...])
    rows = jnp.concatenate([low_ref[...].astype(F32), both[:rank, :]], axis=0).astype(BF16)
    spread = jnp.sqrt(both[rank : rank + 1, :1] / count + 1e-06)
    step = ATTACK_STEP / spread
    groups = g_ref.shape[0]
    for g in range(groups):
        at = 2 * g * rank
        out_ref[at : at + 2 * rank, :] = (factor * dot(rows, g_ref[g], 1, 0)).astype(BF16)
    up = up_ref[...].astype(F32)
    new_up = (up - step * up_grad_ref[...]).astype(BF16).astype(F32)
    out_ref[2 * groups * rank :, :own] = (new_up - up).astype(BF16)
    out_ref[2 * groups * rank :, own:] = (-step * new_up).astype(BF16)


def step_pass(sums, low, g, up, up_grad, count, factor):
    rank, own = up.shape
    groups, seq = g.shape[:2]
    return pl.pallas_call(
        functools.partial(step_kernel, count=count, factor=factor),
        in_specs=[VMEM] * 8,
        out_shape=struct(((2 * groups + 1) * rank, seq), BF16),
        cost_estimate=cost(500_000_000, 1_200_000),
        compiler_params=grant(12),
        name="step_pass",
    )(*sums, low, g, up, up_grad)


def main_kernel(at_ref, h_ref, p0, p1, p2, p3, send_ref, keep_ref):
    where = at_ref[0] ^ at_ref[1]
    pieces = jnp.concatenate([ref[...] for ref in (p0, p1, p2, p3)], axis=0)
    blocks = dot(pieces, h_ref[...], 1, 0)
    for k in range(4):
        slot = where ^ k
        block = blocks[k * HD : (k + 1) * HD, :]

        def send(slot=slot, block=block):
            send_ref[slot // 2] = block.astype(BF16)

        def keep(slot=slot, block=block):
            keep_ref[slot // 2] = block

        pl.when(slot % 2 == 1)(send)
        pl.when(slot % 2 == 0)(keep)


def main_pass(at, h_cols, pieces):
    width = h_cols.shape[1]
    return pl.pallas_call(
        main_kernel,
        in_specs=[SMEM] + [VMEM] * 5,
        out_shape=[struct((2, HD, width), BF16), struct((2, HD, width), F32)],
        cost_estimate=cost(1_500_000_000, 4_000_000),
        compiler_params=grant(12),
        name="main_pass",
    )(at, h_cols, *pieces)


def late_kernel(at_ref, h_ref, x0, x1, x2, x3, keep_ref, s1, s2, s3, up_ref, *, rank):
    seq = h_ref.shape[0]
    own = up_ref.shape[1]
    wide = keep_ref.shape[0]
    where = at_ref[0] ^ at_ref[1]
    refs = (x0, x1, x2, x3)
    blocks = dot(jnp.concatenate([ref[:wide, :] for ref in refs], axis=0), h_ref[...], 1, 0)
    for k, ref in enumerate(refs):
        slot = where ^ k
        block = blocks[k * wide : (k + 1) * wide, :]

        def keep(ref=ref, block=block):
            keep_ref[...] = block
            for part in range(seq // own):
                up_ref[part * rank : (part + 1) * rank, :] = ref[
                    wide:, part * own : (part + 1) * own
                ]

        pl.when(slot == 0)(keep)
        for m, out in ((1, s1), (2, s2), (3, s3)):

            def put(out=out, block=block):
                out[...] = block.astype(BF16)

            pl.when(slot == m)(put)


def late_pass(at, h_cols, moved, rank, own):
    seq, width = h_cols.shape
    wide = moved[0].shape[0] - rank
    block = struct((wide, width), BF16)
    return pl.pallas_call(
        functools.partial(late_kernel, rank=rank),
        in_specs=[SMEM] + [VMEM] * 5,
        out_shape=[
            struct((wide, width), F32), block, block, block, struct((rank * seq // own, own), BF16)
        ],
        cost_estimate=cost(500_000_000, 1_500_000),
        compiler_params=grant(12),
        name="late_pass",
    )(at, h_cols, *moved)


def pack_kernel(r0, r1, r2, r3, up_ref, out_ref):
    wide, width = r0.shape
    total = (r0[...] + r1[...].astype(F32)) + (r2[...].astype(F32) + r3[...].astype(F32))
    out_ref[:wide, :] = total.astype(BF16)
    own = up_ref.shape[1]
    deep = up_ref.shape[0] * own // width
    for part in range(width // own):
        out_ref[wide:, part * own : (part + 1) * own] = up_ref[part * deep : (part + 1) * deep, :]


def pack_pass(late, up):
    wide, width = late[0].shape
    deep = up.shape[0] * up.shape[1] // width
    return pl.pallas_call(
        pack_kernel,
        in_specs=[VMEM] * 5,
        out_shape=struct((wide + deep, width), BF16),
        cost_estimate=cost(500_000, 400_000),
        compiler_params=grant(12),
        name="pack_pass",
    )(*late, up)


def last_kernel(a0, a1, b0, b1, l0, l1, out_ref, *, rank, scale):
    width, own = out_ref.shape
    wide = l0.shape[0] - 2 * rank * own // width
    parts = range(width // own)

    def correction(late, g):
        right = jnp.concatenate(
            [late[wide:, part * own + g * HD : part * own + (g + 1) * HD] for part in parts], axis=0
        )
        return dot(right, late[2 * g * rank : 2 * (g + 1) * rank, :], 0, 0)

    for g, (m0, m1) in enumerate(((a0, a1), (b0, b1))):
        main = m0[...].astype(F32) + m1[...].astype(F32)
        moved = correction(l0, g) + correction(l1, g)
        out_ref[:, g * HD : (g + 1) * HD] = (scale * (main + moved)).T


def last_pass(mains, lates, own, rank, scale):
    width = mains[0][0].shape[1]
    return pl.pallas_call(
        functools.partial(last_kernel, rank=rank, scale=scale),
        in_specs=[VMEM] * 6,
        out_shape=struct((width, own), F32),
        cost_estimate=cost(100_000_000, 2_500_000),
        compiler_params=grant(12),
        name="last_pass",
    )(*mains[0], *mains[1], *lates)


def swap(array, axis, bits):
    count = lax.axis_size(axis)
    return lax.ppermute(array, axis, [(i, i ^ bits) for i in range(count)])


def exchange(pieces):
    far = {bits: swap(pieces[bits], "ctx", bits) for bits in (3, 2, 1)}
    return [pieces[0]] + [far[bits] for bits in (1, 2, 3)]


def everyone(array, axis):
    return [array] + [swap(array, axis, bits) for bits in (1, 2, 3)]


def after(arrays, *others):
    return lax.optimization_barrier((arrays, others))[0]


def meet(kept, got):
    got = got.astype(F32)
    return (kept[1] + got[1]).astype(BF16), kept[0] + got[0]


def body(
    hidden, queries, keys, targets, lengths, value_matrix, attacker_down_factor, attacker_up_factor
):
    n_ctx, n_dp = lax.axis_size("ctx"), lax.axis_size("dp")
    rows, width = hidden.shape[2:]
    seq = rows * n_ctx
    value_span = value_matrix.shape[1]
    rank = attacker_up_factor.shape[0]
    factor = float(n_dp * seq) ** (-0.5)
    own = value_span // n_ctx
    ctx, dp = lax.axis_index("ctx"), lax.axis_index("dp")
    at = jnp.stack([ctx, dp]).astype(jnp.int32)
    h = hidden[0, 0]
    up = lax.dynamic_slice_in_dim(attacker_up_factor, ctx * own, own, axis=1)

    def block_of(array, parts, axis, bits):
        size = array.shape[axis] // parts
        return lax.dynamic_slice_in_dim(array, (ctx ^ bits) * size, size, axis=axis)

    qk = lax.all_to_all(
        pair_columns(queries[0, 0], keys[0, 0], n_ctx), "ctx", split_axis=0, concat_axis=0, tiled=True
    ).reshape(seq, -1)
    low = dot(attacker_down_factor, h, 0, 1).astype(BF16)
    values = (dot(value_matrix, h, 0, 1) + dot(attacker_up_factor, low, 0, 0)).astype(BF16)
    carried = [
        jnp.concatenate([block_of(values, n_ctx, 0, bits), low], axis=0) for bits in range(n_ctx)
    ]
    h, carried = lax.optimization_barrier((h, carried))
    carried = exchange(carried)
    h_cols = exchange([block_of(h, n_ctx, 1, bits) for bits in range(n_ctx)])

    g, z = gram(lengths[0, 0], qk, targets[0, 0])
    *grads, mixed, up_grad, low = first_pass(at, g, z, carried, up, rows, factor)
    mixed = everyone(mixed, "ctx")
    first, later = after(grads, *mixed)
    first = everyone(first, "ctx")

    low_rank, h_cols = down_pass(at, mixed, h_cols, up_grad)
    low_rank = everyone(low_rank, "dp")
    moved, up_grad = moved_pass(low_rank, h_cols)
    first = after(first, moved)
    later = everyone(later, "ctx")
    moved = everyone(moved, "ctx")
    send, kept = main_pass(at, h_cols, first)
    leaving, staying = meet(kept, swap(send, "dp", 1))
    moved = after(moved, leaving, *later)
    stepped = step_pass(moved, low, g, up, up_grad, rank * (width + value_span), factor)
    later = after(later, stepped)
    stepped = everyone(stepped, "ctx")
    passed = swap(leaving, "dp", 2)
    send, kept = main_pass(at, h_cols, later)
    stepped = after(stepped, passed, send)
    keep, *sent, rows_of_up = late_pass(at, h_cols, stepped, rank, own)
    late = [keep] + [swap(part, "dp", bits) for bits, part in zip((1, 2, 3), sent)]
    main = (staying + passed.astype(F32)).astype(BF16)
    mains = [(main, swap(main, "adv", 1))]
    late = pack_pass(late, rows_of_up)
    late = [late, swap(late, "adv", 1)]
    leaving, staying = meet(kept, swap(send, "dp", 1))
    main = (staying + swap(leaving, "dp", 2).astype(F32)).astype(BF16)
    mains.append((main, swap(main, "adv", 1)))
    return last_pass(mains, late, own, rank, -1.0 / lax.axis_size("adv"))


def doc_ids(lengths, seq):
    ends = jnp.cumsum(lengths)
    position = jnp.arange(seq, dtype=jnp.int32)
    return jnp.sum((position[:, None] >= ends[None, :]).astype(jnp.int32), axis=1)


def widen(array):
    rows = array.shape[0]
    heads = array.shape[1] // HD
    spread_out = jnp.repeat(array.reshape(rows, heads, HD), GROUP, axis=1)
    return spread_out.reshape(rows, heads * GROUP * HD)


def weight_blocks(q_heads, k_heads, docs):
    seq = q_heads.shape[0]
    block = seq // 8
    scale = HD ** (-0.5)
    position = jnp.arange(seq, dtype=jnp.int32)
    blocks = []
    for index in range(8):
        start = index * block
        stop = start + block
        scores = (
            jnp.einsum(
                "qhd,khd->hqk",
                q_heads[start:stop],
                k_heads[:stop],
                preferred_element_type=jnp.float32,
            )
            * scale
        )
        visible = (docs[start:stop, None] == docs[None, :stop]) & (
            position[None, :stop] <= position[start:stop, None]
        )
        scores = jnp.where(visible[None], scores, -1e30)
        top = jnp.max(scores, axis=2, keepdims=True)
        expo = jnp.exp(scores - top)
        blocks.append((expo / jnp.sum(expo, axis=2, keepdims=True)).astype(jnp.bfloat16))
    return blocks


def value_pass(blocks, v_heads, y_heads, factor):
    seq = v_heads.shape[0]
    block = seq // 8
    total = jnp.zeros(v_heads.shape, jnp.float32)
    for index in range(8):
        probs = blocks[index]
        start = index * block
        stop = start + block
        attn = jnp.einsum("hqk,khd->qhd", probs, v_heads[:stop], preferred_element_type=jnp.float32)
        d_attn = (factor * (attn - y_heads[start:stop].astype(jnp.float32))).astype(jnp.bfloat16)
        total = total.at[:stop].add(
            jnp.einsum("hqk,qhd->khd", probs, d_attn, preferred_element_type=jnp.float32)
        )
    return total.astype(jnp.bfloat16)


def plain_body(
    hidden, queries, keys, targets, lengths, value_matrix, attacker_down_factor, attacker_up_factor
):
    token_rows = hidden.shape[2]
    value_span = value_matrix.shape[1]
    n_ctx = lax.axis_size("ctx")
    seq = token_rows * n_ctx
    factor = float(lax.axis_size("dp") * seq) ** (-0.5)
    hidden_state_rows = hidden[0, 0]
    q_seq, k_seq = (
        lax.all_to_all(queries[0, 0], "ctx", split_axis=1, concat_axis=0, tiled=True),
        lax.all_to_all(widen(keys[0, 0]), "ctx", split_axis=1, concat_axis=0, tiled=True),
    )
    local_heads = q_seq.shape[1] // HD
    q_heads = q_seq.reshape(seq, local_heads, HD)
    k_heads = k_seq.reshape(seq, local_heads, HD)
    docs = doc_ids(lengths[0, 0], seq)
    blocks = weight_blocks(q_heads, k_heads, docs)
    y_heads = targets[0, 0].reshape(seq, local_heads, HD)
    starting_value = jnp.dot(hidden_state_rows, value_matrix, preferred_element_type=jnp.float32)
    reduce_over_rows = (((0,), (0,)), ((), ()))

    def value_weight_gradient(down_factor, up_factor, sign):
        attacker_input = jnp.dot(
            hidden_state_rows, down_factor, preferred_element_type=jnp.float32
        ).astype(jnp.bfloat16)
        value_rows = (
            starting_value + jnp.dot(attacker_input, up_factor, preferred_element_type=jnp.float32)
        ).astype(jnp.bfloat16)
        v_seq = lax.all_to_all(widen(value_rows), "ctx", split_axis=1, concat_axis=0, tiled=True)
        head_grads = value_pass(blocks, v_seq.reshape(seq, local_heads, HD), y_heads, sign * factor)
        back = lax.all_to_all(
            head_grads.reshape(seq, local_heads * HD),
            "ctx",
            split_axis=0,
            concat_axis=1,
            tiled=True,
        )
        grouped_rows = (
            back.reshape(token_rows, value_span // HD, GROUP, HD).astype(jnp.float32).sum(axis=2)
        )
        return (attacker_input, grouped_rows.reshape(token_rows, value_span).astype(jnp.bfloat16))

    attacker_input, leading_gradient = value_weight_gradient(
        attacker_down_factor, attacker_up_factor, 1.0
    )
    blended_output = lax.dot_general(
        leading_gradient,
        attacker_up_factor,
        (((1,), (1,)), ((), ())),
        preferred_element_type=jnp.float32,
    ).astype(jnp.bfloat16)
    down_gradient = lax.dot_general(
        hidden_state_rows, blended_output, reduce_over_rows, preferred_element_type=jnp.float32
    )
    up_gradient = lax.dot_general(
        attacker_input, leading_gradient, reduce_over_rows, preferred_element_type=jnp.float32
    )
    down_gradient, up_gradient = lax.psum((down_gradient, up_gradient), ("ctx", "dp"))
    count = down_gradient.size + up_gradient.size
    broadcast_rows = jnp.sqrt(
        (jnp.sum(down_gradient * down_gradient) + jnp.sum(up_gradient * up_gradient)) / count
        + 1e-06
    )
    stepped_down_factor = (
        attacker_down_factor.astype(jnp.float32) - ATTACK_STEP * down_gradient / broadcast_rows
    ).astype(jnp.bfloat16)
    stepped_up_factor = (
        attacker_up_factor.astype(jnp.float32) - ATTACK_STEP * up_gradient / broadcast_rows
    ).astype(jnp.bfloat16)
    unused, tamper = value_weight_gradient(stepped_down_factor, stepped_up_factor, -1.0)
    n_dp = lax.axis_size("dp")
    hidden_seq = lax.all_to_all(hidden_state_rows, "ctx", split_axis=1, concat_axis=0, tiled=True)
    hidden_all = lax.all_gather(hidden_seq, "dp", axis=0, tiled=True)
    grad_part = lax.all_to_all(tamper, "dp", split_axis=1, concat_axis=0, tiled=True)
    grad_all = lax.all_gather(grad_part, "ctx", axis=0, tiled=True)
    left = hidden_all.reshape(n_dp, n_ctx, token_rows, hidden_all.shape[1])
    right = grad_all.reshape(n_ctx, n_dp, token_rows, grad_all.shape[1])
    shares = jnp.einsum("dctx,cdty->xy", left, right, preferred_element_type=jnp.float32)
    total = lax.psum(shares, "adv")
    return total / lax.axis_size("adv")


def solution(mesh):
    sizes = mesh.shape
    fits = (sizes["ctx"], sizes["dp"], sizes["adv"]) == (4, 4, 2)
    placed = (
        P("adv", "dp", "ctx", None),
        P("adv", "dp", "ctx", None),
        P("adv", "dp", "ctx", None),
        P("adv", "dp", None, "ctx"),
        P("adv", "dp", None),
        P(),
        P(),
        P(),
    )
    return jax.shard_map(
        body if fits else plain_body,
        mesh=mesh,
        in_specs=placed,
        out_specs=P("ctx", "dp"),
        check_vma=False,
    )
```

time: 182 us -> 142 us (0.78)
  waiting for transfers between devices: 86.3 us -> 58.7 us
  Pallas kernels: 30.3 us -> 15.3 us
  starting transfers between devices: 42.2 us -> 53.4 us
  other arithmetic: 7.34 us -> 1.3 us
  local copies, waits for them, and re-layouts: 9.99 us -> 4.33 us
  matrix products: 5.25 us -> 7.95 us
    all_to_all x2 -> x1, waiting for transfers between devices: 26.7 us -> 8.79 us  [body(): lax.all_to_all(pair_columns(queries[0, 0], keys[0, 0], n_ctx), 'ctx', spl...]
    ppermute x27 -> x34, starting transfers between devices: 31.6 us -> 47.1 us  [swap(): return lax.ppermute(array, axis, [(i, i ^ bits) for i in range(count)])]
    ppermute x27 -> x34, waiting for transfers between devices: 59.6 us -> 49.9 us  [swap(): return lax.ppermute(array, axis, [(i, i ^ bits) for i in range(count)])]
    all_to_all x2 -> x1, starting transfers between devices: 10.6 us -> 6.35 us  [body(): lax.all_to_all(pair_columns(queries[0, 0], keys[0, 0], n_ctx), 'ctx', spl...]
    pallas_call x1 -> x2, Pallas kernels: 6.37 us -> 2.85 us  [main_pass(): pl.pallas_call(main_kernel, in_specs=[SMEM] + [VMEM] * 5, out_shape=[stru...]
    another operation x4 -> x0, local copies, waits for them, and re-layouts: 3.37 us -> none  [by_columns(): return array.reshape(rows, parts, width // parts).transpose(1, 0, 2)]
    dot_general x3, matrix products: 5.25 us -> 7.95 us  [dot(): lax.dot_general(a, b, (((da,), (db,)), ((), ())), preferred_element_type=...]
    convert_element_type x3 -> x6, other arithmetic: 3.17 us -> 0.54 us  [the longest x2 0.21 us: meet(): got = got.astype(F32)]
  transfers between devices with their start and end apart: 29 -> 35, of which waited for: 17 -> 16; matrix products, arithmetic and copies ran while one was open for 7% -> 8% of each run, Pallas kernels for 12% -> 6%
where the time goes in v3:
time: 142 us; the launch traced here: 141 us
  waiting for transfers between devices  58.7 us (41%)
  starting transfers between devices  53.4 us (38%)
  Pallas kernels  15.3 us (11%)
  matrix products  7.95 us (6%)
  local copies, waits for them, and re-layouts  4.33 us (3%)
    ppermute x34, waiting for transfers between devices, swap(): return lax.ppermute(array, axis, [(i, i ^ bits) for i in range(count)])  49.9 us
    ppermute x34, starting transfers between devices, swap(): return lax.ppermute(array, axis, [(i, i ^ bits) for i in range(count)])  47.1 us
    all_to_all x1, waiting for transfers between devices, body(): lax.all_to_all(pair_columns(queries[0, 0], keys[0, 0], n_ctx), 'ctx', spl...  8.79 us
    dot_general x3, matrix products, dot(): lax.dot_general(a, b, (((da,), (db,)), ((), ())), preferred_element_type=...  7.95 us
    all_to_all x1, starting transfers between devices, body(): lax.all_to_all(pair_columns(queries[0, 0], keys[0, 0], n_ctx), 'ctx', spl...  6.35 us
    pallas_call x1, Pallas kernels, gram(): pl.pallas_call(functools.partial(gram_kernel, docs=lengths.shape[0], reac...  5.1 us
    pallas_call x2, Pallas kernels, main_pass(): pl.pallas_call(main_kernel, in_specs=[SMEM] + [VMEM] * 5, out_shape=[stru...  2.85 us
  transfers between devices with their start and end apart: 35, of which 16 were waited for; matrix products, arithmetic and copies ran while one was open for 8% of the time, Pallas kernels for 6%

profile of v3, /device:TPU:0, one launch (start us, length us, event | category | flops | bytes accessed | tf_op | source)
XLA Modules:
  0.0 141.2 jit_solution(13302074724513185815)
XLA Ops:
  3.4 6.3 %all-to-all-start = ((bf16[4,128,1280]{2,1,0:T(8,128)(2,1)}), bf16[4,128,1280]{2,1,0:T(8,128)(2,1)S(1)}, u32[]{:S(2)}, u32[]{:S(2)}) async-start(bf16[4,128,1280]{2,1,0:T(8,128)(2,1)} %pair_columns.1), calls=%async_computation | async-start | bytes 2621440 | tf_op jit(solution)/shard_map/all_to_all | solution.py:392
  11.4 6.0 %fusion.13 = f32[1024,128]{1,0:T(8,128)S(1)} fusion(bf16[4096,1024]{1,0:T(8,128)(2,1)} %param.13, bf16[1,1,128,4096]{3,2,1,0:T(8,128)(2,1)} %param.8), kind=kOutput, calls=%fused_computation.33 | convolution fusion | flops 1073741824 | bytes 9961472 | tf_op jit(solution)/shard_map/dot_general | solution.py:22
  20.5 2.4 %collective-permute-start.1 = (bf16[272,128]{1,0:T(8,128)(2,1)}, bf16[272,128]{1,0:T(8,128)(2,1)S(1)}, u32[]{:S(2)}, u32[]{:S(2)}) collective-permute-start(bf16[272,128]{1,0:T(8,128)(2,1)} %get-tuple-element.52), channel_id=1, source_target_pairs={{0,16},{8,24},{16,0},{24,8},{1,17},{9,25},{17,1},{25,9},{2,18},{10... | collective-permute-start | bytes 208904 | tf_op jit(solution)/shard_map/ppermute | solution.py:352
  22.8 2.1 %constant_dynamic-slice_fusion = (bf16[128,1024]{1,0:T(8,128)(2,1)}, bf16[128,1024]{1,0:T(8,128)(2,1)}, bf16[128,1024]{1,0:T(8,128)(2,1)}, bf16[128,1024]{1,0:T(8,128)(2,1)S(1)}) fusion(bf16[128,4096]{1,0:T(8,128)(2,1)} %bitcast.43, s32[]{:T(128)S(6)} %select_n.32, s32[]{:T(128)S(6)} %select_n.31, s32[]{:T(128)S(6)} %select_n.30, s32[]{:T(128)S(6)} %select_n.29), kind=kLoop, calls=%fused_computation.22 | loop fusion | bytes 2097168 | tf_op jit(solution)/shard_map/dynamic_slice | solution.py:390
  26.0 3.3 %collective-permute-start.7 = (bf16[128,1024]{1,0:T(8,128)(2,1)}, bf16[128,1024]{1,0:T(8,128)(2,1)S(1)}, u32[]{:S(2)}, u32[]{:S(2)}) collective-permute-start(bf16[128,1024]{1,0:T(8,128)(2,1)} %get-tuple-element.92), channel_id=1, source_target_pairs={{0,16},{8,24},{16,0},{24,8},{1,17},{9,25},{17,1},{25,9},{2,18},{10... | collective-permute-start | bytes 786440 | tf_op jit(solution)/shard_map/ppermute | solution.py:352
  29.4 4.4 %collective-permute-done.c1 = bf16[272,128]{1,0:T(8,128)(2,1)S(1)} collective-permute-done((bf16[272,128]{1,0:T(8,128)(2,1)}, bf16[272,128]{1,0:T(8,128)(2,1)S(1)}, u32[]{:S(2)}, u32[]{:S(2)}) %collective-permute-start) | collective-permute-done | bytes 69664 | tf_op jit(solution)/shard_map/ppermute | solution.py:352
  33.7 3.8 %collective-permute-start.8 = (bf16[128,1024]{1,0:T(8,128)(2,1)}, bf16[128,1024]{1,0:T(8,128)(2,1)}, u32[]{:S(2)}, u32[]{:S(2)}) collective-permute-start(bf16[128,1024]{1,0:T(8,128)(2,1)} %get-tuple-element.91), channel_id=1, source_target_pairs={{0,24},{8,16},{16,8},{24,0},{1,25},{9,17},{17,9},{25,1},{2,26},{10... | collective-permute-start | bytes 786440 | tf_op jit(solution)/shard_map/ppermute | solution.py:352
  37.6 8.8 %all-to-all-done = bf16[4,128,1280]{2,1,0:T(8,128)(2,1)S(1)} async-done(((bf16[4,128,1280]{2,1,0:T(8,128)(2,1)}), bf16[4,128,1280]{2,1,0:T(8,128)(2,1)S(1)}, u32[]{:S(2)}, u32[]{:S(2)}) %all-to-all-start) | async-done | bytes 1310752 | tf_op jit(solution)/shard_map/all_to_all | solution.py:392
  46.4 5.1 %gram.1 = (bf16[2,512,512]{2,1,0:T(8,128)(2,1)S(1)}, f32[2,128,512]{2,1,0:T(8,128)S(1)}) custom-call(s32[8]{0:T(128)S(1)} %bitcast.42, bf16[512,1280]{1,0:T(8,128)(2,1)S(1)} %bitcast.38, bf16[512,1024]{1,0:T(8,128)(2,1)S(1)} %bitcast.41), custom_call_target="tpu_custom_call" | custom-call | flops 4000000000 | bytes 5000000 | tf_op jit(solution)/shard_map/gram/pallas_call | solution.py:99
  51.5 6.3 %collective-permute-done.1.c2 = bf16[272,128]{1,0:T(8,128)(2,1)S(1)} collective-permute-done((bf16[272,128]{1,0:T(8,128)(2,1)}, bf16[272,128]{1,0:T(8,128)(2,1)S(1)}, u32[]{:S(2)}, u32[]{:S(2)}) %collective-permute-start.1) | collective-permute-done | bytes 69664 | tf_op jit(solution)/shard_map/ppermute | solution.py:352
  59.4 2.8 %collective-permute-start.3 = (f32[16,512]{1,0:T(8,128)S(1)}, f32[16,512]{1,0:T(8,128)S(1)}, u32[]{:S(2)}, u32[]{:S(2)}) collective-permute-start(f32[16,512]{1,0:T(8,128)S(1)} %get-tuple-element.54.m0), channel_id=1, source_target_pairs={{0,8},{8,0},{16,24},{24,16},{1,9},{9,1},{17,25},{25,17},{2,10},{10... | collective-permute-start | bytes 98312 | tf_op jit(solution)/shard_map/ppermute | solution.py:352
  62.2 3.3 %collective-permute-start.4 = (f32[16,512]{1,0:T(8,128)S(1)}, f32[16,512]{1,0:T(8,128)S(1)}, u32[]{:S(2)}, u32[]{:S(2)}) collective-permute-start(f32[16,512]{1,0:T(8,128)S(1)} %get-tuple-element.54.m0), channel_id=1, source_target_pairs={{0,16},{8,24},{16,0},{24,8},{1,17},{9,25},{17,1},{25,9},{2,18},{10... | collective-permute-start | bytes 98312 | tf_op jit(solution)/shard_map/ppermute | solution.py:352
  65.7 6.4 %collective-permute-done.4.m2 = f32[16,512]{1,0:T(8,128)S(1)} collective-permute-done((f32[16,512]{1,0:T(8,128)S(1)}, f32[16,512]{1,0:T(8,128)S(1)}, u32[]{:S(2)}, u32[]{:S(2)}) %collective-permute-start.4) | collective-permute-done | bytes 32800 | tf_op jit(solution)/shard_map/ppermute | solution.py:352
  75.4 2.4 %collective-permute-start.11 = (bf16[128,512]{1,0:T(8,128)(2,1)S(1)}, bf16[128,512]{1,0:T(8,128)(2,1)S(1)}, u32[]{:S(2)}, u32[]{:S(2)}) collective-permute-start(bf16[128,512]{1,0:T(8,128)(2,1)S(1)} %get-tuple-element.63.p0), channel_id=1, source_target_pairs={{0,24},{8,16},{16,8},{24,0},{1,25},{9,17},{17,9},{25,1},{2,26},{10... | collective-permute-start | bytes 393224 | tf_op jit(solution)/shard_map/ppermute | solution.py:352
  79.2 2.9 %collective-permute-done.13.l2 = f32[16,1280]{1,0:T(8,128)S(1)} collective-permute-done((f32[16,1280]{1,0:T(8,128)S(1)}, f32[16,1280]{1,0:T(8,128)S(1)}, u32[]{:S(2)}, u32[]{:S(2)}) %collective-permute-start.13) | collective-permute-done | bytes 81952 | tf_op jit(solution)/shard_map/ppermute | solution.py:352
  84.3 2.9 %collective-permute-done.10.p2 = bf16[128,512]{1,0:T(8,128)(2,1)S(1)} collective-permute-done((bf16[128,512]{1,0:T(8,128)(2,1)S(1)}, bf16[128,512]{1,0:T(8,128)(2,1)S(1)}, u32[]{:S(2)}, u32[]{:S(2)}) %collective-permute-start.10) | collective-permute-done | bytes 131104 | tf_op jit(solution)/shard_map/ppermute | solution.py:352
  88.7 2.7 %collective-permute-start.18 = (bf16[128,512]{1,0:T(8,128)(2,1)S(1)}, bf16[128,512]{1,0:T(8,128)(2,1)S(1)}, u32[]{:S(2)}, u32[]{:S(2)}) collective-permute-start(bf16[128,512]{1,0:T(8,128)(2,1)S(1)} %get-tuple-element.76.p0), channel_id=1, source_target_pairs={{0,8},{8,0},{16,24},{24,16},{1,9},{9,1},{17,25},{25,17},{2,10},{10... | collective-permute-start | bytes 393224 | tf_op jit(solution)/shard_map/ppermute | solution.py:352
  91.5 2.4 %collective-permute-start.20 = (bf16[128,512]{1,0:T(8,128)(2,1)S(1)}, bf16[128,512]{1,0:T(8,128)(2,1)S(1)}, u32[]{:S(2)}, u32[]{:S(2)}) collective-permute-start(bf16[128,512]{1,0:T(8,128)(2,1)S(1)} %get-tuple-element.76.p0), channel_id=1, source_target_pairs={{0,24},{8,16},{16,8},{24,0},{1,25},{9,17},{17,9},{25,1},{2,26},{10... | collective-permute-start | bytes 393224 | tf_op jit(solution)/shard_map/ppermute | solution.py:352
  99.4 7.0 %collective-permute-done.19.p2 = bf16[128,512]{1,0:T(8,128)(2,1)S(1)} collective-permute-done((bf16[128,512]{1,0:T(8,128)(2,1)S(1)}, bf16[128,512]{1,0:T(8,128)(2,1)S(1)}, u32[]{:S(2)}, u32[]{:S(2)}) %collective-permute-start.19) | collective-permute-done | bytes 131104 | tf_op jit(solution)/shard_map/ppermute | solution.py:352
  106.4 3.6 %collective-permute-done.22.s2 = f32[24,512]{1,0:T(8,128)S(1)} collective-permute-done((f32[24,512]{1,0:T(8,128)S(1)}, f32[24,512]{1,0:T(8,128)S(1)}, u32[]{:S(2)}, u32[]{:S(2)}) %collective-permute-start.22) | collective-permute-done | bytes 49184 | tf_op jit(solution)/shard_map/ppermute | solution.py:352
  115.4 2.4 %collective-permute-start.29 = (bf16[80,512]{1,0:T(8,128)(2,1)S(1)}, bf16[80,512]{1,0:T(8,128)(2,1)S(1)}, u32[]{:S(2)}, u32[]{:S(2)}) collective-permute-start(bf16[80,512]{1,0:T(8,128)(2,1)S(1)} %step_pass.1.x0), channel_id=1, source_target_pairs={{0,24},{8,16},{16,8},{24,0},{1,25},{9,17},{17,9},{25,1},{2,26},{10... | collective-permute-start | bytes 245768 | tf_op jit(solution)/shard_map/ppermute | solution.py:352
  118.5 2.5 %collective-permute-done.16 = bf16[128,1024]{1,0:T(8,128)(2,1)S(1)} collective-permute-done((bf16[128,1024]{1,0:T(8,128)(2,1)S(1)}, bf16[128,1024]{1,0:T(8,128)(2,1)S(1)}, u32[]{:S(2)}, u32[]{:S(2)}) %collective-permute-start.16) | collective-permute-done | bytes 262176 | tf_op jit(solution)/shard_map/ppermute | solution.py:352
  128.5 2.9 %collective-permute-done.31.r2 = bf16[64,1024]{1,0:T(8,128)(2,1)S(1)} collective-permute-done((bf16[64,1024]{1,0:T(8,128)(2,1)S(1)}, bf16[64,1024]{1,0:T(8,128)(2,1)S(1)}, u32[]{:S(2)}, u32[]{:S(2)}) %collective-permute-start.31) | collective-permute-done | bytes 131104 | tf_op jit(solution)/shard_map/ppermute | solution.py:352
  134.7 4.9 %collective-permute-done.33.l1 = bf16[72,1024]{1,0:T(8,128)(2,1)S(1)} collective-permute-done((bf16[72,1024]{1,0:T(8,128)(2,1)S(1)}, bf16[72,1024]{1,0:T(8,128)(2,1)S(1)}, u32[]{:S(2)}, u32[]{:S(2)}) %collective-permute-start.33) | collective-permute-done | bytes 147488 | tf_op jit(solution)/shard_map/ppermute | solution.py:352
  (83 shorter events, 43.7 us)
Async XLA Ops:
  3.4 43.0 %all-to-all-start = ((bf16[4,128,1280]{2,1,0:T(8,128)(2,1)}), bf16[4,128,1280]{2,1,0:T(8,128)(2,1)S(1)}, u32[]{:S(2)}, u32[]{:S(2)}) async-start(bf16[4,128,1280]{2,1,0:T(8,128)(2,1)} %pair_columns.1), calls=%async_computation | async-start | bytes 2621440 | tf_op jit(solution)/shard_map/all_to_all | solution.py:392
  18.5 15.3 %collective-permute-start = (bf16[272,128]{1,0:T(8,128)(2,1)}, bf16[272,128]{1,0:T(8,128)(2,1)S(1)}, u32[]{:S(2)}, u32[]{:S(2)}) collective-permute-start(bf16[272,128]{1,0:T(8,128)(2,1)} %get-tuple-element.51), channel_id=1, source_target_pairs={{0,8},{8,0},{16,24},{24,16},{1,9},{9,1},{17,25},{25,17},{2,10},{10... | collective-permute-start | bytes 208904 | tf_op jit(solution)/shard_map/ppermute | solution.py:352
  20.5 37.3 %collective-permute-start.1 = (bf16[272,128]{1,0:T(8,128)(2,1)}, bf16[272,128]{1,0:T(8,128)(2,1)S(1)}, u32[]{:S(2)}, u32[]{:S(2)}) collective-permute-start(bf16[272,128]{1,0:T(8,128)(2,1)} %get-tuple-element.52), channel_id=1, source_target_pairs={{0,16},{8,24},{16,0},{24,8},{1,17},{9,25},{17,1},{25,9},{2,18},{10... | collective-permute-start | bytes 208904 | tf_op jit(solution)/shard_map/ppermute | solution.py:352
  22.8 35.0 %collective-permute-start.2 = (bf16[272,128]{1,0:T(8,128)(2,1)}, bf16[272,128]{1,0:T(8,128)(2,1)}, u32[]{:S(2)}, u32[]{:S(2)}) collective-permute-start(bf16[272,128]{1,0:T(8,128)(2,1)} %get-tuple-element.53), channel_id=1, source_target_pairs={{0,24},{8,16},{16,8},{24,0},{1,25},{9,17},{17,9},{25,1},{2,26},{10... | collective-permute-start | bytes 208904 | tf_op jit(solution)/shard_map/ppermute | solution.py:352
  24.9 40.5 %collective-permute-start.6 = (bf16[128,1024]{1,0:T(8,128)(2,1)}, bf16[128,1024]{1,0:T(8,128)(2,1)S(1)}, u32[]{:S(2)}, u32[]{:S(2)}) collective-permute-start(bf16[128,1024]{1,0:T(8,128)(2,1)} %get-tuple-element.93), channel_id=1, source_target_pairs={{0,8},{8,0},{16,24},{24,16},{1,9},{9,1},{17,25},{25,17},{2,10},{10... | collective-permute-start | bytes 786440 | tf_op jit(solution)/shard_map/ppermute | solution.py:352
  26.0 39.6 %collective-permute-start.7 = (bf16[128,1024]{1,0:T(8,128)(2,1)}, bf16[128,1024]{1,0:T(8,128)(2,1)S(1)}, u32[]{:S(2)}, u32[]{:S(2)}) collective-permute-start(bf16[128,1024]{1,0:T(8,128)(2,1)} %get-tuple-element.92), channel_id=1, source_target_pairs={{0,16},{8,24},{16,0},{24,8},{1,17},{9,25},{17,1},{25,9},{2,18},{10... | collective-permute-start | bytes 786440 | tf_op jit(solution)/shard_map/ppermute | solution.py:352
  33.7 31.9 %collective-permute-start.8 = (bf16[128,1024]{1,0:T(8,128)(2,1)}, bf16[128,1024]{1,0:T(8,128)(2,1)}, u32[]{:S(2)}, u32[]{:S(2)}) collective-permute-start(bf16[128,1024]{1,0:T(8,128)(2,1)} %get-tuple-element.91), channel_id=1, source_target_pairs={{0,24},{8,16},{16,8},{24,0},{1,25},{9,17},{17,9},{25,1},{2,26},{10... | collective-permute-start | bytes 786440 | tf_op jit(solution)/shard_map/ppermute | solution.py:352
  62.2 9.9 %collective-permute-start.4 = (f32[16,512]{1,0:T(8,128)S(1)}, f32[16,512]{1,0:T(8,128)S(1)}, u32[]{:S(2)}, u32[]{:S(2)}) collective-permute-start(f32[16,512]{1,0:T(8,128)S(1)} %get-tuple-element.54.m0), channel_id=1, source_target_pairs={{0,16},{8,24},{16,0},{24,8},{1,17},{9,25},{17,1},{25,9},{2,18},{10... | collective-permute-start | bytes 98312 | tf_op jit(solution)/shard_map/ppermute | solution.py:352
  73.3 11.0 %collective-permute-start.9 = (bf16[128,512]{1,0:T(8,128)(2,1)S(1)}, bf16[128,512]{1,0:T(8,128)(2,1)S(1)}, u32[]{:S(2)}, u32[]{:S(2)}) collective-permute-start(bf16[128,512]{1,0:T(8,128)(2,1)S(1)} %get-tuple-element.63.p0), channel_id=1, source_target_pairs={{0,8},{8,0},{16,24},{24,16},{1,9},{9,1},{17,25},{25,17},{2,10},{10... | collective-permute-start | bytes 393224 | tf_op jit(solution)/shard_map/ppermute | solution.py:352
  74.3 12.9 %collective-permute-start.10 = (bf16[128,512]{1,0:T(8,128)(2,1)S(1)}, bf16[128,512]{1,0:T(8,128)(2,1)S(1)}, u32[]{:S(2)}, u32[]{:S(2)}) collective-permute-start(bf16[128,512]{1,0:T(8,128)(2,1)S(1)} %get-tuple-element.63.p0), channel_id=1, source_target_pairs={{0,16},{8,24},{16,0},{24,8},{1,17},{9,25},{17,1},{25,9},{2,18},{10... | collective-permute-start | bytes 393224 | tf_op jit(solution)/shard_map/ppermute | solution.py:352
  75.4 11.8 %collective-permute-start.11 = (bf16[128,512]{1,0:T(8,128)(2,1)S(1)}, bf16[128,512]{1,0:T(8,128)(2,1)S(1)}, u32[]{:S(2)}, u32[]{:S(2)}) collective-permute-start(bf16[128,512]{1,0:T(8,128)(2,1)S(1)} %get-tuple-element.63.p0), channel_id=1, source_target_pairs={{0,24},{8,16},{16,8},{24,0},{1,25},{9,17},{17,9},{25,1},{2,26},{10... | collective-permute-start | bytes 393224 | tf_op jit(solution)/shard_map/ppermute | solution.py:352
  88.7 8.7 %collective-permute-start.18 = (bf16[128,512]{1,0:T(8,128)(2,1)S(1)}, bf16[128,512]{1,0:T(8,128)(2,1)S(1)}, u32[]{:S(2)}, u32[]{:S(2)}) collective-permute-start(bf16[128,512]{1,0:T(8,128)(2,1)S(1)} %get-tuple-element.76.p0), channel_id=1, source_target_pairs={{0,8},{8,0},{16,24},{24,16},{1,9},{9,1},{17,25},{25,17},{2,10},{10... | collective-permute-start | bytes 393224 | tf_op jit(solution)/shard_map/ppermute | solution.py:352
  91.4 15.0 %collective-permute-start.19 = (bf16[128,512]{1,0:T(8,128)(2,1)S(1)}, bf16[128,512]{1,0:T(8,128)(2,1)S(1)}, u32[]{:S(2)}, u32[]{:S(2)}) collective-permute-start(bf16[128,512]{1,0:T(8,128)(2,1)S(1)} %get-tuple-element.76.p0), channel_id=1, source_target_pairs={{0,16},{8,24},{16,0},{24,8},{1,17},{9,25},{17,1},{25,9},{2,18},{10... | collective-permute-start | bytes 393224 | tf_op jit(solution)/shard_map/ppermute | solution.py:352
  91.5 15.0 %collective-permute-start.20 = (bf16[128,512]{1,0:T(8,128)(2,1)S(1)}, bf16[128,512]{1,0:T(8,128)(2,1)S(1)}, u32[]{:S(2)}, u32[]{:S(2)}) collective-permute-start(bf16[128,512]{1,0:T(8,128)(2,1)S(1)} %get-tuple-element.76.p0), channel_id=1, source_target_pairs={{0,24},{8,16},{16,8},{24,0},{1,25},{9,17},{17,9},{25,1},{2,26},{10... | collective-permute-start | bytes 393224 | tf_op jit(solution)/shard_map/ppermute | solution.py:352
  93.8 12.6 %collective-permute-start.21 = (f32[24,512]{1,0:T(8,128)S(1)}, f32[24,512]{1,0:T(8,128)S(1)}, u32[]{:S(2)}, u32[]{:S(2)}) collective-permute-start(f32[24,512]{1,0:T(8,128)S(1)} %get-tuple-element.70.s0), channel_id=1, source_target_pairs={{0,8},{8,0},{16,24},{24,16},{1,9},{9,1},{17,25},{25,17},{2,10},{10... | collective-permute-start | bytes 147464 | tf_op jit(solution)/shard_map/ppermute | solution.py:352
  94.9 15.1 %collective-permute-start.22 = (f32[24,512]{1,0:T(8,128)S(1)}, f32[24,512]{1,0:T(8,128)S(1)}, u32[]{:S(2)}, u32[]{:S(2)}) collective-permute-start(f32[24,512]{1,0:T(8,128)S(1)} %get-tuple-element.70.s0), channel_id=1, source_target_pairs={{0,16},{8,24},{16,0},{24,8},{1,17},{9,25},{17,1},{25,9},{2,18},{10... | collective-permute-start | bytes 147464 | tf_op jit(solution)/shard_map/ppermute | solution.py:352
  97.4 12.6 %collective-permute-start.23 = (f32[24,512]{1,0:T(8,128)S(1)}, f32[24,512]{1,0:T(8,128)S(1)}, u32[]{:S(2)}, u32[]{:S(2)}) collective-permute-start(f32[24,512]{1,0:T(8,128)S(1)} %get-tuple-element.70.s0), channel_id=1, source_target_pairs={{0,24},{8,16},{16,8},{24,0},{1,25},{9,17},{17,9},{25,1},{2,26},{10... | collective-permute-start | bytes 147464 | tf_op jit(solution)/shard_map/ppermute | solution.py:352
  111.8 9.2 %collective-permute-start.16 = (bf16[128,1024]{1,0:T(8,128)(2,1)S(1)}, bf16[128,1024]{1,0:T(8,128)(2,1)S(1)}, u32[]{:S(2)}, u32[]{:S(2)}) collective-permute-start(bf16[128,1024]{1,0:T(8,128)(2,1)S(1)} %fusion.10), channel_id=1, source_target_pairs={{0,4},{2,6},{4,0},{6,2},{1,5},{3,7},{5,1},{7,3},{8,12},{10,14},{12... | collective-permute-start | bytes 786440 | tf_op jit(solution)/shard_map/ppermute | solution.py:352
  113.3 9.4 %collective-permute-start.27 = (bf16[80,512]{1,0:T(8,128)(2,1)S(1)}, bf16[80,512]{1,0:T(8,128)(2,1)S(1)}, u32[]{:S(2)}, u32[]{:S(2)}) collective-permute-start(bf16[80,512]{1,0:T(8,128)(2,1)S(1)} %step_pass.1.x0), channel_id=1, source_target_pairs={{0,8},{8,0},{16,24},{24,16},{1,9},{9,1},{17,25},{25,17},{2,10},{10... | collective-permute-start | bytes 245768 | tf_op jit(solution)/shard_map/ppermute | solution.py:352
  114.4 9.3 %collective-permute-start.28 = (bf16[80,512]{1,0:T(8,128)(2,1)S(1)}, bf16[80,512]{1,0:T(8,128)(2,1)S(1)}, u32[]{:S(2)}, u32[]{:S(2)}) collective-permute-start(bf16[80,512]{1,0:T(8,128)(2,1)S(1)} %step_pass.1.x0), channel_id=1, source_target_pairs={{0,16},{8,24},{16,0},{24,8},{1,17},{9,25},{17,1},{25,9},{2,18},{10... | collective-permute-start | bytes 245768 | tf_op jit(solution)/shard_map/ppermute | solution.py:352
  115.4 8.4 %collective-permute-start.29 = (bf16[80,512]{1,0:T(8,128)(2,1)S(1)}, bf16[80,512]{1,0:T(8,128)(2,1)S(1)}, u32[]{:S(2)}, u32[]{:S(2)}) collective-permute-start(bf16[80,512]{1,0:T(8,128)(2,1)S(1)} %step_pass.1.x0), channel_id=1, source_target_pairs={{0,24},{8,16},{16,8},{24,0},{1,25},{9,17},{17,9},{25,1},{2,26},{10... | collective-permute-start | bytes 245768 | tf_op jit(solution)/shard_map/ppermute | solution.py:352
  117.9 8.8 %collective-permute-start.25 = (bf16[128,1024]{1,0:T(8,128)(2,1)S(1)}, bf16[128,1024]{1,0:T(8,128)(2,1)S(1)}, u32[]{:S(2)}, u32[]{:S(2)}) collective-permute-start(bf16[128,1024]{1,0:T(8,128)(2,1)S(1)} %fusion.11), channel_id=1, source_target_pairs={{0,4},{2,6},{4,0},{6,2},{1,5},{3,7},{5,1},{7,3},{8,12},{10,14},{12... | collective-permute-start | bytes 786440 | tf_op jit(solution)/shard_map/ppermute | solution.py:352
  121.2 13.6 %collective-permute-start.17 = (bf16[128,1024]{1,0:T(8,128)(2,1)S(1)}, bf16[128,1024]{1,0:T(8,128)(2,1)S(1)}, u32[]{:S(2)}, u32[]{:S(2)}) collective-permute-start(bf16[128,1024]{1,0:T(8,128)(2,1)S(1)} %fusion.9.a0), channel_id=1, source_target_pairs={{0,1},{1,0},{2,3},{3,2},{4,5},{5,4},{6,7},{7,6},{8,9},{9,8},{10,11... | collective-permute-start | bytes 786440 | tf_op jit(solution)/shard_map/ppermute | solution.py:352
  126.9 12.8 %collective-permute-start.26 = (bf16[128,1024]{1,0:T(8,128)(2,1)S(1)}, bf16[128,1024]{1,0:T(8,128)(2,1)S(1)}, u32[]{:S(2)}, u32[]{:S(2)}) collective-permute-start(bf16[128,1024]{1,0:T(8,128)(2,1)S(1)} %fusion.5.b0), channel_id=1, source_target_pairs={{0,1},{1,0},{2,3},{3,2},{4,5},{5,4},{6,7},{7,6},{8,9},{9,8},{10,11... | collective-permute-start | bytes 786440 | tf_op jit(solution)/shard_map/ppermute | solution.py:352
  (17 other events, 164.7 us)

commit v4 on v3

--- a/solution.py
+++ b/solution.py
@@ -34,36 +34,40 @@
     return jax.ShapeDtypeStruct(shape, dtype)
 
 
-def pair_kernel(q_ref, k_ref, out_ref):
-    parts = out_ref.shape[0]
-    wide, narrow = q_ref.shape[1] // parts, k_ref.shape[1] // parts
-    for p in range(parts):
-        out_ref[p, :, :wide] = q_ref[:, p * wide : (p + 1) * wide]
-        out_ref[p, :, wide:] = k_ref[:, p * narrow : (p + 1) * narrow]
-
-
-def pair_columns(q, k, parts):
+def pair_kernel(at_ref, q_ref, k_ref, *out_refs):
+    for bits, out_ref in enumerate(out_refs):
+        wide, narrow = q_ref.shape[1] // len(out_refs), k_ref.shape[1] // len(out_refs)
+        part = at_ref[0] ^ bits
+        out_ref[:, :wide] = q_ref[:, pl.ds(pl.multiple_of(part * wide, wide), wide)]
+        out_ref[:, wide:] = k_ref[:, pl.ds(pl.multiple_of(part * narrow, narrow), narrow)]
+
+
+def pair_columns(at, q, k, parts):
+    block = struct((q.shape[0], (q.shape[1] + k.shape[1]) // parts), BF16)
     return pl.pallas_call(
         pair_kernel,
-        in_specs=[VMEM] * 2,
-        out_shape=struct((parts, q.shape[0], (q.shape[1] + k.shape[1]) // parts), BF16),
+        in_specs=[SMEM] + [VMEM] * 2,
+        out_shape=[block] * parts,
         cost_estimate=cost(1000, 2_600_000),
         compiler_params=grant(12),
         name="pair_columns",
-    )(q, k)
+    )(at, q, k)
 
 
 def gram_kernel(
-    len_ref, q_all, y_ref, g_ref, z_ref, g_acc, z_acc, *, docs, reach
+    at_ref, len_ref, p0, p1, p2, p3, y_ref, g_ref, z_ref, q_all, g_acc, z_acc, *, docs, reach
 ):
     seq = q_all.shape[0]
-    block = seq // 4
+    block = p0.shape[0]
     groups = g_ref.shape[0]
     scale = HD ** (-0.5)
     ends, total = [], jnp.int32(0)
     for j in range(docs):
         total = total + len_ref[j]
         ends.append(total)
+    for k, ref in enumerate((p0, p1, p2, p3)):
+        at = pl.multiple_of((at_ref[0] ^ k) * block, block)
+        q_all[pl.ds(at, block), :] = ref[...]
     for g in range(groups):
         g_acc[...] = jnp.zeros_like(g_acc)
         z_acc[...] = jnp.zeros_like(z_acc)
@@ -93,23 +97,27 @@
         z_ref[g] = z_acc[...]
 
 
-def gram(lengths, qk, targets):
+def gram(at, lengths, pieces, targets):
     seq, width = targets.shape
     groups = width // (GROUP * HD)
     return pl.pallas_call(
         functools.partial(gram_kernel, docs=lengths.shape[0], reach=seq // 4),
-        in_specs=[SMEM] + [VMEM] * 2,
+        in_specs=[SMEM] * 2 + [VMEM] * 5,
         out_shape=[struct((groups, seq, seq), BF16), struct((groups, HD, seq), F32)],
-        scratch_shapes=[pltpu.VMEM((seq, seq), F32), pltpu.VMEM((HD, seq), F32)],
+        scratch_shapes=[
+            pltpu.VMEM((seq, pieces[0].shape[1]), BF16),
+            pltpu.VMEM((seq, seq), F32),
+            pltpu.VMEM((HD, seq), F32),
+        ],
         cost_estimate=cost(4_000_000_000, 5_000_000),
         compiler_params=grant(20),
         name="gram",
-    )(lengths, qk, targets)
+    )(at, lengths, *pieces, targets)
 
 
 def first_kernel(
     at_ref, g_ref, z_ref, c0, c1, c2, c3, up_ref,
-    grad0_ref, grad1_ref, mixed_ref, up_grad_ref, low_ref, v_ref, *, rows, factor,
+    grad0_ref, grad1_ref, up_grad_ref, low_ref, v_ref, *, rows, factor,
 ):
     own = v_ref.shape[0]
     for k, ref in enumerate((c0, c1, c2, c3)):
@@ -121,11 +129,11 @@
     for g, out in enumerate((grad0_ref, grad1_ref)):
         cols = slice(g * HD, (g + 1) * HD)
         grad = (factor * (dot(v_ref[cols, :], g_ref[g], 1, 0) - z_ref[g])).astype(BF16)
-        out[...] = grad
+        out[:HD, :] = grad
         part = dot(up_ref[:, cols], grad, 1, 0)
         mixed = part if mixed is None else mixed + part
         up_grad_ref[:, cols] = dot(low, grad, 1, 1)
-    mixed_ref[...] = mixed
+    grad0_ref[HD:, :] = mixed.astype(BF16)
 
 
 def first_pass(at, g, z, carried, up, rows, factor):
@@ -135,9 +143,8 @@
         functools.partial(first_kernel, rows=rows, factor=factor),
         in_specs=[SMEM] + [VMEM] * 7,
         out_shape=[
+            struct((HD + rank, seq), BF16),
             struct((HD, seq), BF16),
-            struct((HD, seq), BF16),
-            struct((rank, seq), F32),
             struct((rank, own), F32),
             struct((rank, seq), BF16),
         ],
@@ -152,7 +159,8 @@
     rows, width = h0.shape
     for k, ref in enumerate((h0, h1, h2, h3)):
         h_ref[pl.ds(pl.multiple_of((at_ref[0] ^ k) * rows, rows), rows), :] = ref[...]
-    mixed = ((m0[...] + m1[...]) + (m2[...] + m3[...])).astype(BF16)
+    mixed = [ref[HD:, :].astype(F32) for ref in (m0, m1, m2, m3)]
+    mixed = ((mixed[0] + mixed[1]) + (mixed[2] + mixed[3])).astype(BF16)
     out_ref[:, :width] = dot(mixed, h_ref[...], 1, 0)
     out_ref[:, width:] = up_grad_ref[...]
 
@@ -224,7 +232,7 @@
 
 def main_kernel(at_ref, h_ref, p0, p1, p2, p3, send_ref, keep_ref):
     where = at_ref[0] ^ at_ref[1]
-    pieces = jnp.concatenate([ref[...] for ref in (p0, p1, p2, p3)], axis=0)
+    pieces = jnp.concatenate([ref[:HD, :] for ref in (p0, p1, p2, p3)], axis=0)
     blocks = dot(pieces, h_ref[...], 1, 0)
     for k in range(4):
         slot = where ^ k
@@ -353,7 +361,7 @@
 
 
 def exchange(pieces):
-    far = {bits: swap(pieces[bits], "ctx", bits) for bits in (3, 2, 1)}
+    far = {bits: swap(pieces[bits], "ctx", bits) for bits in (1, 2, 3)}
     return [pieces[0]] + [far[bits] for bits in (1, 2, 3)]
 
 
@@ -389,9 +397,8 @@
         size = array.shape[axis] // parts
         return lax.dynamic_slice_in_dim(array, (ctx ^ bits) * size, size, axis=axis)
 
-    qk = lax.all_to_all(
-        pair_columns(queries[0, 0], keys[0, 0], n_ctx), "ctx", split_axis=0, concat_axis=0, tiled=True
-    ).reshape(seq, -1)
+    qk = exchange(pair_columns(at, queries[0, 0], keys[0, 0], n_ctx))
+    h = after((h,), qk[1])[0]
     low = dot(attacker_down_factor, h, 0, 1).astype(BF16)
     values = (dot(value_matrix, h, 0, 1) + dot(attacker_up_factor, low, 0, 0)).astype(BF16)
     carried = [
@@ -401,36 +408,33 @@
     carried = exchange(carried)
     h_cols = exchange([block_of(h, n_ctx, 1, bits) for bits in range(n_ctx)])
 
-    g, z = gram(lengths[0, 0], qk, targets[0, 0])
-    *grads, mixed, up_grad, low = first_pass(at, g, z, carried, up, rows, factor)
-    mixed = everyone(mixed, "ctx")
-    first, later = after(grads, *mixed)
+    g, z = gram(at, lengths[0, 0], qk, targets[0, 0])
+    carried = after(carried, h_cols[1])
+    first, later, up_grad, low = first_pass(at, g, z, carried, up, rows, factor)
     first = everyone(first, "ctx")
-
-    low_rank, h_cols = down_pass(at, mixed, h_cols, up_grad)
+    later = everyone(later, "ctx")
+
+    low_rank, h_cols = down_pass(at, first, h_cols, up_grad)
     low_rank = everyone(low_rank, "dp")
+    halves = [main_pass(at, h_cols, first)]
+    low_rank = after(low_rank, halves[0][0], *later)
     moved, up_grad = moved_pass(low_rank, h_cols)
-    first = after(first, moved)
-    later = everyone(later, "ctx")
+    halves.append(main_pass(at, h_cols, after(later, moved)))
     moved = everyone(moved, "ctx")
-    send, kept = main_pass(at, h_cols, first)
-    leaving, staying = meet(kept, swap(send, "dp", 1))
-    moved = after(moved, leaving, *later)
+    halves = [meet(kept, swap(send, "dp", 1)) for send, kept in halves]
+    moved = after(moved, halves[0][0])
     stepped = step_pass(moved, low, g, up, up_grad, rank * (width + value_span), factor)
-    later = after(later, stepped)
     stepped = everyone(stepped, "ctx")
-    passed = swap(leaving, "dp", 2)
-    send, kept = main_pass(at, h_cols, later)
-    stepped = after(stepped, passed, send)
+    passed = [swap(leaving, "dp", 2) for leaving, staying in halves]
+    stepped = after(stepped, passed[0], halves[1][0])
     keep, *sent, rows_of_up = late_pass(at, h_cols, stepped, rank, own)
     late = [keep] + [swap(part, "dp", bits) for bits, part in zip((1, 2, 3), sent)]
-    main = (staying + passed.astype(F32)).astype(BF16)
-    mains = [(main, swap(main, "adv", 1))]
-    late = pack_pass(late, rows_of_up)
+    mains = []
+    for (leaving, staying), block in zip(halves, passed):
+        main = (staying + block.astype(F32)).astype(BF16)
+        mains.append((main, swap(main, "adv", 1)))
+    late = pack_pass(after(late, mains[1][0]), rows_of_up)
     late = [late, swap(late, "adv", 1)]
-    leaving, staying = meet(kept, swap(send, "dp", 1))
-    main = (staying + swap(leaving, "dp", 2).astype(F32)).astype(BF16)
-    mains.append((main, swap(main, "adv", 1)))
     return last_pass(mains, late, own, rank, -1.0 / lax.axis_size("adv"))
 
 

time: 142 us -> 132 us (0.930)
  waiting for transfers between devices: 58.7 us -> 47.6 us
  starting transfers between devices: 53.4 us -> 57.1 us
    ppermute x34, starting transfers between devices: 47.1 us -> 57.1 us  [swap(): return lax.ppermute(array, axis, [(i, i ^ bits) for i in range(count)])]
    all_to_all x1 -> x0, waiting for transfers between devices: 8.79 us -> none  [body(): lax.all_to_all(pair_columns(queries[0, 0], keys[0, 0], n_ctx), 'ctx', spl...]
    all_to_all x1 -> x0, starting transfers between devices: 6.35 us -> none  [body(): lax.all_to_all(pair_columns(queries[0, 0], keys[0, 0], n_ctx), 'ctx', spl...]
    ppermute x34, waiting for transfers between devices: 49.9 us -> 47.6 us  [swap(): return lax.ppermute(array, axis, [(i, i ^ bits) for i in range(count)])]
    dynamic_slice x2, local copies, waits for them, and re-layouts: 2.11 us -> 0.1 us  [block_of(): return lax.dynamic_slice_in_dim(array, (ctx ^ bits) * size, size, axis=axis)]
  transfers between devices with their start and end apart: 35 -> 34, of which waited for: 16 -> 12; matrix products, arithmetic and copies ran while one was open for 8% -> 8% of each run, Pallas kernels for 6% -> 9%
where the time goes in v4:
time: 132 us
  starting transfers between devices  57.1 us (43%)
  waiting for transfers between devices  47.6 us (36%)
  Pallas kernels  14.3 us (11%)
  matrix products  8.96 us (7%)
  local copies, waits for them, and re-layouts  3.08 us (2%)
    ppermute x34, starting transfers between devices, swap(): return lax.ppermute(array, axis, [(i, i ^ bits) for i in range(count)])  57.1 us
    ppermute x34, waiting for transfers between devices, swap(): return lax.ppermute(array, axis, [(i, i ^ bits) for i in range(count)])  47.6 us
    dot_general x3, matrix products, dot(): lax.dot_general(a, b, (((da,), (db,)), ((), ())), preferred_element_type=...  8.96 us
    pallas_call x1, Pallas kernels, gram(): pl.pallas_call(functools.partial(gram_kernel, docs=lengths.shape[0], reac...  5.2 us
    pallas_call x2, Pallas kernels, main_pass(): pl.pallas_call(main_kernel, in_specs=[SMEM] + [VMEM] * 5, out_shape=[stru...  3.06 us
  transfers between devices with their start and end apart: 34, of which 12 were waited for; matrix products, arithmetic and copies ran while one was open for 8% of the time, Pallas kernels for 9%

profile of v4, /device:TPU:0, one launch (start us, length us, event | category | flops | bytes accessed | tf_op | source)
XLA Modules:
  0.0 131.9 jit_solution(10802845347567360309)
XLA Ops:
  2.9 3.1 %collective-permute-start = (bf16[128,1280]{1,0:T(8,128)(2,1)S(1)}, bf16[128,1280]{1,0:T(8,128)(2,1)S(1)}, u32[]{:S(2)}, u32[]{:S(2)}) collective-permute-start(bf16[128,1280]{1,0:T(8,128)(2,1)S(1)} %get-tuple-element.59), channel_id=1, source_target_pairs={{0,8},{8,0},{16,24},{24,16},{1,9},{9,1},{17,25},{25,17},{2,10},{10... | collective-permute-start | bytes 983048 | tf_op jit(solution)/shard_map/ppermute | solution.py:360
  6.0 2.6 %collective-permute-start.1 = (bf16[128,1280]{1,0:T(8,128)(2,1)S(1)}, bf16[128,1280]{1,0:T(8,128)(2,1)S(1)}, u32[]{:S(2)}, u32[]{:S(2)}) collective-permute-start(bf16[128,1280]{1,0:T(8,128)(2,1)S(1)} %get-tuple-element.60), channel_id=1, source_target_pairs={{0,16},{8,24},{16,0},{24,8},{1,17},{9,25},{17,1},{25,9},{2,18},{10... | collective-permute-start | bytes 983048 | tf_op jit(solution)/shard_map/ppermute | solution.py:360
  9.4 10.6 %collective-permute-done.p1 = bf16[128,1280]{1,0:T(8,128)(2,1)S(1)} collective-permute-done((bf16[128,1280]{1,0:T(8,128)(2,1)S(1)}, bf16[128,1280]{1,0:T(8,128)(2,1)S(1)}, u32[]{:S(2)}, u32[]{:S(2)}) %collective-permute-start) | collective-permute-done | bytes 327712 | tf_op jit(solution)/shard_map/ppermute | solution.py:360
  22.7 6.3 %fusion = bf16[128,1024]{0,1:T(8,128)(2,1)S(1)} fusion(f32[128,1024]{0,1:T(8,128)S(1)} %fusion.11, bf16[128,4096]{1,0:T(8,128)(2,1)} %bitcast.43, bf16[4096,1024]{1,0:T(8,128)(2,1)} %param.13), kind=kOutput, calls=%fused_computation.1 | convolution fusion | flops 1074003968 | bytes 10223616 | tf_op jit(solution)/shard_map/dot_general | solution.py:22
  29.1 3.8 %collective-permute-start.4 = (bf16[272,128]{1,0:T(8,128)(2,1)S(1)}, bf16[272,128]{1,0:T(8,128)(2,1)S(1)}, u32[]{:S(2)}, u32[]{:S(2)}) collective-permute-start(bf16[272,128]{1,0:T(8,128)(2,1)S(1)} %get-tuple-element.67), channel_id=1, source_target_pairs={{0,16},{8,24},{16,0},{24,8},{1,17},{9,25},{17,1},{25,9},{2,18},{10... | collective-permute-start | bytes 208904 | tf_op jit(solution)/shard_map/ppermute | solution.py:360
  33.6 3.3 %collective-permute-start.11 = (bf16[128,1024]{1,0:T(8,128)(2,1)S(1)}, bf16[128,1024]{1,0:T(8,128)(2,1)S(1)}, u32[]{:S(2)}, u32[]{:S(2)}) collective-permute-start(bf16[128,1024]{1,0:T(8,128)(2,1)S(1)} %get-tuple-element.111), channel_id=1, source_target_pairs={{0,24},{8,16},{16,8},{24,0},{1,25},{9,17},{17,9},{25,1},{2,26},{10... | collective-permute-start | bytes 786440 | tf_op jit(solution)/shard_map/ppermute | solution.py:360
  36.9 11.9 %collective-permute-start.10 = (bf16[128,1024]{1,0:T(8,128)(2,1)S(1)}, bf16[128,1024]{1,0:T(8,128)(2,1)S(1)}, u32[]{:S(2)}, u32[]{:S(2)}) collective-permute-start(bf16[128,1024]{1,0:T(8,128)(2,1)S(1)} %get-tuple-element.112), channel_id=1, source_target_pairs={{0,16},{8,24},{16,0},{24,8},{1,17},{9,25},{17,1},{25,9},{2,18},{10... | collective-permute-start | bytes 786440 | tf_op jit(solution)/shard_map/ppermute | solution.py:360
  48.8 5.2 %gram.1 = (bf16[2,512,512]{2,1,0:T(8,128)(2,1)S(1)}, f32[2,128,512]{2,1,0:T(8,128)S(1)}) custom-call(s32[2]{0:T(128)S(1)} %pad_add_fusion.at_ref, s32[8]{0:T(128)S(1)} %bitcast.41, bf16[128,1280]{1,0:T(8,128)(2,1)S(1)} %get-tuple-element.58.p0, bf16[128,1280]{1,0:T(8,128)(2,1)S(1)} %collective-permute-done.p1, ...), custom_call_target="tpu_custom_call" | custom-call | flops 4000000000 | bytes 5000000 | tf_op jit(solution)/shard_map/gram/pallas_call | solution.py:103
  54.0 4.3 %collective-permute-done.6.h1 = bf16[128,1024]{1,0:T(8,128)(2,1)S(1)} collective-permute-done((bf16[128,1024]{1,0:T(8,128)(2,1)S(1)}, bf16[128,1024]{1,0:T(8,128)(2,1)S(1)}, u32[]{:S(2)}, u32[]{:S(2)}) %collective-permute-start.6) | collective-permute-done | bytes 262176 | tf_op jit(solution)/shard_map/ppermute | solution.py:360
  60.1 3.3 %collective-permute-start.8 = (bf16[144,512]{1,0:T(8,128)(2,1)S(1)}, bf16[144,512]{1,0:T(8,128)(2,1)S(1)}, u32[]{:S(2)}, u32[]{:S(2)}) collective-permute-start(bf16[144,512]{1,0:T(8,128)(2,1)S(1)} %get-tuple-element.74.m0.p0), channel_id=1, source_target_pairs={{0,16},{8,24},{16,0},{24,8},{1,17},{9,25},{17,1},{25,9},{2,18},{10... | collective-permute-start | bytes 442376 | tf_op jit(solution)/shard_map/ppermute | solution.py:360
  64.9 11.2 %collective-permute-done.10.h2 = bf16[128,1024]{1,0:T(8,128)(2,1)S(1)} collective-permute-done((bf16[128,1024]{1,0:T(8,128)(2,1)S(1)}, bf16[128,1024]{1,0:T(8,128)(2,1)S(1)}, u32[]{:S(2)}, u32[]{:S(2)}) %collective-permute-start.10) | collective-permute-done | bytes 262176 | tf_op jit(solution)/shard_map/ppermute | solution.py:360
  76.1 5.5 %collective-permute-start.15 = (bf16[128,512]{1,0:T(8,128)(2,1)S(1)}, bf16[128,512]{1,0:T(8,128)(2,1)S(1)}, u32[]{:S(2)}, u32[]{:S(2)}) collective-permute-start(bf16[128,512]{1,0:T(8,128)(2,1)S(1)} %get-tuple-element.86.p0), channel_id=1, source_target_pairs={{0,8},{8,0},{16,24},{24,16},{1,9},{9,1},{17,25},{25,17},{2,10},{10... | collective-permute-start | bytes 393224 | tf_op jit(solution)/shard_map/ppermute | solution.py:360
  81.6 3.7 %collective-permute-done.8.m2.p2 = bf16[144,512]{1,0:T(8,128)(2,1)S(1)} collective-permute-done((bf16[144,512]{1,0:T(8,128)(2,1)S(1)}, bf16[144,512]{1,0:T(8,128)(2,1)S(1)}, u32[]{:S(2)}, u32[]{:S(2)}) %collective-permute-start.8) | collective-permute-done | bytes 147488 | tf_op jit(solution)/shard_map/ppermute | solution.py:360
  89.8 2.3 %collective-permute-done.20.l3 = f32[16,1280]{1,0:T(8,128)S(1)} collective-permute-done((f32[16,1280]{1,0:T(8,128)S(1)}, f32[16,1280]{1,0:T(8,128)S(1)}, u32[]{:S(2)}, u32[]{:S(2)}) %collective-permute-start.20) | collective-permute-done | bytes 81952 | tf_op jit(solution)/shard_map/ppermute | solution.py:360
  92.1 2.1 %collective-permute-done.19.l2 = f32[16,1280]{1,0:T(8,128)S(1)} collective-permute-done((f32[16,1280]{1,0:T(8,128)S(1)}, f32[16,1280]{1,0:T(8,128)S(1)}, u32[]{:S(2)}, u32[]{:S(2)}) %collective-permute-start.19) | collective-permute-done | bytes 81952 | tf_op jit(solution)/shard_map/ppermute | solution.py:360
  94.6 1.6 %main_pass.3 = (bf16[2,128,1024]{2,1,0:T(8,128)(2,1)S(1)}, f32[2,128,1024]{2,1,0:T(8,128)S(1)}) custom-call(s32[2]{0:T(128)S(1)} %pad_add_fusion.at_ref, bf16[512,1024]{1,0:T(8,128)(2,1)S(1)} %get-tuple-element.76.h_ref, bf16[128,512]{1,0:T(8,128)(2,1)S(1)} %get-tuple-element.86.p0, bf16[128,512]{1,0:T(8,128)(2,1)S(1)} %collective-permute-done.15.p1, ...), custom_call_target="tpu_custom_call" | custom-call | flops 1500000000 | bytes 4000000 | tf_op jit(solution)/shard_map/main_pass/pallas_call | solution.py:253
  96.3 2.5 %collective-permute-start.26 = (f32[24,512]{1,0:T(8,128)S(1)}, f32[24,512]{1,0:T(8,128)S(1)}, u32[]{:S(2)}, u32[]{:S(2)}) collective-permute-start(f32[24,512]{1,0:T(8,128)S(1)} %get-tuple-element.92.s0), channel_id=1, source_target_pairs={{0,24},{8,16},{16,8},{24,0},{1,25},{9,17},{17,9},{25,1},{2,26},{10... | collective-permute-start | bytes 147464 | tf_op jit(solution)/shard_map/ppermute | solution.py:360
  98.8 1.9 %collective-permute-start.24 = (f32[24,512]{1,0:T(8,128)S(1)}, f32[24,512]{1,0:T(8,128)S(1)}, u32[]{:S(2)}, u32[]{:S(2)}) collective-permute-start(f32[24,512]{1,0:T(8,128)S(1)} %get-tuple-element.92.s0), channel_id=1, source_target_pairs={{0,8},{8,0},{16,24},{24,16},{1,9},{9,1},{17,25},{25,17},{2,10},{10... | collective-permute-start | bytes 147464 | tf_op jit(solution)/shard_map/ppermute | solution.py:360
  104.6 2.5 %collective-permute-start.29 = (bf16[80,512]{1,0:T(8,128)(2,1)S(1)}, bf16[80,512]{1,0:T(8,128)(2,1)S(1)}, u32[]{:S(2)}, u32[]{:S(2)}) collective-permute-start(bf16[80,512]{1,0:T(8,128)(2,1)S(1)} %step_pass.1.x0), channel_id=1, source_target_pairs={{0,24},{8,16},{16,8},{24,0},{1,25},{9,17},{17,9},{25,1},{2,26},{10... | collective-permute-start | bytes 245768 | tf_op jit(solution)/shard_map/ppermute | solution.py:360
  107.1 1.9 %collective-permute-start.27 = (bf16[80,512]{1,0:T(8,128)(2,1)S(1)}, bf16[80,512]{1,0:T(8,128)(2,1)S(1)}, u32[]{:S(2)}, u32[]{:S(2)}) collective-permute-start(bf16[80,512]{1,0:T(8,128)(2,1)S(1)} %step_pass.1.x0), channel_id=1, source_target_pairs={{0,8},{8,0},{16,24},{24,16},{1,9},{9,1},{17,25},{25,17},{2,10},{10... | collective-permute-start | bytes 245768 | tf_op jit(solution)/shard_map/ppermute | solution.py:360
  112.5 2.0 %collective-permute-done.28.x2 = bf16[80,512]{1,0:T(8,128)(2,1)S(1)} collective-permute-done((bf16[80,512]{1,0:T(8,128)(2,1)S(1)}, bf16[80,512]{1,0:T(8,128)(2,1)S(1)}, u32[]{:S(2)}, u32[]{:S(2)}) %collective-permute-start.28) | collective-permute-done | bytes 81952 | tf_op jit(solution)/shard_map/ppermute | solution.py:360
  119.2 2.9 %collective-permute-done.31.r2 = bf16[64,1024]{1,0:T(8,128)(2,1)S(1)} collective-permute-done((bf16[64,1024]{1,0:T(8,128)(2,1)S(1)}, bf16[64,1024]{1,0:T(8,128)(2,1)S(1)}, u32[]{:S(2)}, u32[]{:S(2)}) %collective-permute-start.31) | collective-permute-done | bytes 131104 | tf_op jit(solution)/shard_map/ppermute | solution.py:360
  122.1 1.7 %collective-permute-done.32.r3 = bf16[64,1024]{1,0:T(8,128)(2,1)S(1)} collective-permute-done((bf16[64,1024]{1,0:T(8,128)(2,1)S(1)}, bf16[64,1024]{1,0:T(8,128)(2,1)S(1)}, u32[]{:S(2)}, u32[]{:S(2)}) %collective-permute-start.32) | collective-permute-done | bytes 131104 | tf_op jit(solution)/shard_map/ppermute | solution.py:360
  125.4 4.9 %collective-permute-done.33.l1 = bf16[72,1024]{1,0:T(8,128)(2,1)S(1)} collective-permute-done((bf16[72,1024]{1,0:T(8,128)(2,1)S(1)}, bf16[72,1024]{1,0:T(8,128)(2,1)S(1)}, u32[]{:S(2)}, u32[]{:S(2)}) %collective-permute-start.33) | collective-permute-done | bytes 147488 | tf_op jit(solution)/shard_map/ppermute | solution.py:360
  (81 shorter events, 30.6 us)
Async XLA Ops:
  2.9 17.1 %collective-permute-start = (bf16[128,1280]{1,0:T(8,128)(2,1)S(1)}, bf16[128,1280]{1,0:T(8,128)(2,1)S(1)}, u32[]{:S(2)}, u32[]{:S(2)}) collective-permute-start(bf16[128,1280]{1,0:T(8,128)(2,1)S(1)} %get-tuple-element.59), channel_id=1, source_target_pairs={{0,8},{8,0},{16,24},{24,16},{1,9},{9,1},{17,25},{25,17},{2,10},{10... | collective-permute-start | bytes 983048 | tf_op jit(solution)/shard_map/ppermute | solution.py:360
  6.0 27.6 %collective-permute-start.1 = (bf16[128,1280]{1,0:T(8,128)(2,1)S(1)}, bf16[128,1280]{1,0:T(8,128)(2,1)S(1)}, u32[]{:S(2)}, u32[]{:S(2)}) collective-permute-start(bf16[128,1280]{1,0:T(8,128)(2,1)S(1)} %get-tuple-element.60), channel_id=1, source_target_pairs={{0,16},{8,24},{16,0},{24,8},{1,17},{9,25},{17,1},{25,9},{2,18},{10... | collective-permute-start | bytes 983048 | tf_op jit(solution)/shard_map/ppermute | solution.py:360
  8.6 28.3 %collective-permute-start.2 = (bf16[128,1280]{1,0:T(8,128)(2,1)S(1)}, bf16[128,1280]{1,0:T(8,128)(2,1)S(1)}, u32[]{:S(2)}, u32[]{:S(2)}) collective-permute-start(bf16[128,1280]{1,0:T(8,128)(2,1)S(1)} %get-tuple-element.61), channel_id=1, source_target_pairs={{0,24},{8,16},{16,8},{24,0},{1,25},{9,17},{17,9},{25,1},{2,26},{10... | collective-permute-start | bytes 983048 | tf_op jit(solution)/shard_map/ppermute | solution.py:360
  29.1 19.7 %collective-permute-start.3 = (bf16[272,128]{1,0:T(8,128)(2,1)S(1)}, bf16[272,128]{1,0:T(8,128)(2,1)S(1)}, u32[]{:S(2)}, u32[]{:S(2)}) collective-permute-start(bf16[272,128]{1,0:T(8,128)(2,1)S(1)} %get-tuple-element.66), channel_id=1, source_target_pairs={{0,8},{8,0},{16,24},{24,16},{1,9},{9,1},{17,25},{25,17},{2,10},{10... | collective-permute-start | bytes 208904 | tf_op jit(solution)/shard_map/ppermute | solution.py:360
  29.1 24.8 %collective-permute-start.4 = (bf16[272,128]{1,0:T(8,128)(2,1)S(1)}, bf16[272,128]{1,0:T(8,128)(2,1)S(1)}, u32[]{:S(2)}, u32[]{:S(2)}) collective-permute-start(bf16[272,128]{1,0:T(8,128)(2,1)S(1)} %get-tuple-element.67), channel_id=1, source_target_pairs={{0,16},{8,24},{16,0},{24,8},{1,17},{9,25},{17,1},{25,9},{2,18},{10... | collective-permute-start | bytes 208904 | tf_op jit(solution)/shard_map/ppermute | solution.py:360
  32.9 21.1 %collective-permute-start.5 = (bf16[272,128]{1,0:T(8,128)(2,1)S(1)}, bf16[272,128]{1,0:T(8,128)(2,1)S(1)}, u32[]{:S(2)}, u32[]{:S(2)}) collective-permute-start(bf16[272,128]{1,0:T(8,128)(2,1)S(1)} %get-tuple-element.68), channel_id=1, source_target_pairs={{0,24},{8,16},{16,8},{24,0},{1,25},{9,17},{17,9},{25,1},{2,26},{10... | collective-permute-start | bytes 208904 | tf_op jit(solution)/shard_map/ppermute | solution.py:360
  33.6 30.3 %collective-permute-start.11 = (bf16[128,1024]{1,0:T(8,128)(2,1)S(1)}, bf16[128,1024]{1,0:T(8,128)(2,1)S(1)}, u32[]{:S(2)}, u32[]{:S(2)}) collective-permute-start(bf16[128,1024]{1,0:T(8,128)(2,1)S(1)} %get-tuple-element.111), channel_id=1, source_target_pairs={{0,24},{8,16},{16,8},{24,0},{1,25},{9,17},{17,9},{25,1},{2,26},{10... | collective-permute-start | bytes 786440 | tf_op jit(solution)/shard_map/ppermute | solution.py:360
  36.9 39.3 %collective-permute-start.10 = (bf16[128,1024]{1,0:T(8,128)(2,1)S(1)}, bf16[128,1024]{1,0:T(8,128)(2,1)S(1)}, u32[]{:S(2)}, u32[]{:S(2)}) collective-permute-start(bf16[128,1024]{1,0:T(8,128)(2,1)S(1)} %get-tuple-element.112), channel_id=1, source_target_pairs={{0,16},{8,24},{16,0},{24,8},{1,17},{9,25},{17,1},{25,9},{2,18},{10... | collective-permute-start | bytes 786440 | tf_op jit(solution)/shard_map/ppermute | solution.py:360
  48.7 9.5 %collective-permute-start.6 = (bf16[128,1024]{1,0:T(8,128)(2,1)S(1)}, bf16[128,1024]{1,0:T(8,128)(2,1)S(1)}, u32[]{:S(2)}, u32[]{:S(2)}) collective-permute-start(bf16[128,1024]{1,0:T(8,128)(2,1)S(1)} %get-tuple-element.114), channel_id=1, source_target_pairs={{0,8},{8,0},{16,24},{24,16},{1,9},{9,1},{17,25},{25,17},{2,10},{10... | collective-permute-start | bytes 786440 | tf_op jit(solution)/shard_map/ppermute | solution.py:360
  59.5 16.7 %collective-permute-start.9 = (bf16[144,512]{1,0:T(8,128)(2,1)S(1)}, bf16[144,512]{1,0:T(8,128)(2,1)S(1)}, u32[]{:S(2)}, u32[]{:S(2)}) collective-permute-start(bf16[144,512]{1,0:T(8,128)(2,1)S(1)} %get-tuple-element.74.m0.p0), channel_id=1, source_target_pairs={{0,24},{8,16},{16,8},{24,0},{1,25},{9,17},{17,9},{25,1},{2,26},{10... | collective-permute-start | bytes 442376 | tf_op jit(solution)/shard_map/ppermute | solution.py:360
  60.1 25.2 %collective-permute-start.8 = (bf16[144,512]{1,0:T(8,128)(2,1)S(1)}, bf16[144,512]{1,0:T(8,128)(2,1)S(1)}, u32[]{:S(2)}, u32[]{:S(2)}) collective-permute-start(bf16[144,512]{1,0:T(8,128)(2,1)S(1)} %get-tuple-element.74.m0.p0), channel_id=1, source_target_pairs={{0,16},{8,24},{16,0},{24,8},{1,17},{9,25},{17,1},{25,9},{2,18},{10... | collective-permute-start | bytes 442376 | tf_op jit(solution)/shard_map/ppermute | solution.py:360
  63.4 21.8 %collective-permute-start.7 = (bf16[144,512]{1,0:T(8,128)(2,1)S(1)}, bf16[144,512]{1,0:T(8,128)(2,1)S(1)}, u32[]{:S(2)}, u32[]{:S(2)}) collective-permute-start(bf16[144,512]{1,0:T(8,128)(2,1)S(1)} %get-tuple-element.74.m0.p0), channel_id=1, source_target_pairs={{0,8},{8,0},{16,24},{24,16},{1,9},{9,1},{17,25},{25,17},{2,10},{10... | collective-permute-start | bytes 442376 | tf_op jit(solution)/shard_map/ppermute | solution.py:360
  63.9 25.4 %collective-permute-start.17 = (bf16[128,512]{1,0:T(8,128)(2,1)S(1)}, bf16[128,512]{1,0:T(8,128)(2,1)S(1)}, u32[]{:S(2)}, u32[]{:S(2)}) collective-permute-start(bf16[128,512]{1,0:T(8,128)(2,1)S(1)} %get-tuple-element.86.p0), channel_id=1, source_target_pairs={{0,24},{8,16},{16,8},{24,0},{1,25},{9,17},{17,9},{25,1},{2,26},{10... | collective-permute-start | bytes 393224 | tf_op jit(solution)/shard_map/ppermute | solution.py:360
  76.1 13.6 %collective-permute-start.16 = (bf16[128,512]{1,0:T(8,128)(2,1)S(1)}, bf16[128,512]{1,0:T(8,128)(2,1)S(1)}, u32[]{:S(2)}, u32[]{:S(2)}) collective-permute-start(bf16[128,512]{1,0:T(8,128)(2,1)S(1)} %get-tuple-element.86.p0), channel_id=1, source_target_pairs={{0,16},{8,24},{16,0},{24,8},{1,17},{9,25},{17,1},{25,9},{2,18},{10... | collective-permute-start | bytes 393224 | tf_op jit(solution)/shard_map/ppermute | solution.py:360
  76.1 13.6 %collective-permute-start.15 = (bf16[128,512]{1,0:T(8,128)(2,1)S(1)}, bf16[128,512]{1,0:T(8,128)(2,1)S(1)}, u32[]{:S(2)}, u32[]{:S(2)}) collective-permute-start(bf16[128,512]{1,0:T(8,128)(2,1)S(1)} %get-tuple-element.86.p0), channel_id=1, source_target_pairs={{0,8},{8,0},{16,24},{24,16},{1,9},{9,1},{17,25},{25,17},{2,10},{10... | collective-permute-start | bytes 393224 | tf_op jit(solution)/shard_map/ppermute | solution.py:360
  87.6 13.2 %collective-permute-start.12 = (bf16[2,128,1024]{2,1,0:T(8,128)(2,1)S(1)}, bf16[2,128,1024]{2,1,0:T(8,128)(2,1)S(1)}, u32[]{:S(2)}, u32[]{:S(2)}) collective-permute-start(bf16[2,128,1024]{2,1,0:T(8,128)(2,1)S(1)} %get-tuple-element.78), channel_id=1, source_target_pairs={{0,2},{2,0},{4,6},{6,4},{1,3},{3,1},{5,7},{7,5},{8,10},{10,8},{12,... | collective-permute-start | bytes 1572872 | tf_op jit(solution)/shard_map/ppermute | solution.py:360
  96.2 12.8 %collective-permute-start.21 = (bf16[2,128,1024]{2,1,0:T(8,128)(2,1)S(1)}, bf16[2,128,1024]{2,1,0:T(8,128)(2,1)S(1)}, u32[]{:S(2)}, u32[]{:S(2)}) collective-permute-start(bf16[2,128,1024]{2,1,0:T(8,128)(2,1)S(1)} %get-tuple-element.91), channel_id=1, source_target_pairs={{0,2},{2,0},{4,6},{6,4},{1,3},{3,1},{5,7},{7,5},{8,10},{10,8},{12,... | collective-permute-start | bytes 1572872 | tf_op jit(solution)/shard_map/ppermute | solution.py:360
  100.9 9.8 %collective-permute-start.13 = (bf16[128,1024]{1,0:T(8,128)(2,1)S(1)}, bf16[128,1024]{1,0:T(8,128)(2,1)S(1)}, u32[]{:S(2)}, u32[]{:S(2)}) collective-permute-start(bf16[128,1024]{1,0:T(8,128)(2,1)S(1)} %fusion.9), channel_id=1, source_target_pairs={{0,4},{2,6},{4,0},{6,2},{1,5},{3,7},{5,1},{7,3},{8,12},{10,14},{12... | collective-permute-start | bytes 786440 | tf_op jit(solution)/shard_map/ppermute | solution.py:360
  104.6 7.8 %collective-permute-start.29 = (bf16[80,512]{1,0:T(8,128)(2,1)S(1)}, bf16[80,512]{1,0:T(8,128)(2,1)S(1)}, u32[]{:S(2)}, u32[]{:S(2)}) collective-permute-start(bf16[80,512]{1,0:T(8,128)(2,1)S(1)} %step_pass.1.x0), channel_id=1, source_target_pairs={{0,24},{8,16},{16,8},{24,0},{1,25},{9,17},{17,9},{25,1},{2,26},{10... | collective-permute-start | bytes 245768 | tf_op jit(solution)/shard_map/ppermute | solution.py:360
  107.1 7.3 %collective-permute-start.28 = (bf16[80,512]{1,0:T(8,128)(2,1)S(1)}, bf16[80,512]{1,0:T(8,128)(2,1)S(1)}, u32[]{:S(2)}, u32[]{:S(2)}) collective-permute-start(bf16[80,512]{1,0:T(8,128)(2,1)S(1)} %step_pass.1.x0), channel_id=1, source_target_pairs={{0,16},{8,24},{16,0},{24,8},{1,17},{9,25},{17,1},{25,9},{2,18},{10... | collective-permute-start | bytes 245768 | tf_op jit(solution)/shard_map/ppermute | solution.py:360
  107.1 7.3 %collective-permute-start.27 = (bf16[80,512]{1,0:T(8,128)(2,1)S(1)}, bf16[80,512]{1,0:T(8,128)(2,1)S(1)}, u32[]{:S(2)}, u32[]{:S(2)}) collective-permute-start(bf16[80,512]{1,0:T(8,128)(2,1)S(1)} %step_pass.1.x0), channel_id=1, source_target_pairs={{0,8},{8,0},{16,24},{24,16},{1,9},{9,1},{17,25},{25,17},{2,10},{10... | collective-permute-start | bytes 245768 | tf_op jit(solution)/shard_map/ppermute | solution.py:360
  109.2 8.3 %collective-permute-start.22 = (bf16[128,1024]{1,0:T(8,128)(2,1)S(1)}, bf16[128,1024]{1,0:T(8,128)(2,1)S(1)}, u32[]{:S(2)}, u32[]{:S(2)}) collective-permute-start(bf16[128,1024]{1,0:T(8,128)(2,1)S(1)} %fusion.10), channel_id=1, source_target_pairs={{0,4},{2,6},{4,0},{6,2},{1,5},{3,7},{5,1},{7,3},{8,12},{10,14},{12... | collective-permute-start | bytes 786440 | tf_op jit(solution)/shard_map/ppermute | solution.py:360
  110.9 14.5 %collective-permute-start.14 = (bf16[128,1024]{1,0:T(8,128)(2,1)S(1)}, bf16[128,1024]{1,0:T(8,128)(2,1)S(1)}, u32[]{:S(2)}, u32[]{:S(2)}) collective-permute-start(bf16[128,1024]{1,0:T(8,128)(2,1)S(1)} %fusion.8.a0), channel_id=1, source_target_pairs={{0,1},{1,0},{2,3},{3,2},{4,5},{5,4},{6,7},{7,6},{8,9},{9,8},{10,11... | collective-permute-start | bytes 786440 | tf_op jit(solution)/shard_map/ppermute | solution.py:360
  117.6 12.8 %collective-permute-start.23 = (bf16[128,1024]{1,0:T(8,128)(2,1)S(1)}, bf16[128,1024]{1,0:T(8,128)(2,1)S(1)}, u32[]{:S(2)}, u32[]{:S(2)}) collective-permute-start(bf16[128,1024]{1,0:T(8,128)(2,1)S(1)} %fusion.4.b0), channel_id=1, source_target_pairs={{0,1},{1,0},{2,3},{3,2},{4,5},{5,4},{6,7},{7,6},{8,9},{9,8},{10,11... | collective-permute-start | bytes 786440 | tf_op jit(solution)/shard_map/ppermute | solution.py:360
  (16 other events, 196.7 us)

commit v5 on v4

--- a/solution.py
+++ b/solution.py
@@ -416,7 +416,7 @@
 
     low_rank, h_cols = down_pass(at, first, h_cols, up_grad)
     low_rank = everyone(low_rank, "dp")
-    halves = [main_pass(at, h_cols, first)]
+    halves = [main_pass(at, h_cols, after(first, low_rank[1]))]
     low_rank = after(low_rank, halves[0][0], *later)
     moved, up_grad = moved_pass(low_rank, h_cols)
     halves.append(main_pass(at, h_cols, after(later, moved)))

time: 132 us -> 131 us (level)
  transfers between devices with their start and end apart: 34 -> 34, of which waited for: 12 -> 13; matrix products, arithmetic and copies ran while one was open for 8% -> 8% of each run, Pallas kernels for 9% -> 9%
where the time goes in v5:
time: 131 us; the launch traced here: 130 us
  starting transfers between devices  56 us (43%)
  waiting for transfers between devices  47.1 us (36%)
  Pallas kernels  14.3 us (11%)
  matrix products  8.96 us (7%)
  local copies, waits for them, and re-layouts  3.08 us (2%)
    ppermute x34, starting transfers between devices, swap(): return lax.ppermute(array, axis, [(i, i ^ bits) for i in range(count)])  56 us
    ppermute x34, waiting for transfers between devices, swap(): return lax.ppermute(array, axis, [(i, i ^ bits) for i in range(count)])  47.1 us
    dot_general x3, matrix products, dot(): lax.dot_general(a, b, (((da,), (db,)), ((), ())), preferred_element_type=...  8.96 us
    pallas_call x1, Pallas kernels, gram(): pl.pallas_call(functools.partial(gram_kernel, docs=lengths.shape[0], reac...  5.2 us
    pallas_call x2, Pallas kernels, main_pass(): pl.pallas_call(main_kernel, in_specs=[SMEM] + [VMEM] * 5, out_shape=[stru...  3.04 us
  transfers between devices with their start and end apart: 34, of which 13 were waited for; matrix products, arithmetic and copies ran while one was open for 8% of the time, Pallas kernels for 9%

profile of v5, /device:TPU:0, one launch (start us, length us, event | category | flops | bytes accessed | tf_op | source)
XLA Modules:
  0.0 130.2 jit_solution(1677537640814653183)
XLA Ops:
  2.9 3.1 %collective-permute-start = (bf16[128,1280]{1,0:T(8,128)(2,1)S(1)}, bf16[128,1280]{1,0:T(8,128)(2,1)S(1)}, u32[]{:S(2)}, u32[]{:S(2)}) collective-permute-start(bf16[128,1280]{1,0:T(8,128)(2,1)S(1)} %get-tuple-element.63), channel_id=1, source_target_pairs={{0,8},{8,0},{16,24},{24,16},{1,9},{9,1},{17,25},{25,17},{2,10},{10... | collective-permute-start | bytes 983048 | tf_op jit(solution)/shard_map/ppermute | solution.py:360
  6.0 2.6 %collective-permute-start.1 = (bf16[128,1280]{1,0:T(8,128)(2,1)S(1)}, bf16[128,1280]{1,0:T(8,128)(2,1)S(1)}, u32[]{:S(2)}, u32[]{:S(2)}) collective-permute-start(bf16[128,1280]{1,0:T(8,128)(2,1)S(1)} %get-tuple-element.64), channel_id=1, source_target_pairs={{0,16},{8,24},{16,0},{24,8},{1,17},{9,25},{17,1},{25,9},{2,18},{10... | collective-permute-start | bytes 983048 | tf_op jit(solution)/shard_map/ppermute | solution.py:360
  9.4 10.6 %collective-permute-done.p1 = bf16[128,1280]{1,0:T(8,128)(2,1)S(1)} collective-permute-done((bf16[128,1280]{1,0:T(8,128)(2,1)S(1)}, bf16[128,1280]{1,0:T(8,128)(2,1)S(1)}, u32[]{:S(2)}, u32[]{:S(2)}) %collective-permute-start) | collective-permute-done | bytes 327712 | tf_op jit(solution)/shard_map/ppermute | solution.py:360
  22.7 6.3 %fusion = bf16[128,1024]{0,1:T(8,128)(2,1)S(1)} fusion(f32[128,1024]{0,1:T(8,128)S(1)} %fusion.11, bf16[128,4096]{1,0:T(8,128)(2,1)} %bitcast.43, bf16[4096,1024]{1,0:T(8,128)(2,1)} %param.13), kind=kOutput, calls=%fused_computation.1 | convolution fusion | flops 1074003968 | bytes 10223616 | tf_op jit(solution)/shard_map/dot_general | solution.py:22
  29.1 3.8 %collective-permute-start.4 = (bf16[272,128]{1,0:T(8,128)(2,1)S(1)}, bf16[272,128]{1,0:T(8,128)(2,1)S(1)}, u32[]{:S(2)}, u32[]{:S(2)}) collective-permute-start(bf16[272,128]{1,0:T(8,128)(2,1)S(1)} %get-tuple-element.71), channel_id=1, source_target_pairs={{0,16},{8,24},{16,0},{24,8},{1,17},{9,25},{17,1},{25,9},{2,18},{10... | collective-permute-start | bytes 208904 | tf_op jit(solution)/shard_map/ppermute | solution.py:360
  33.6 3.3 %collective-permute-start.11 = (bf16[128,1024]{1,0:T(8,128)(2,1)S(1)}, bf16[128,1024]{1,0:T(8,128)(2,1)S(1)}, u32[]{:S(2)}, u32[]{:S(2)}) collective-permute-start(bf16[128,1024]{1,0:T(8,128)(2,1)S(1)} %get-tuple-element.119), channel_id=1, source_target_pairs={{0,24},{8,16},{16,8},{24,0},{1,25},{9,17},{17,9},{25,1},{2,26},{10... | collective-permute-start | bytes 786440 | tf_op jit(solution)/shard_map/ppermute | solution.py:360
  36.9 11.9 %collective-permute-start.10 = (bf16[128,1024]{1,0:T(8,128)(2,1)S(1)}, bf16[128,1024]{1,0:T(8,128)(2,1)S(1)}, u32[]{:S(2)}, u32[]{:S(2)}) collective-permute-start(bf16[128,1024]{1,0:T(8,128)(2,1)S(1)} %get-tuple-element.120), channel_id=1, source_target_pairs={{0,16},{8,24},{16,0},{24,8},{1,17},{9,25},{17,1},{25,9},{2,18},{10... | collective-permute-start | bytes 786440 | tf_op jit(solution)/shard_map/ppermute | solution.py:360
  48.8 5.2 %gram.1 = (bf16[2,512,512]{2,1,0:T(8,128)(2,1)S(1)}, f32[2,128,512]{2,1,0:T(8,128)S(1)}) custom-call(s32[2]{0:T(128)S(1)} %pad_add_fusion.at_ref, s32[8]{0:T(128)S(1)} %bitcast.41, bf16[128,1280]{1,0:T(8,128)(2,1)S(1)} %get-tuple-element.62.p0, bf16[128,1280]{1,0:T(8,128)(2,1)S(1)} %collective-permute-done.p1, ...), custom_call_target="tpu_custom_call" | custom-call | flops 4000000000 | bytes 5000000 | tf_op jit(solution)/shard_map/gram/pallas_call | solution.py:103
  54.0 4.3 %collective-permute-done.6.h1 = bf16[128,1024]{1,0:T(8,128)(2,1)S(1)} collective-permute-done((bf16[128,1024]{1,0:T(8,128)(2,1)S(1)}, bf16[128,1024]{1,0:T(8,128)(2,1)S(1)}, u32[]{:S(2)}, u32[]{:S(2)}) %collective-permute-start.6) | collective-permute-done | bytes 262176 | tf_op jit(solution)/shard_map/ppermute | solution.py:360
  60.1 3.3 %collective-permute-start.8 = (bf16[144,512]{1,0:T(8,128)(2,1)S(1)}, bf16[144,512]{1,0:T(8,128)(2,1)S(1)}, u32[]{:S(2)}, u32[]{:S(2)}) collective-permute-start(bf16[144,512]{1,0:T(8,128)(2,1)S(1)} %get-tuple-element.82.m0.p0), channel_id=1, source_target_pairs={{0,16},{8,24},{16,0},{24,8},{1,17},{9,25},{17,1},{25,9},{2,18},{10... | collective-permute-start | bytes 442376 | tf_op jit(solution)/shard_map/ppermute | solution.py:360
  63.9 9.5 %collective-permute-done.10.h2 = bf16[128,1024]{1,0:T(8,128)(2,1)S(1)} collective-permute-done((bf16[128,1024]{1,0:T(8,128)(2,1)S(1)}, bf16[128,1024]{1,0:T(8,128)(2,1)S(1)}, u32[]{:S(2)}, u32[]{:S(2)}) %collective-permute-start.10) | collective-permute-done | bytes 262176 | tf_op jit(solution)/shard_map/ppermute | solution.py:360
  73.4 5.0 %collective-permute-done.8.m2.p2 = bf16[144,512]{1,0:T(8,128)(2,1)S(1)} collective-permute-done((bf16[144,512]{1,0:T(8,128)(2,1)S(1)}, bf16[144,512]{1,0:T(8,128)(2,1)S(1)}, u32[]{:S(2)}, u32[]{:S(2)}) %collective-permute-start.8) | collective-permute-done | bytes 147488 | tf_op jit(solution)/shard_map/ppermute | solution.py:360
  79.2 2.5 %collective-permute-start.18 = (bf16[128,512]{1,0:T(8,128)(2,1)S(1)}, bf16[128,512]{1,0:T(8,128)(2,1)S(1)}, u32[]{:S(2)}, u32[]{:S(2)}) collective-permute-start(bf16[128,512]{1,0:T(8,128)(2,1)S(1)} %get-tuple-element.94.p0), channel_id=1, source_target_pairs={{0,24},{8,16},{16,8},{24,0},{1,25},{9,17},{17,9},{25,1},{2,26},{10... | collective-permute-start | bytes 393224 | tf_op jit(solution)/shard_map/ppermute | solution.py:360
  81.7 2.0 %collective-permute-start.16 = (bf16[128,512]{1,0:T(8,128)(2,1)S(1)}, bf16[128,512]{1,0:T(8,128)(2,1)S(1)}, u32[]{:S(2)}, u32[]{:S(2)}) collective-permute-start(bf16[128,512]{1,0:T(8,128)(2,1)S(1)} %get-tuple-element.94.p0), channel_id=1, source_target_pairs={{0,8},{8,0},{16,24},{24,16},{1,9},{9,1},{17,25},{25,17},{2,10},{10... | collective-permute-start | bytes 393224 | tf_op jit(solution)/shard_map/ppermute | solution.py:360
  89.0 3.6 %collective-permute-done.17.p2 = bf16[128,512]{1,0:T(8,128)(2,1)S(1)} collective-permute-done((bf16[128,512]{1,0:T(8,128)(2,1)S(1)}, bf16[128,512]{1,0:T(8,128)(2,1)S(1)}, u32[]{:S(2)}, u32[]{:S(2)}) %collective-permute-start.17) | collective-permute-done | bytes 131104 | tf_op jit(solution)/shard_map/ppermute | solution.py:360
  93.0 1.6 %main_pass.3 = (bf16[2,128,1024]{2,1,0:T(8,128)(2,1)S(1)}, f32[2,128,1024]{2,1,0:T(8,128)S(1)}) custom-call(s32[2]{0:T(128)S(1)} %pad_add_fusion.at_ref, bf16[512,1024]{1,0:T(8,128)(2,1)S(1)} %get-tuple-element.80.h_ref, bf16[128,512]{1,0:T(8,128)(2,1)S(1)} %get-tuple-element.94.p0, bf16[128,512]{1,0:T(8,128)(2,1)S(1)} %collective-permute-done.16.p1, ...), custom_call_target="tpu_custom_call" | custom-call | flops 1500000000 | bytes 4000000 | tf_op jit(solution)/shard_map/main_pass/pallas_call | solution.py:253
  94.8 2.4 %collective-permute-start.26 = (f32[24,512]{1,0:T(8,128)S(1)}, f32[24,512]{1,0:T(8,128)S(1)}, u32[]{:S(2)}, u32[]{:S(2)}) collective-permute-start(f32[24,512]{1,0:T(8,128)S(1)} %get-tuple-element.100.s0), channel_id=1, source_target_pairs={{0,24},{8,16},{16,8},{24,0},{1,25},{9,17},{17,9},{25,1},{2,26},{10... | collective-permute-start | bytes 147464 | tf_op jit(solution)/shard_map/ppermute | solution.py:360
  97.2 2.0 %collective-permute-start.24 = (f32[24,512]{1,0:T(8,128)S(1)}, f32[24,512]{1,0:T(8,128)S(1)}, u32[]{:S(2)}, u32[]{:S(2)}) collective-permute-start(f32[24,512]{1,0:T(8,128)S(1)} %get-tuple-element.100.s0), channel_id=1, source_target_pairs={{0,8},{8,0},{16,24},{24,16},{1,9},{9,1},{17,25},{25,17},{2,10},{10... | collective-permute-start | bytes 147464 | tf_op jit(solution)/shard_map/ppermute | solution.py:360
  103.1 2.4 %collective-permute-start.29 = (bf16[80,512]{1,0:T(8,128)(2,1)S(1)}, bf16[80,512]{1,0:T(8,128)(2,1)S(1)}, u32[]{:S(2)}, u32[]{:S(2)}) collective-permute-start(bf16[80,512]{1,0:T(8,128)(2,1)S(1)} %step_pass.1.x0), channel_id=1, source_target_pairs={{0,24},{8,16},{16,8},{24,0},{1,25},{9,17},{17,9},{25,1},{2,26},{10... | collective-permute-start | bytes 245768 | tf_op jit(solution)/shard_map/ppermute | solution.py:360
  105.4 2.0 %collective-permute-start.27 = (bf16[80,512]{1,0:T(8,128)(2,1)S(1)}, bf16[80,512]{1,0:T(8,128)(2,1)S(1)}, u32[]{:S(2)}, u32[]{:S(2)}) collective-permute-start(bf16[80,512]{1,0:T(8,128)(2,1)S(1)} %step_pass.1.x0), channel_id=1, source_target_pairs={{0,8},{8,0},{16,24},{24,16},{1,9},{9,1},{17,25},{25,17},{2,10},{10... | collective-permute-start | bytes 245768 | tf_op jit(solution)/shard_map/ppermute | solution.py:360
  110.9 1.9 %collective-permute-done.28.x2 = bf16[80,512]{1,0:T(8,128)(2,1)S(1)} collective-permute-done((bf16[80,512]{1,0:T(8,128)(2,1)S(1)}, bf16[80,512]{1,0:T(8,128)(2,1)S(1)}, u32[]{:S(2)}, u32[]{:S(2)}) %collective-permute-start.28) | collective-permute-done | bytes 81952 | tf_op jit(solution)/shard_map/ppermute | solution.py:360
  117.5 2.9 %collective-permute-done.31.r2 = bf16[64,1024]{1,0:T(8,128)(2,1)S(1)} collective-permute-done((bf16[64,1024]{1,0:T(8,128)(2,1)S(1)}, bf16[64,1024]{1,0:T(8,128)(2,1)S(1)}, u32[]{:S(2)}, u32[]{:S(2)}) %collective-permute-start.31) | collective-permute-done | bytes 131104 | tf_op jit(solution)/shard_map/ppermute | solution.py:360
  120.4 1.7 %collective-permute-done.32.r3 = bf16[64,1024]{1,0:T(8,128)(2,1)S(1)} collective-permute-done((bf16[64,1024]{1,0:T(8,128)(2,1)S(1)}, bf16[64,1024]{1,0:T(8,128)(2,1)S(1)}, u32[]{:S(2)}, u32[]{:S(2)}) %collective-permute-start.32) | collective-permute-done | bytes 131104 | tf_op jit(solution)/shard_map/ppermute | solution.py:360
  124.5 4.1 %collective-permute-done.33.l1 = bf16[72,1024]{1,0:T(8,128)(2,1)S(1)} collective-permute-done((bf16[72,1024]{1,0:T(8,128)(2,1)S(1)}, bf16[72,1024]{1,0:T(8,128)(2,1)S(1)}, u32[]{:S(2)}, u32[]{:S(2)}) %collective-permute-start.33) | collective-permute-done | bytes 147488 | tf_op jit(solution)/shard_map/ppermute | solution.py:360
  (81 shorter events, 32.2 us)
Async XLA Ops:
  2.9 17.1 %collective-permute-start = (bf16[128,1280]{1,0:T(8,128)(2,1)S(1)}, bf16[128,1280]{1,0:T(8,128)(2,1)S(1)}, u32[]{:S(2)}, u32[]{:S(2)}) collective-permute-start(bf16[128,1280]{1,0:T(8,128)(2,1)S(1)} %get-tuple-element.63), channel_id=1, source_target_pairs={{0,8},{8,0},{16,24},{24,16},{1,9},{9,1},{17,25},{25,17},{2,10},{10... | collective-permute-start | bytes 983048 | tf_op jit(solution)/shard_map/ppermute | solution.py:360
  6.0 27.6 %collective-permute-start.1 = (bf16[128,1280]{1,0:T(8,128)(2,1)S(1)}, bf16[128,1280]{1,0:T(8,128)(2,1)S(1)}, u32[]{:S(2)}, u32[]{:S(2)}) collective-permute-start(bf16[128,1280]{1,0:T(8,128)(2,1)S(1)} %get-tuple-element.64), channel_id=1, source_target_pairs={{0,16},{8,24},{16,0},{24,8},{1,17},{9,25},{17,1},{25,9},{2,18},{10... | collective-permute-start | bytes 983048 | tf_op jit(solution)/shard_map/ppermute | solution.py:360
  8.6 28.3 %collective-permute-start.2 = (bf16[128,1280]{1,0:T(8,128)(2,1)S(1)}, bf16[128,1280]{1,0:T(8,128)(2,1)S(1)}, u32[]{:S(2)}, u32[]{:S(2)}) collective-permute-start(bf16[128,1280]{1,0:T(8,128)(2,1)S(1)} %get-tuple-element.65), channel_id=1, source_target_pairs={{0,24},{8,16},{16,8},{24,0},{1,25},{9,17},{17,9},{25,1},{2,26},{10... | collective-permute-start | bytes 983048 | tf_op jit(solution)/shard_map/ppermute | solution.py:360
  29.1 19.7 %collective-permute-start.3 = (bf16[272,128]{1,0:T(8,128)(2,1)S(1)}, bf16[272,128]{1,0:T(8,128)(2,1)S(1)}, u32[]{:S(2)}, u32[]{:S(2)}) collective-permute-start(bf16[272,128]{1,0:T(8,128)(2,1)S(1)} %get-tuple-element.70), channel_id=1, source_target_pairs={{0,8},{8,0},{16,24},{24,16},{1,9},{9,1},{17,25},{25,17},{2,10},{10... | collective-permute-start | bytes 208904 | tf_op jit(solution)/shard_map/ppermute | solution.py:360
  29.1 24.8 %collective-permute-start.4 = (bf16[272,128]{1,0:T(8,128)(2,1)S(1)}, bf16[272,128]{1,0:T(8,128)(2,1)S(1)}, u32[]{:S(2)}, u32[]{:S(2)}) collective-permute-start(bf16[272,128]{1,0:T(8,128)(2,1)S(1)} %get-tuple-element.71), channel_id=1, source_target_pairs={{0,16},{8,24},{16,0},{24,8},{1,17},{9,25},{17,1},{25,9},{2,18},{10... | collective-permute-start | bytes 208904 | tf_op jit(solution)/shard_map/ppermute | solution.py:360
  32.9 21.1 %collective-permute-start.5 = (bf16[272,128]{1,0:T(8,128)(2,1)S(1)}, bf16[272,128]{1,0:T(8,128)(2,1)S(1)}, u32[]{:S(2)}, u32[]{:S(2)}) collective-permute-start(bf16[272,128]{1,0:T(8,128)(2,1)S(1)} %get-tuple-element.72), channel_id=1, source_target_pairs={{0,24},{8,16},{16,8},{24,0},{1,25},{9,17},{17,9},{25,1},{2,26},{10... | collective-permute-start | bytes 208904 | tf_op jit(solution)/shard_map/ppermute | solution.py:360
  33.6 30.3 %collective-permute-start.11 = (bf16[128,1024]{1,0:T(8,128)(2,1)S(1)}, bf16[128,1024]{1,0:T(8,128)(2,1)S(1)}, u32[]{:S(2)}, u32[]{:S(2)}) collective-permute-start(bf16[128,1024]{1,0:T(8,128)(2,1)S(1)} %get-tuple-element.119), channel_id=1, source_target_pairs={{0,24},{8,16},{16,8},{24,0},{1,25},{9,17},{17,9},{25,1},{2,26},{10... | collective-permute-start | bytes 786440 | tf_op jit(solution)/shard_map/ppermute | solution.py:360
  36.9 36.5 %collective-permute-start.10 = (bf16[128,1024]{1,0:T(8,128)(2,1)S(1)}, bf16[128,1024]{1,0:T(8,128)(2,1)S(1)}, u32[]{:S(2)}, u32[]{:S(2)}) collective-permute-start(bf16[128,1024]{1,0:T(8,128)(2,1)S(1)} %get-tuple-element.120), channel_id=1, source_target_pairs={{0,16},{8,24},{16,0},{24,8},{1,17},{9,25},{17,1},{25,9},{2,18},{10... | collective-permute-start | bytes 786440 | tf_op jit(solution)/shard_map/ppermute | solution.py:360
  48.7 9.5 %collective-permute-start.6 = (bf16[128,1024]{1,0:T(8,128)(2,1)S(1)}, bf16[128,1024]{1,0:T(8,128)(2,1)S(1)}, u32[]{:S(2)}, u32[]{:S(2)}) collective-permute-start(bf16[128,1024]{1,0:T(8,128)(2,1)S(1)} %get-tuple-element.122), channel_id=1, source_target_pairs={{0,8},{8,0},{16,24},{24,16},{1,9},{9,1},{17,25},{25,17},{2,10},{10... | collective-permute-start | bytes 786440 | tf_op jit(solution)/shard_map/ppermute | solution.py:360
  59.5 13.9 %collective-permute-start.9 = (bf16[144,512]{1,0:T(8,128)(2,1)S(1)}, bf16[144,512]{1,0:T(8,128)(2,1)S(1)}, u32[]{:S(2)}, u32[]{:S(2)}) collective-permute-start(bf16[144,512]{1,0:T(8,128)(2,1)S(1)} %get-tuple-element.82.m0.p0), channel_id=1, source_target_pairs={{0,24},{8,16},{16,8},{24,0},{1,25},{9,17},{17,9},{25,1},{2,26},{10... | collective-permute-start | bytes 442376 | tf_op jit(solution)/shard_map/ppermute | solution.py:360
  60.1 18.2 %collective-permute-start.8 = (bf16[144,512]{1,0:T(8,128)(2,1)S(1)}, bf16[144,512]{1,0:T(8,128)(2,1)S(1)}, u32[]{:S(2)}, u32[]{:S(2)}) collective-permute-start(bf16[144,512]{1,0:T(8,128)(2,1)S(1)} %get-tuple-element.82.m0.p0), channel_id=1, source_target_pairs={{0,16},{8,24},{16,0},{24,8},{1,17},{9,25},{17,1},{25,9},{2,18},{10... | collective-permute-start | bytes 442376 | tf_op jit(solution)/shard_map/ppermute | solution.py:360
  63.4 14.9 %collective-permute-start.7 = (bf16[144,512]{1,0:T(8,128)(2,1)S(1)}, bf16[144,512]{1,0:T(8,128)(2,1)S(1)}, u32[]{:S(2)}, u32[]{:S(2)}) collective-permute-start(bf16[144,512]{1,0:T(8,128)(2,1)S(1)} %get-tuple-element.82.m0.p0), channel_id=1, source_target_pairs={{0,8},{8,0},{16,24},{24,16},{1,9},{9,1},{17,25},{25,17},{2,10},{10... | collective-permute-start | bytes 442376 | tf_op jit(solution)/shard_map/ppermute | solution.py:360
  79.2 8.4 %collective-permute-start.18 = (bf16[128,512]{1,0:T(8,128)(2,1)S(1)}, bf16[128,512]{1,0:T(8,128)(2,1)S(1)}, u32[]{:S(2)}, u32[]{:S(2)}) collective-permute-start(bf16[128,512]{1,0:T(8,128)(2,1)S(1)} %get-tuple-element.94.p0), channel_id=1, source_target_pairs={{0,24},{8,16},{16,8},{24,0},{1,25},{9,17},{17,9},{25,1},{2,26},{10... | collective-permute-start | bytes 393224 | tf_op jit(solution)/shard_map/ppermute | solution.py:360
  81.7 11.0 %collective-permute-start.17 = (bf16[128,512]{1,0:T(8,128)(2,1)S(1)}, bf16[128,512]{1,0:T(8,128)(2,1)S(1)}, u32[]{:S(2)}, u32[]{:S(2)}) collective-permute-start(bf16[128,512]{1,0:T(8,128)(2,1)S(1)} %get-tuple-element.94.p0), channel_id=1, source_target_pairs={{0,16},{8,24},{16,0},{24,8},{1,17},{9,25},{17,1},{25,9},{2,18},{10... | collective-permute-start | bytes 393224 | tf_op jit(solution)/shard_map/ppermute | solution.py:360
  81.7 11.0 %collective-permute-start.16 = (bf16[128,512]{1,0:T(8,128)(2,1)S(1)}, bf16[128,512]{1,0:T(8,128)(2,1)S(1)}, u32[]{:S(2)}, u32[]{:S(2)}) collective-permute-start(bf16[128,512]{1,0:T(8,128)(2,1)S(1)} %get-tuple-element.94.p0), channel_id=1, source_target_pairs={{0,8},{8,0},{16,24},{24,16},{1,9},{9,1},{17,25},{25,17},{2,10},{10... | collective-permute-start | bytes 393224 | tf_op jit(solution)/shard_map/ppermute | solution.py:360
  85.1 14.1 %collective-permute-start.13 = (bf16[2,128,1024]{2,1,0:T(8,128)(2,1)S(1)}, bf16[2,128,1024]{2,1,0:T(8,128)(2,1)S(1)}, u32[]{:S(2)}, u32[]{:S(2)}) collective-permute-start(bf16[2,128,1024]{2,1,0:T(8,128)(2,1)S(1)} %get-tuple-element.87), channel_id=1, source_target_pairs={{0,2},{2,0},{4,6},{6,4},{1,3},{3,1},{5,7},{7,5},{8,10},{10,8},{12,... | collective-permute-start | bytes 1572872 | tf_op jit(solution)/shard_map/ppermute | solution.py:360
  85.1 7.5 %collective-permute-start.20 = (f32[16,1280]{1,0:T(8,128)S(1)}, f32[16,1280]{1,0:T(8,128)S(1)}, u32[]{:S(2)}, u32[]{:S(2)}) collective-permute-start(f32[16,1280]{1,0:T(8,128)S(1)} %get-tuple-element.89.l0), channel_id=1, source_target_pairs={{0,6},{2,4},{4,2},{6,0},{1,7},{3,5},{5,3},{7,1},{8,14},{10,12},{12... | collective-permute-start | bytes 245768 | tf_op jit(solution)/shard_map/ppermute | solution.py:360
  94.6 12.8 %collective-permute-start.21 = (bf16[2,128,1024]{2,1,0:T(8,128)(2,1)S(1)}, bf16[2,128,1024]{2,1,0:T(8,128)(2,1)S(1)}, u32[]{:S(2)}, u32[]{:S(2)}) collective-permute-start(bf16[2,128,1024]{2,1,0:T(8,128)(2,1)S(1)} %get-tuple-element.99), channel_id=1, source_target_pairs={{0,2},{2,0},{4,6},{6,4},{1,3},{3,1},{5,7},{7,5},{8,10},{10,8},{12,... | collective-permute-start | bytes 1572872 | tf_op jit(solution)/shard_map/ppermute | solution.py:360
  99.4 9.8 %collective-permute-start.14 = (bf16[128,1024]{1,0:T(8,128)(2,1)S(1)}, bf16[128,1024]{1,0:T(8,128)(2,1)S(1)}, u32[]{:S(2)}, u32[]{:S(2)}) collective-permute-start(bf16[128,1024]{1,0:T(8,128)(2,1)S(1)} %fusion.9), channel_id=1, source_target_pairs={{0,4},{2,6},{4,0},{6,2},{1,5},{3,7},{5,1},{7,3},{8,12},{10,14},{12... | collective-permute-start | bytes 786440 | tf_op jit(solution)/shard_map/ppermute | solution.py:360
  103.1 7.8 %collective-permute-start.29 = (bf16[80,512]{1,0:T(8,128)(2,1)S(1)}, bf16[80,512]{1,0:T(8,128)(2,1)S(1)}, u32[]{:S(2)}, u32[]{:S(2)}) collective-permute-start(bf16[80,512]{1,0:T(8,128)(2,1)S(1)} %step_pass.1.x0), channel_id=1, source_target_pairs={{0,24},{8,16},{16,8},{24,0},{1,25},{9,17},{17,9},{25,1},{2,26},{10... | collective-permute-start | bytes 245768 | tf_op jit(solution)/shard_map/ppermute | solution.py:360
  105.4 7.3 %collective-permute-start.28 = (bf16[80,512]{1,0:T(8,128)(2,1)S(1)}, bf16[80,512]{1,0:T(8,128)(2,1)S(1)}, u32[]{:S(2)}, u32[]{:S(2)}) collective-permute-start(bf16[80,512]{1,0:T(8,128)(2,1)S(1)} %step_pass.1.x0), channel_id=1, source_target_pairs={{0,16},{8,24},{16,0},{24,8},{1,17},{9,25},{17,1},{25,9},{2,18},{10... | collective-permute-start | bytes 245768 | tf_op jit(solution)/shard_map/ppermute | solution.py:360
  107.6 8.2 %collective-permute-start.22 = (bf16[128,1024]{1,0:T(8,128)(2,1)S(1)}, bf16[128,1024]{1,0:T(8,128)(2,1)S(1)}, u32[]{:S(2)}, u32[]{:S(2)}) collective-permute-start(bf16[128,1024]{1,0:T(8,128)(2,1)S(1)} %fusion.10), channel_id=1, source_target_pairs={{0,4},{2,6},{4,0},{6,2},{1,5},{3,7},{5,1},{7,3},{8,12},{10,14},{12... | collective-permute-start | bytes 786440 | tf_op jit(solution)/shard_map/ppermute | solution.py:360
  109.3 14.5 %collective-permute-start.15 = (bf16[128,1024]{1,0:T(8,128)(2,1)S(1)}, bf16[128,1024]{1,0:T(8,128)(2,1)S(1)}, u32[]{:S(2)}, u32[]{:S(2)}) collective-permute-start(bf16[128,1024]{1,0:T(8,128)(2,1)S(1)} %fusion.8.a0), channel_id=1, source_target_pairs={{0,1},{1,0},{2,3},{3,2},{4,5},{5,4},{6,7},{7,6},{8,9},{9,8},{10,11... | collective-permute-start | bytes 786440 | tf_op jit(solution)/shard_map/ppermute | solution.py:360
  115.9 8.6 %collective-permute-start.23 = (bf16[128,1024]{1,0:T(8,128)(2,1)S(1)}, bf16[128,1024]{1,0:T(8,128)(2,1)S(1)}, u32[]{:S(2)}, u32[]{:S(2)}) collective-permute-start(bf16[128,1024]{1,0:T(8,128)(2,1)S(1)} %fusion.4.b0), channel_id=1, source_target_pairs={{0,1},{1,0},{2,3},{3,2},{4,5},{5,4},{6,7},{7,6},{8,9},{9,8},{10,11... | collective-permute-start | bytes 786440 | tf_op jit(solution)/shard_map/ppermute | solution.py:360
  (16 other events, 200.0 us)

commit v6 on v5

--- a/solution.py
+++ b/solution.py
@@ -182,9 +182,12 @@
     rank, own = up_grad_ref.shape
     width = h_ref.shape[1]
     low_rank = (l0[...] + l1[...]) + (l2[...] + l3[...])
-    out_ref[:rank, :] = dot(low_rank[:, :width].astype(BF16), h_ref[...], 1, 1)
+    moved = dot(low_rank[:, :width].astype(BF16), h_ref[...], 1, 1)
     squares = jnp.sum(jnp.sum(low_rank * low_rank, axis=1, keepdims=True), axis=0, keepdims=True)
-    out_ref[rank:, :] = jnp.broadcast_to(squares, (out_ref.shape[0] - rank, out_ref.shape[1]))
+    rough = squares.astype(BF16).astype(F32)
+    shape = ((out_ref.shape[0] - rank) // 2, out_ref.shape[1])
+    sums = [jnp.broadcast_to(part, shape) for part in (rough, squares - rough)]
+    out_ref[...] = jnp.concatenate([moved] + sums, axis=0).astype(BF16)
     up_grad_ref[...] = low_rank[:, width:]
 
 
@@ -194,7 +197,7 @@
     return pl.pallas_call(
         moved_kernel,
         in_specs=[VMEM] * 5,
-        out_shape=[struct((rank + 8, seq), F32), struct((rank, total - width), F32)],
+        out_shape=[struct((rank + 16, seq), BF16), struct((rank, total - width), F32)],
         cost_estimate=cost(500_000_000, 1_200_000),
         compiler_params=grant(12),
         name="moved_pass",
@@ -203,9 +206,11 @@
 
 def step_kernel(s0, s1, s2, s3, low_ref, g_ref, up_ref, up_grad_ref, out_ref, *, count, factor):
     rank, own = up_ref.shape
-    both = (s0[...] + s1[...]) + (s2[...] + s3[...])
+    both = [ref[...].astype(F32) for ref in (s0, s1, s2, s3)]
+    both = (both[0] + both[1]) + (both[2] + both[3])
+    squares = both[rank : rank + 1, :1] + both[rank + 8 : rank + 9, :1]
     rows = jnp.concatenate([low_ref[...].astype(F32), both[:rank, :]], axis=0).astype(BF16)
-    spread = jnp.sqrt(both[rank : rank + 1, :1] / count + 1e-06)
+    spread = jnp.sqrt(squares / count + 1e-06)
     step = ATTACK_STEP / spread
     groups = g_ref.shape[0]
     for g in range(groups):

time: 131 us -> 130 us (level)
  transfers between devices with their start and end apart: 34 -> 34, of which waited for: 13 -> 12; matrix products, arithmetic and copies ran while one was open for 8% -> 8% of each run, Pallas kernels for 9% -> 9%
where the time goes in v6:
time: 130 us; the launch traced here: 129 us
  starting transfers between devices  56 us (43%)
  waiting for transfers between devices  46.3 us (36%)
  Pallas kernels  14.3 us (11%)
  matrix products  8.96 us (7%)
  local copies, waits for them, and re-layouts  3.08 us (2%)
    ppermute x34, starting transfers between devices, swap(): return lax.ppermute(array, axis, [(i, i ^ bits) for i in range(count)])  56 us
    ppermute x34, waiting for transfers between devices, swap(): return lax.ppermute(array, axis, [(i, i ^ bits) for i in range(count)])  46.3 us
    dot_general x3, matrix products, dot(): lax.dot_general(a, b, (((da,), (db,)), ((), ())), preferred_element_type=...  8.96 us
    pallas_call x1, Pallas kernels, gram(): pl.pallas_call(functools.partial(gram_kernel, docs=lengths.shape[0], reac...  5.2 us
    pallas_call x2, Pallas kernels, main_pass(): pl.pallas_call(main_kernel, in_specs=[SMEM] + [VMEM] * 5, out_shape=[stru...  3.04 us
  transfers between devices with their start and end apart: 34, of which 12 were waited for; matrix products, arithmetic and copies ran while one was open for 8% of the time, Pallas kernels for 9%

profile of v6, /device:TPU:0, one launch (start us, length us, event | category | flops | bytes accessed | tf_op | source)
XLA Modules:
  0.0 129.5 jit_solution(17354182064057950897)
XLA Ops:
  2.9 3.1 %collective-permute-start = (bf16[128,1280]{1,0:T(8,128)(2,1)S(1)}, bf16[128,1280]{1,0:T(8,128)(2,1)S(1)}, u32[]{:S(2)}, u32[]{:S(2)}) collective-permute-start(bf16[128,1280]{1,0:T(8,128)(2,1)S(1)} %get-tuple-element.63), channel_id=1, source_target_pairs={{0,8},{8,0},{16,24},{24,16},{1,9},{9,1},{17,25},{25,17},{2,10},{10... | collective-permute-start | bytes 983048 | tf_op jit(solution)/shard_map/ppermute | solution.py:365
  6.0 2.6 %collective-permute-start.1 = (bf16[128,1280]{1,0:T(8,128)(2,1)S(1)}, bf16[128,1280]{1,0:T(8,128)(2,1)S(1)}, u32[]{:S(2)}, u32[]{:S(2)}) collective-permute-start(bf16[128,1280]{1,0:T(8,128)(2,1)S(1)} %get-tuple-element.64), channel_id=1, source_target_pairs={{0,16},{8,24},{16,0},{24,8},{1,17},{9,25},{17,1},{25,9},{2,18},{10... | collective-permute-start | bytes 983048 | tf_op jit(solution)/shard_map/ppermute | solution.py:365
  9.4 10.6 %collective-permute-done.p1 = bf16[128,1280]{1,0:T(8,128)(2,1)S(1)} collective-permute-done((bf16[128,1280]{1,0:T(8,128)(2,1)S(1)}, bf16[128,1280]{1,0:T(8,128)(2,1)S(1)}, u32[]{:S(2)}, u32[]{:S(2)}) %collective-permute-start) | collective-permute-done | bytes 327712 | tf_op jit(solution)/shard_map/ppermute | solution.py:365
  22.7 6.3 %fusion = bf16[128,1024]{0,1:T(8,128)(2,1)S(1)} fusion(f32[128,1024]{0,1:T(8,128)S(1)} %fusion.11, bf16[128,4096]{1,0:T(8,128)(2,1)} %bitcast.43, bf16[4096,1024]{1,0:T(8,128)(2,1)} %param.13), kind=kOutput, calls=%fused_computation.1 | convolution fusion | flops 1074003968 | bytes 10223616 | tf_op jit(solution)/shard_map/dot_general | solution.py:22
  29.1 3.8 %collective-permute-start.4 = (bf16[272,128]{1,0:T(8,128)(2,1)S(1)}, bf16[272,128]{1,0:T(8,128)(2,1)S(1)}, u32[]{:S(2)}, u32[]{:S(2)}) collective-permute-start(bf16[272,128]{1,0:T(8,128)(2,1)S(1)} %get-tuple-element.71), channel_id=1, source_target_pairs={{0,16},{8,24},{16,0},{24,8},{1,17},{9,25},{17,1},{25,9},{2,18},{10... | collective-permute-start | bytes 208904 | tf_op jit(solution)/shard_map/ppermute | solution.py:365
  33.6 3.3 %collective-permute-start.11 = (bf16[128,1024]{1,0:T(8,128)(2,1)S(1)}, bf16[128,1024]{1,0:T(8,128)(2,1)S(1)}, u32[]{:S(2)}, u32[]{:S(2)}) collective-permute-start(bf16[128,1024]{1,0:T(8,128)(2,1)S(1)} %get-tuple-element.119), channel_id=1, source_target_pairs={{0,24},{8,16},{16,8},{24,0},{1,25},{9,17},{17,9},{25,1},{2,26},{10... | collective-permute-start | bytes 786440 | tf_op jit(solution)/shard_map/ppermute | solution.py:365
  36.9 11.9 %collective-permute-start.10 = (bf16[128,1024]{1,0:T(8,128)(2,1)S(1)}, bf16[128,1024]{1,0:T(8,128)(2,1)S(1)}, u32[]{:S(2)}, u32[]{:S(2)}) collective-permute-start(bf16[128,1024]{1,0:T(8,128)(2,1)S(1)} %get-tuple-element.120), channel_id=1, source_target_pairs={{0,16},{8,24},{16,0},{24,8},{1,17},{9,25},{17,1},{25,9},{2,18},{10... | collective-permute-start | bytes 786440 | tf_op jit(solution)/shard_map/ppermute | solution.py:365
  48.8 5.2 %gram.1 = (bf16[2,512,512]{2,1,0:T(8,128)(2,1)S(1)}, f32[2,128,512]{2,1,0:T(8,128)S(1)}) custom-call(s32[2]{0:T(128)S(1)} %pad_add_fusion.at_ref, s32[8]{0:T(128)S(1)} %bitcast.41, bf16[128,1280]{1,0:T(8,128)(2,1)S(1)} %get-tuple-element.62.p0, bf16[128,1280]{1,0:T(8,128)(2,1)S(1)} %collective-permute-done.p1, ...), custom_call_target="tpu_custom_call" | custom-call | flops 4000000000 | bytes 5000000 | tf_op jit(solution)/shard_map/gram/pallas_call | solution.py:103
  54.0 4.3 %collective-permute-done.6.h1 = bf16[128,1024]{1,0:T(8,128)(2,1)S(1)} collective-permute-done((bf16[128,1024]{1,0:T(8,128)(2,1)S(1)}, bf16[128,1024]{1,0:T(8,128)(2,1)S(1)}, u32[]{:S(2)}, u32[]{:S(2)}) %collective-permute-start.6) | collective-permute-done | bytes 262176 | tf_op jit(solution)/shard_map/ppermute | solution.py:365
  60.1 3.3 %collective-permute-start.8 = (bf16[144,512]{1,0:T(8,128)(2,1)S(1)}, bf16[144,512]{1,0:T(8,128)(2,1)S(1)}, u32[]{:S(2)}, u32[]{:S(2)}) collective-permute-start(bf16[144,512]{1,0:T(8,128)(2,1)S(1)} %get-tuple-element.82.m0.p0), channel_id=1, source_target_pairs={{0,16},{8,24},{16,0},{24,8},{1,17},{9,25},{17,1},{25,9},{2,18},{10... | collective-permute-start | bytes 442376 | tf_op jit(solution)/shard_map/ppermute | solution.py:365
  63.9 9.5 %collective-permute-done.10.h2 = bf16[128,1024]{1,0:T(8,128)(2,1)S(1)} collective-permute-done((bf16[128,1024]{1,0:T(8,128)(2,1)S(1)}, bf16[128,1024]{1,0:T(8,128)(2,1)S(1)}, u32[]{:S(2)}, u32[]{:S(2)}) %collective-permute-start.10) | collective-permute-done | bytes 262176 | tf_op jit(solution)/shard_map/ppermute | solution.py:365
  73.4 5.0 %collective-permute-done.8.m2.p2 = bf16[144,512]{1,0:T(8,128)(2,1)S(1)} collective-permute-done((bf16[144,512]{1,0:T(8,128)(2,1)S(1)}, bf16[144,512]{1,0:T(8,128)(2,1)S(1)}, u32[]{:S(2)}, u32[]{:S(2)}) %collective-permute-start.8) | collective-permute-done | bytes 147488 | tf_op jit(solution)/shard_map/ppermute | solution.py:365
  79.2 2.5 %collective-permute-start.18 = (bf16[128,512]{1,0:T(8,128)(2,1)S(1)}, bf16[128,512]{1,0:T(8,128)(2,1)S(1)}, u32[]{:S(2)}, u32[]{:S(2)}) collective-permute-start(bf16[128,512]{1,0:T(8,128)(2,1)S(1)} %get-tuple-element.94.p0), channel_id=1, source_target_pairs={{0,24},{8,16},{16,8},{24,0},{1,25},{9,17},{17,9},{25,1},{2,26},{10... | collective-permute-start | bytes 393224 | tf_op jit(solution)/shard_map/ppermute | solution.py:365
  81.7 2.0 %collective-permute-start.16 = (bf16[128,512]{1,0:T(8,128)(2,1)S(1)}, bf16[128,512]{1,0:T(8,128)(2,1)S(1)}, u32[]{:S(2)}, u32[]{:S(2)}) collective-permute-start(bf16[128,512]{1,0:T(8,128)(2,1)S(1)} %get-tuple-element.94.p0), channel_id=1, source_target_pairs={{0,8},{8,0},{16,24},{24,16},{1,9},{9,1},{17,25},{25,17},{2,10},{10... | collective-permute-start | bytes 393224 | tf_op jit(solution)/shard_map/ppermute | solution.py:365
  89.0 3.6 %collective-permute-done.17.p2 = bf16[128,512]{1,0:T(8,128)(2,1)S(1)} collective-permute-done((bf16[128,512]{1,0:T(8,128)(2,1)S(1)}, bf16[128,512]{1,0:T(8,128)(2,1)S(1)}, u32[]{:S(2)}, u32[]{:S(2)}) %collective-permute-start.17) | collective-permute-done | bytes 131104 | tf_op jit(solution)/shard_map/ppermute | solution.py:365
  93.0 1.6 %main_pass.3 = (bf16[2,128,1024]{2,1,0:T(8,128)(2,1)S(1)}, f32[2,128,1024]{2,1,0:T(8,128)S(1)}) custom-call(s32[2]{0:T(128)S(1)} %pad_add_fusion.at_ref, bf16[512,1024]{1,0:T(8,128)(2,1)S(1)} %get-tuple-element.80.h_ref, bf16[128,512]{1,0:T(8,128)(2,1)S(1)} %get-tuple-element.94.p0, bf16[128,512]{1,0:T(8,128)(2,1)S(1)} %collective-permute-done.16.p1, ...), custom_call_target="tpu_custom_call" | custom-call | flops 1500000000 | bytes 4000000 | tf_op jit(solution)/shard_map/main_pass/pallas_call | solution.py:258
  94.8 2.4 %collective-permute-start.26 = (bf16[32,512]{1,0:T(8,128)(2,1)S(1)}, bf16[32,512]{1,0:T(8,128)(2,1)S(1)}, u32[]{:S(2)}, u32[]{:S(2)}) collective-permute-start(bf16[32,512]{1,0:T(8,128)(2,1)S(1)} %get-tuple-element.100.s0), channel_id=1, source_target_pairs={{0,24},{8,16},{16,8},{24,0},{1,25},{9,17},{17,9},{25,1},{2,26},{10... | collective-permute-start | bytes 98312 | tf_op jit(solution)/shard_map/ppermute | solution.py:365
  97.2 2.0 %collective-permute-start.24 = (bf16[32,512]{1,0:T(8,128)(2,1)S(1)}, bf16[32,512]{1,0:T(8,128)(2,1)S(1)}, u32[]{:S(2)}, u32[]{:S(2)}) collective-permute-start(bf16[32,512]{1,0:T(8,128)(2,1)S(1)} %get-tuple-element.100.s0), channel_id=1, source_target_pairs={{0,8},{8,0},{16,24},{24,16},{1,9},{9,1},{17,25},{25,17},{2,10},{10... | collective-permute-start | bytes 98312 | tf_op jit(solution)/shard_map/ppermute | solution.py:365
  102.3 2.1 %collective-permute-start.29 = (bf16[80,512]{1,0:T(8,128)(2,1)S(1)}, bf16[80,512]{1,0:T(8,128)(2,1)S(1)}, u32[]{:S(2)}, u32[]{:S(2)}) collective-permute-start(bf16[80,512]{1,0:T(8,128)(2,1)S(1)} %step_pass.1.x0), channel_id=1, source_target_pairs={{0,24},{8,16},{16,8},{24,0},{1,25},{9,17},{17,9},{25,1},{2,26},{10... | collective-permute-start | bytes 245768 | tf_op jit(solution)/shard_map/ppermute | solution.py:365
  104.8 1.8 %collective-permute-start.27 = (bf16[80,512]{1,0:T(8,128)(2,1)S(1)}, bf16[80,512]{1,0:T(8,128)(2,1)S(1)}, u32[]{:S(2)}, u32[]{:S(2)}) collective-permute-start(bf16[80,512]{1,0:T(8,128)(2,1)S(1)} %step_pass.1.x0), channel_id=1, source_target_pairs={{0,8},{8,0},{16,24},{24,16},{1,9},{9,1},{17,25},{25,17},{2,10},{10... | collective-permute-start | bytes 245768 | tf_op jit(solution)/shard_map/ppermute | solution.py:365
  110.1 1.9 %collective-permute-done.28.x2 = bf16[80,512]{1,0:T(8,128)(2,1)S(1)} collective-permute-done((bf16[80,512]{1,0:T(8,128)(2,1)S(1)}, bf16[80,512]{1,0:T(8,128)(2,1)S(1)}, u32[]{:S(2)}, u32[]{:S(2)}) %collective-permute-start.28) | collective-permute-done | bytes 81952 | tf_op jit(solution)/shard_map/ppermute | solution.py:365
  116.7 2.9 %collective-permute-done.31.r2 = bf16[64,1024]{1,0:T(8,128)(2,1)S(1)} collective-permute-done((bf16[64,1024]{1,0:T(8,128)(2,1)S(1)}, bf16[64,1024]{1,0:T(8,128)(2,1)S(1)}, u32[]{:S(2)}, u32[]{:S(2)}) %collective-permute-start.31) | collective-permute-done | bytes 131104 | tf_op jit(solution)/shard_map/ppermute | solution.py:365
  119.6 1.7 %collective-permute-done.32.r3 = bf16[64,1024]{1,0:T(8,128)(2,1)S(1)} collective-permute-done((bf16[64,1024]{1,0:T(8,128)(2,1)S(1)}, bf16[64,1024]{1,0:T(8,128)(2,1)S(1)}, u32[]{:S(2)}, u32[]{:S(2)}) %collective-permute-start.32) | collective-permute-done | bytes 131104 | tf_op jit(solution)/shard_map/ppermute | solution.py:365
  123.8 4.1 %collective-permute-done.33.l1 = bf16[72,1024]{1,0:T(8,128)(2,1)S(1)} collective-permute-done((bf16[72,1024]{1,0:T(8,128)(2,1)S(1)}, bf16[72,1024]{1,0:T(8,128)(2,1)S(1)}, u32[]{:S(2)}, u32[]{:S(2)}) %collective-permute-start.33) | collective-permute-done | bytes 147488 | tf_op jit(solution)/shard_map/ppermute | solution.py:365
  (81 shorter events, 31.8 us)
Async XLA Ops:
  2.9 17.1 %collective-permute-start = (bf16[128,1280]{1,0:T(8,128)(2,1)S(1)}, bf16[128,1280]{1,0:T(8,128)(2,1)S(1)}, u32[]{:S(2)}, u32[]{:S(2)}) collective-permute-start(bf16[128,1280]{1,0:T(8,128)(2,1)S(1)} %get-tuple-element.63), channel_id=1, source_target_pairs={{0,8},{8,0},{16,24},{24,16},{1,9},{9,1},{17,25},{25,17},{2,10},{10... | collective-permute-start | bytes 983048 | tf_op jit(solution)/shard_map/ppermute | solution.py:365
  6.0 27.6 %collective-permute-start.1 = (bf16[128,1280]{1,0:T(8,128)(2,1)S(1)}, bf16[128,1280]{1,0:T(8,128)(2,1)S(1)}, u32[]{:S(2)}, u32[]{:S(2)}) collective-permute-start(bf16[128,1280]{1,0:T(8,128)(2,1)S(1)} %get-tuple-element.64), channel_id=1, source_target_pairs={{0,16},{8,24},{16,0},{24,8},{1,17},{9,25},{17,1},{25,9},{2,18},{10... | collective-permute-start | bytes 983048 | tf_op jit(solution)/shard_map/ppermute | solution.py:365
  8.6 28.3 %collective-permute-start.2 = (bf16[128,1280]{1,0:T(8,128)(2,1)S(1)}, bf16[128,1280]{1,0:T(8,128)(2,1)S(1)}, u32[]{:S(2)}, u32[]{:S(2)}) collective-permute-start(bf16[128,1280]{1,0:T(8,128)(2,1)S(1)} %get-tuple-element.65), channel_id=1, source_target_pairs={{0,24},{8,16},{16,8},{24,0},{1,25},{9,17},{17,9},{25,1},{2,26},{10... | collective-permute-start | bytes 983048 | tf_op jit(solution)/shard_map/ppermute | solution.py:365
  29.1 19.7 %collective-permute-start.3 = (bf16[272,128]{1,0:T(8,128)(2,1)S(1)}, bf16[272,128]{1,0:T(8,128)(2,1)S(1)}, u32[]{:S(2)}, u32[]{:S(2)}) collective-permute-start(bf16[272,128]{1,0:T(8,128)(2,1)S(1)} %get-tuple-element.70), channel_id=1, source_target_pairs={{0,8},{8,0},{16,24},{24,16},{1,9},{9,1},{17,25},{25,17},{2,10},{10... | collective-permute-start | bytes 208904 | tf_op jit(solution)/shard_map/ppermute | solution.py:365
  29.1 24.8 %collective-permute-start.4 = (bf16[272,128]{1,0:T(8,128)(2,1)S(1)}, bf16[272,128]{1,0:T(8,128)(2,1)S(1)}, u32[]{:S(2)}, u32[]{:S(2)}) collective-permute-start(bf16[272,128]{1,0:T(8,128)(2,1)S(1)} %get-tuple-element.71), channel_id=1, source_target_pairs={{0,16},{8,24},{16,0},{24,8},{1,17},{9,25},{17,1},{25,9},{2,18},{10... | collective-permute-start | bytes 208904 | tf_op jit(solution)/shard_map/ppermute | solution.py:365
  32.9 21.1 %collective-permute-start.5 = (bf16[272,128]{1,0:T(8,128)(2,1)S(1)}, bf16[272,128]{1,0:T(8,128)(2,1)S(1)}, u32[]{:S(2)}, u32[]{:S(2)}) collective-permute-start(bf16[272,128]{1,0:T(8,128)(2,1)S(1)} %get-tuple-element.72), channel_id=1, source_target_pairs={{0,24},{8,16},{16,8},{24,0},{1,25},{9,17},{17,9},{25,1},{2,26},{10... | collective-permute-start | bytes 208904 | tf_op jit(solution)/shard_map/ppermute | solution.py:365
  33.6 30.3 %collective-permute-start.11 = (bf16[128,1024]{1,0:T(8,128)(2,1)S(1)}, bf16[128,1024]{1,0:T(8,128)(2,1)S(1)}, u32[]{:S(2)}, u32[]{:S(2)}) collective-permute-start(bf16[128,1024]{1,0:T(8,128)(2,1)S(1)} %get-tuple-element.119), channel_id=1, source_target_pairs={{0,24},{8,16},{16,8},{24,0},{1,25},{9,17},{17,9},{25,1},{2,26},{10... | collective-permute-start | bytes 786440 | tf_op jit(solution)/shard_map/ppermute | solution.py:365
  36.9 36.5 %collective-permute-start.10 = (bf16[128,1024]{1,0:T(8,128)(2,1)S(1)}, bf16[128,1024]{1,0:T(8,128)(2,1)S(1)}, u32[]{:S(2)}, u32[]{:S(2)}) collective-permute-start(bf16[128,1024]{1,0:T(8,128)(2,1)S(1)} %get-tuple-element.120), channel_id=1, source_target_pairs={{0,16},{8,24},{16,0},{24,8},{1,17},{9,25},{17,1},{25,9},{2,18},{10... | collective-permute-start | bytes 786440 | tf_op jit(solution)/shard_map/ppermute | solution.py:365
  48.7 9.5 %collective-permute-start.6 = (bf16[128,1024]{1,0:T(8,128)(2,1)S(1)}, bf16[128,1024]{1,0:T(8,128)(2,1)S(1)}, u32[]{:S(2)}, u32[]{:S(2)}) collective-permute-start(bf16[128,1024]{1,0:T(8,128)(2,1)S(1)} %get-tuple-element.122), channel_id=1, source_target_pairs={{0,8},{8,0},{16,24},{24,16},{1,9},{9,1},{17,25},{25,17},{2,10},{10... | collective-permute-start | bytes 786440 | tf_op jit(solution)/shard_map/ppermute | solution.py:365
  59.5 13.9 %collective-permute-start.9 = (bf16[144,512]{1,0:T(8,128)(2,1)S(1)}, bf16[144,512]{1,0:T(8,128)(2,1)S(1)}, u32[]{:S(2)}, u32[]{:S(2)}) collective-permute-start(bf16[144,512]{1,0:T(8,128)(2,1)S(1)} %get-tuple-element.82.m0.p0), channel_id=1, source_target_pairs={{0,24},{8,16},{16,8},{24,0},{1,25},{9,17},{17,9},{25,1},{2,26},{10... | collective-permute-start | bytes 442376 | tf_op jit(solution)/shard_map/ppermute | solution.py:365
  60.1 18.2 %collective-permute-start.8 = (bf16[144,512]{1,0:T(8,128)(2,1)S(1)}, bf16[144,512]{1,0:T(8,128)(2,1)S(1)}, u32[]{:S(2)}, u32[]{:S(2)}) collective-permute-start(bf16[144,512]{1,0:T(8,128)(2,1)S(1)} %get-tuple-element.82.m0.p0), channel_id=1, source_target_pairs={{0,16},{8,24},{16,0},{24,8},{1,17},{9,25},{17,1},{25,9},{2,18},{10... | collective-permute-start | bytes 442376 | tf_op jit(solution)/shard_map/ppermute | solution.py:365
  63.4 14.9 %collective-permute-start.7 = (bf16[144,512]{1,0:T(8,128)(2,1)S(1)}, bf16[144,512]{1,0:T(8,128)(2,1)S(1)}, u32[]{:S(2)}, u32[]{:S(2)}) collective-permute-start(bf16[144,512]{1,0:T(8,128)(2,1)S(1)} %get-tuple-element.82.m0.p0), channel_id=1, source_target_pairs={{0,8},{8,0},{16,24},{24,16},{1,9},{9,1},{17,25},{25,17},{2,10},{10... | collective-permute-start | bytes 442376 | tf_op jit(solution)/shard_map/ppermute | solution.py:365
  79.2 8.4 %collective-permute-start.18 = (bf16[128,512]{1,0:T(8,128)(2,1)S(1)}, bf16[128,512]{1,0:T(8,128)(2,1)S(1)}, u32[]{:S(2)}, u32[]{:S(2)}) collective-permute-start(bf16[128,512]{1,0:T(8,128)(2,1)S(1)} %get-tuple-element.94.p0), channel_id=1, source_target_pairs={{0,24},{8,16},{16,8},{24,0},{1,25},{9,17},{17,9},{25,1},{2,26},{10... | collective-permute-start | bytes 393224 | tf_op jit(solution)/shard_map/ppermute | solution.py:365
  81.7 11.0 %collective-permute-start.17 = (bf16[128,512]{1,0:T(8,128)(2,1)S(1)}, bf16[128,512]{1,0:T(8,128)(2,1)S(1)}, u32[]{:S(2)}, u32[]{:S(2)}) collective-permute-start(bf16[128,512]{1,0:T(8,128)(2,1)S(1)} %get-tuple-element.94.p0), channel_id=1, source_target_pairs={{0,16},{8,24},{16,0},{24,8},{1,17},{9,25},{17,1},{25,9},{2,18},{10... | collective-permute-start | bytes 393224 | tf_op jit(solution)/shard_map/ppermute | solution.py:365
  81.7 11.0 %collective-permute-start.16 = (bf16[128,512]{1,0:T(8,128)(2,1)S(1)}, bf16[128,512]{1,0:T(8,128)(2,1)S(1)}, u32[]{:S(2)}, u32[]{:S(2)}) collective-permute-start(bf16[128,512]{1,0:T(8,128)(2,1)S(1)} %get-tuple-element.94.p0), channel_id=1, source_target_pairs={{0,8},{8,0},{16,24},{24,16},{1,9},{9,1},{17,25},{25,17},{2,10},{10... | collective-permute-start | bytes 393224 | tf_op jit(solution)/shard_map/ppermute | solution.py:365
  85.1 14.1 %collective-permute-start.13 = (bf16[2,128,1024]{2,1,0:T(8,128)(2,1)S(1)}, bf16[2,128,1024]{2,1,0:T(8,128)(2,1)S(1)}, u32[]{:S(2)}, u32[]{:S(2)}) collective-permute-start(bf16[2,128,1024]{2,1,0:T(8,128)(2,1)S(1)} %get-tuple-element.87), channel_id=1, source_target_pairs={{0,2},{2,0},{4,6},{6,4},{1,3},{3,1},{5,7},{7,5},{8,10},{10,8},{12,... | collective-permute-start | bytes 1572872 | tf_op jit(solution)/shard_map/ppermute | solution.py:365
  85.1 7.5 %collective-permute-start.20 = (f32[16,1280]{1,0:T(8,128)S(1)}, f32[16,1280]{1,0:T(8,128)S(1)}, u32[]{:S(2)}, u32[]{:S(2)}) collective-permute-start(f32[16,1280]{1,0:T(8,128)S(1)} %get-tuple-element.89.l0), channel_id=1, source_target_pairs={{0,6},{2,4},{4,2},{6,0},{1,7},{3,5},{5,3},{7,1},{8,14},{10,12},{12... | collective-permute-start | bytes 245768 | tf_op jit(solution)/shard_map/ppermute | solution.py:365
  94.6 12.0 %collective-permute-start.21 = (bf16[2,128,1024]{2,1,0:T(8,128)(2,1)S(1)}, bf16[2,128,1024]{2,1,0:T(8,128)(2,1)S(1)}, u32[]{:S(2)}, u32[]{:S(2)}) collective-permute-start(bf16[2,128,1024]{2,1,0:T(8,128)(2,1)S(1)} %get-tuple-element.99), channel_id=1, source_target_pairs={{0,2},{2,0},{4,6},{6,4},{1,3},{3,1},{5,7},{7,5},{8,10},{10,8},{12,... | collective-permute-start | bytes 1572872 | tf_op jit(solution)/shard_map/ppermute | solution.py:365
  99.4 9.0 %collective-permute-start.14 = (bf16[128,1024]{1,0:T(8,128)(2,1)S(1)}, bf16[128,1024]{1,0:T(8,128)(2,1)S(1)}, u32[]{:S(2)}, u32[]{:S(2)}) collective-permute-start(bf16[128,1024]{1,0:T(8,128)(2,1)S(1)} %fusion.9), channel_id=1, source_target_pairs={{0,4},{2,6},{4,0},{6,2},{1,5},{3,7},{5,1},{7,3},{8,12},{10,14},{12... | collective-permute-start | bytes 786440 | tf_op jit(solution)/shard_map/ppermute | solution.py:365
  102.3 7.8 %collective-permute-start.29 = (bf16[80,512]{1,0:T(8,128)(2,1)S(1)}, bf16[80,512]{1,0:T(8,128)(2,1)S(1)}, u32[]{:S(2)}, u32[]{:S(2)}) collective-permute-start(bf16[80,512]{1,0:T(8,128)(2,1)S(1)} %step_pass.1.x0), channel_id=1, source_target_pairs={{0,24},{8,16},{16,8},{24,0},{1,25},{9,17},{17,9},{25,1},{2,26},{10... | collective-permute-start | bytes 245768 | tf_op jit(solution)/shard_map/ppermute | solution.py:365
  104.4 7.6 %collective-permute-start.28 = (bf16[80,512]{1,0:T(8,128)(2,1)S(1)}, bf16[80,512]{1,0:T(8,128)(2,1)S(1)}, u32[]{:S(2)}, u32[]{:S(2)}) collective-permute-start(bf16[80,512]{1,0:T(8,128)(2,1)S(1)} %step_pass.1.x0), channel_id=1, source_target_pairs={{0,16},{8,24},{16,0},{24,8},{1,17},{9,25},{17,1},{25,9},{2,18},{10... | collective-permute-start | bytes 245768 | tf_op jit(solution)/shard_map/ppermute | solution.py:365
  106.8 8.2 %collective-permute-start.22 = (bf16[128,1024]{1,0:T(8,128)(2,1)S(1)}, bf16[128,1024]{1,0:T(8,128)(2,1)S(1)}, u32[]{:S(2)}, u32[]{:S(2)}) collective-permute-start(bf16[128,1024]{1,0:T(8,128)(2,1)S(1)} %fusion.10), channel_id=1, source_target_pairs={{0,4},{2,6},{4,0},{6,2},{1,5},{3,7},{5,1},{7,3},{8,12},{10,14},{12... | collective-permute-start | bytes 786440 | tf_op jit(solution)/shard_map/ppermute | solution.py:365
  108.5 14.5 %collective-permute-start.15 = (bf16[128,1024]{1,0:T(8,128)(2,1)S(1)}, bf16[128,1024]{1,0:T(8,128)(2,1)S(1)}, u32[]{:S(2)}, u32[]{:S(2)}) collective-permute-start(bf16[128,1024]{1,0:T(8,128)(2,1)S(1)} %fusion.8.a0), channel_id=1, source_target_pairs={{0,1},{1,0},{2,3},{3,2},{4,5},{5,4},{6,7},{7,6},{8,9},{9,8},{10,11... | collective-permute-start | bytes 786440 | tf_op jit(solution)/shard_map/ppermute | solution.py:365
  115.1 8.6 %collective-permute-start.23 = (bf16[128,1024]{1,0:T(8,128)(2,1)S(1)}, bf16[128,1024]{1,0:T(8,128)(2,1)S(1)}, u32[]{:S(2)}, u32[]{:S(2)}) collective-permute-start(bf16[128,1024]{1,0:T(8,128)(2,1)S(1)} %fusion.4.b0), channel_id=1, source_target_pairs={{0,1},{1,0},{2,3},{3,2},{4,5},{5,4},{6,7},{7,6},{8,9},{9,8},{10,11... | collective-permute-start | bytes 786440 | tf_op jit(solution)/shard_map/ppermute | solution.py:365
  (16 other events, 197.9 us)

commit v7 on v6

--- a/solution.py
+++ b/solution.py
@@ -411,7 +411,11 @@
     ]
     h, carried = lax.optimization_barrier((h, carried))
     carried = exchange(carried)
-    h_cols = exchange([block_of(h, n_ctx, 1, bits) for bits in range(n_ctx)])
+    h_cols = [block_of(h, n_ctx, 1, bits) for bits in range(n_ctx)]
+    h_cols[1] = swap(h_cols[1], "ctx", 1)
+    h_cols[2], h_cols[3] = after((h_cols[2], h_cols[3]), h_cols[1])
+    h_cols[2] = swap(h_cols[2], "ctx", 2)
+    h_cols[3] = swap(h_cols[3], "ctx", 3)
 
     g, z = gram(at, lengths[0, 0], qk, targets[0, 0])
     carried = after(carried, h_cols[1])

time: 130 us -> 130 us (level)
  no operation moved by 1% of the time
where the time goes in v7:
time: 130 us
  starting transfers between devices  56.2 us (43%)
  waiting for transfers between devices  46.5 us (36%)
  Pallas kernels  14.3 us (11%)
  matrix products  8.96 us (7%)
  local copies, waits for them, and re-layouts  3.02 us (2%)
    ppermute x34, starting transfers between devices, swap(): return lax.ppermute(array, axis, [(i, i ^ bits) for i in range(count)])  56.2 us
    ppermute x34, waiting for transfers between devices, swap(): return lax.ppermute(array, axis, [(i, i ^ bits) for i in range(count)])  46.5 us
    dot_general x3, matrix products, dot(): lax.dot_general(a, b, (((da,), (db,)), ((), ())), preferred_element_type=...  8.96 us
    pallas_call x1, Pallas kernels, gram(): pl.pallas_call(functools.partial(gram_kernel, docs=lengths.shape[0], reac...  5.2 us
    pallas_call x2, Pallas kernels, main_pass(): pl.pallas_call(main_kernel, in_specs=[SMEM] + [VMEM] * 5, out_shape=[stru...  3.04 us
  transfers between devices with their start and end apart: 34, of which 12 were waited for; matrix products, arithmetic and copies ran while one was open for 8% of the time, Pallas kernels for 9%

profile of v7, /device:TPU:0, one launch (start us, length us, event | category | flops | bytes accessed | tf_op | source)
XLA Modules:
  0.0 129.8 jit_solution(8272756571206777426)
XLA Ops:
  2.9 3.1 %collective-permute-start = (bf16[128,1280]{1,0:T(8,128)(2,1)S(1)}, bf16[128,1280]{1,0:T(8,128)(2,1)S(1)}, u32[]{:S(2)}, u32[]{:S(2)}) collective-permute-start(bf16[128,1280]{1,0:T(8,128)(2,1)S(1)} %get-tuple-element.65), channel_id=1, source_target_pairs={{0,8},{8,0},{16,24},{24,16},{1,9},{9,1},{17,25},{25,17},{2,10},{10... | collective-permute-start | bytes 983048 | tf_op jit(solution)/shard_map/ppermute | solution.py:365
  6.0 2.6 %collective-permute-start.1 = (bf16[128,1280]{1,0:T(8,128)(2,1)S(1)}, bf16[128,1280]{1,0:T(8,128)(2,1)S(1)}, u32[]{:S(2)}, u32[]{:S(2)}) collective-permute-start(bf16[128,1280]{1,0:T(8,128)(2,1)S(1)} %get-tuple-element.66), channel_id=1, source_target_pairs={{0,16},{8,24},{16,0},{24,8},{1,17},{9,25},{17,1},{25,9},{2,18},{10... | collective-permute-start | bytes 983048 | tf_op jit(solution)/shard_map/ppermute | solution.py:365
  8.6 11.4 %collective-permute-done.p1 = bf16[128,1280]{1,0:T(8,128)(2,1)S(1)} collective-permute-done((bf16[128,1280]{1,0:T(8,128)(2,1)S(1)}, bf16[128,1280]{1,0:T(8,128)(2,1)S(1)}, u32[]{:S(2)}, u32[]{:S(2)}) %collective-permute-start) | collective-permute-done | bytes 327712 | tf_op jit(solution)/shard_map/ppermute | solution.py:365
  22.7 6.3 %fusion = bf16[128,1024]{0,1:T(8,128)(2,1)S(1)} fusion(f32[128,1024]{0,1:T(8,128)S(1)} %fusion.11, bf16[128,4096]{1,0:T(8,128)(2,1)} %bitcast.43, bf16[4096,1024]{1,0:T(8,128)(2,1)} %param.13), kind=kOutput, calls=%fused_computation.1 | convolution fusion | flops 1074003968 | bytes 10223616 | tf_op jit(solution)/shard_map/dot_general | solution.py:22
  29.9 2.0 %collective-permute-start.3 = (bf16[272,128]{1,0:T(8,128)(2,1)S(1)}, bf16[272,128]{1,0:T(8,128)(2,1)S(1)}, u32[]{:S(2)}, u32[]{:S(2)}) collective-permute-start(bf16[272,128]{1,0:T(8,128)(2,1)S(1)} %get-tuple-element.72), channel_id=1, source_target_pairs={{0,8},{8,0},{16,24},{24,16},{1,9},{9,1},{17,25},{25,17},{2,10},{10... | collective-permute-start | bytes 208904 | tf_op jit(solution)/shard_map/ppermute | solution.py:365
  31.9 1.8 %collective-permute-start.4 = (bf16[272,128]{1,0:T(8,128)(2,1)S(1)}, bf16[272,128]{1,0:T(8,128)(2,1)S(1)}, u32[]{:S(2)}, u32[]{:S(2)}) collective-permute-start(bf16[272,128]{1,0:T(8,128)(2,1)S(1)} %get-tuple-element.73), channel_id=1, source_target_pairs={{0,16},{8,24},{16,0},{24,8},{1,17},{9,25},{17,1},{25,9},{2,18},{10... | collective-permute-start | bytes 208904 | tf_op jit(solution)/shard_map/ppermute | solution.py:365
  33.7 4.7 %collective-permute-done.6.h1 = bf16[128,1024]{1,0:T(8,128)(2,1)S(1)} collective-permute-done((bf16[128,1024]{1,0:T(8,128)(2,1)S(1)}, bf16[128,1024]{1,0:T(8,128)(2,1)S(1)}, u32[]{:S(2)}, u32[]{:S(2)}) %collective-permute-start.6) | collective-permute-done | bytes 262176 | tf_op jit(solution)/shard_map/ppermute | solution.py:365
  38.4 2.7 %collective-permute-start.5 = (bf16[272,128]{1,0:T(8,128)(2,1)S(1)}, bf16[272,128]{1,0:T(8,128)(2,1)S(1)}, u32[]{:S(2)}, u32[]{:S(2)}) collective-permute-start(bf16[272,128]{1,0:T(8,128)(2,1)S(1)} %get-tuple-element.74), channel_id=1, source_target_pairs={{0,24},{8,16},{16,8},{24,0},{1,25},{9,17},{17,9},{25,1},{2,26},{10... | collective-permute-start | bytes 208904 | tf_op jit(solution)/shard_map/ppermute | solution.py:365
  42.9 5.2 %gram.1 = (bf16[2,512,512]{2,1,0:T(8,128)(2,1)S(1)}, f32[2,128,512]{2,1,0:T(8,128)S(1)}) custom-call(s32[2]{0:T(128)S(1)} %pad_add_fusion.at_ref, s32[8]{0:T(128)S(1)} %bitcast.41, bf16[128,1280]{1,0:T(8,128)(2,1)S(1)} %get-tuple-element.64.p0, bf16[128,1280]{1,0:T(8,128)(2,1)S(1)} %collective-permute-done.p1, ...), custom_call_target="tpu_custom_call" | custom-call | flops 4000000000 | bytes 5000000 | tf_op jit(solution)/shard_map/gram/pallas_call | solution.py:103
  49.3 10.2 %collective-permute-start.9 = (bf16[144,512]{1,0:T(8,128)(2,1)S(1)}, bf16[144,512]{1,0:T(8,128)(2,1)S(1)}, u32[]{:S(2)}, u32[]{:S(2)}) collective-permute-start(bf16[144,512]{1,0:T(8,128)(2,1)S(1)} %get-tuple-element.86.m0.p0), channel_id=1, source_target_pairs={{0,24},{8,16},{16,8},{24,0},{1,25},{9,17},{17,9},{25,1},{2,26},{10... | collective-permute-start | bytes 442376 | tf_op jit(solution)/shard_map/ppermute | solution.py:365
  59.6 4.9 %collective-permute-start.8 = (bf16[144,512]{1,0:T(8,128)(2,1)S(1)}, bf16[144,512]{1,0:T(8,128)(2,1)S(1)}, u32[]{:S(2)}, u32[]{:S(2)}) collective-permute-start(bf16[144,512]{1,0:T(8,128)(2,1)S(1)} %get-tuple-element.86.m0.p0), channel_id=1, source_target_pairs={{0,16},{8,24},{16,0},{24,8},{1,17},{9,25},{17,1},{25,9},{2,18},{10... | collective-permute-start | bytes 442376 | tf_op jit(solution)/shard_map/ppermute | solution.py:365
  64.4 13.8 %collective-permute-done.8.m2.p2 = bf16[144,512]{1,0:T(8,128)(2,1)S(1)} collective-permute-done((bf16[144,512]{1,0:T(8,128)(2,1)S(1)}, bf16[144,512]{1,0:T(8,128)(2,1)S(1)}, u32[]{:S(2)}, u32[]{:S(2)}) %collective-permute-start.8) | collective-permute-done | bytes 147488 | tf_op jit(solution)/shard_map/ppermute | solution.py:365
  79.2 2.5 %collective-permute-start.18 = (bf16[128,512]{1,0:T(8,128)(2,1)S(1)}, bf16[128,512]{1,0:T(8,128)(2,1)S(1)}, u32[]{:S(2)}, u32[]{:S(2)}) collective-permute-start(bf16[128,512]{1,0:T(8,128)(2,1)S(1)} %get-tuple-element.98.p0), channel_id=1, source_target_pairs={{0,24},{8,16},{16,8},{24,0},{1,25},{9,17},{17,9},{25,1},{2,26},{10... | collective-permute-start | bytes 393224 | tf_op jit(solution)/shard_map/ppermute | solution.py:365
  81.7 1.9 %collective-permute-start.16 = (bf16[128,512]{1,0:T(8,128)(2,1)S(1)}, bf16[128,512]{1,0:T(8,128)(2,1)S(1)}, u32[]{:S(2)}, u32[]{:S(2)}) collective-permute-start(bf16[128,512]{1,0:T(8,128)(2,1)S(1)} %get-tuple-element.98.p0), channel_id=1, source_target_pairs={{0,8},{8,0},{16,24},{24,16},{1,9},{9,1},{17,25},{25,17},{2,10},{10... | collective-permute-start | bytes 393224 | tf_op jit(solution)/shard_map/ppermute | solution.py:365
  89.0 3.6 %collective-permute-done.17.p2 = bf16[128,512]{1,0:T(8,128)(2,1)S(1)} collective-permute-done((bf16[128,512]{1,0:T(8,128)(2,1)S(1)}, bf16[128,512]{1,0:T(8,128)(2,1)S(1)}, u32[]{:S(2)}, u32[]{:S(2)}) %collective-permute-start.17) | collective-permute-done | bytes 131104 | tf_op jit(solution)/shard_map/ppermute | solution.py:365
  94.8 2.3 %collective-permute-start.26 = (bf16[32,512]{1,0:T(8,128)(2,1)S(1)}, bf16[32,512]{1,0:T(8,128)(2,1)S(1)}, u32[]{:S(2)}, u32[]{:S(2)}) collective-permute-start(bf16[32,512]{1,0:T(8,128)(2,1)S(1)} %get-tuple-element.104.s0), channel_id=1, source_target_pairs={{0,24},{8,16},{16,8},{24,0},{1,25},{9,17},{17,9},{25,1},{2,26},{10... | collective-permute-start | bytes 98312 | tf_op jit(solution)/shard_map/ppermute | solution.py:365
  102.4 2.0 %collective-permute-start.29 = (bf16[80,512]{1,0:T(8,128)(2,1)S(1)}, bf16[80,512]{1,0:T(8,128)(2,1)S(1)}, u32[]{:S(2)}, u32[]{:S(2)}) collective-permute-start(bf16[80,512]{1,0:T(8,128)(2,1)S(1)} %step_pass.1.x0), channel_id=1, source_target_pairs={{0,24},{8,16},{16,8},{24,0},{1,25},{9,17},{17,9},{25,1},{2,26},{10... | collective-permute-start | bytes 245768 | tf_op jit(solution)/shard_map/ppermute | solution.py:365
  104.9 1.9 %collective-permute-start.27 = (bf16[80,512]{1,0:T(8,128)(2,1)S(1)}, bf16[80,512]{1,0:T(8,128)(2,1)S(1)}, u32[]{:S(2)}, u32[]{:S(2)}) collective-permute-start(bf16[80,512]{1,0:T(8,128)(2,1)S(1)} %step_pass.1.x0), channel_id=1, source_target_pairs={{0,8},{8,0},{16,24},{24,16},{1,9},{9,1},{17,25},{25,17},{2,10},{10... | collective-permute-start | bytes 245768 | tf_op jit(solution)/shard_map/ppermute | solution.py:365
  106.9 1.8 %collective-permute-start.22 = (bf16[128,1024]{1,0:T(8,128)(2,1)S(1)}, bf16[128,1024]{1,0:T(8,128)(2,1)S(1)}, u32[]{:S(2)}, u32[]{:S(2)}) collective-permute-start(bf16[128,1024]{1,0:T(8,128)(2,1)S(1)} %fusion.10), channel_id=1, source_target_pairs={{0,4},{2,6},{4,0},{6,2},{1,5},{3,7},{5,1},{7,3},{8,12},{10,14},{12... | collective-permute-start | bytes 786440 | tf_op jit(solution)/shard_map/ppermute | solution.py:365
  113.2 2.1 %collective-permute-start.31 = (bf16[64,1024]{1,0:T(8,128)(2,1)S(1)}, bf16[64,1024]{1,0:T(8,128)(2,1)S(1)}, u32[]{:S(2)}, u32[]{:S(2)}) collective-permute-start(bf16[64,1024]{1,0:T(8,128)(2,1)S(1)} %get-tuple-element.116), channel_id=1, source_target_pairs={{0,4},{2,6},{4,0},{6,2},{1,5},{3,7},{5,1},{7,3},{8,12},{10,14},{12... | collective-permute-start | bytes 393224 | tf_op jit(solution)/shard_map/ppermute | solution.py:365
  115.4 1.8 %collective-permute-start.23 = (bf16[128,1024]{1,0:T(8,128)(2,1)S(1)}, bf16[128,1024]{1,0:T(8,128)(2,1)S(1)}, u32[]{:S(2)}, u32[]{:S(2)}) collective-permute-start(bf16[128,1024]{1,0:T(8,128)(2,1)S(1)} %fusion.4.b0), channel_id=1, source_target_pairs={{0,1},{1,0},{2,3},{3,2},{4,5},{5,4},{6,7},{7,6},{8,9},{9,8},{10,11... | collective-permute-start | bytes 786440 | tf_op jit(solution)/shard_map/ppermute | solution.py:365
  117.3 2.4 %collective-permute-done.31.r2 = bf16[64,1024]{1,0:T(8,128)(2,1)S(1)} collective-permute-done((bf16[64,1024]{1,0:T(8,128)(2,1)S(1)}, bf16[64,1024]{1,0:T(8,128)(2,1)S(1)}, u32[]{:S(2)}, u32[]{:S(2)}) %collective-permute-start.31) | collective-permute-done | bytes 131104 | tf_op jit(solution)/shard_map/ppermute | solution.py:365
  119.6 2.3 %collective-permute-done.32.r3 = bf16[64,1024]{1,0:T(8,128)(2,1)S(1)} collective-permute-done((bf16[64,1024]{1,0:T(8,128)(2,1)S(1)}, bf16[64,1024]{1,0:T(8,128)(2,1)S(1)}, u32[]{:S(2)}, u32[]{:S(2)}) %collective-permute-start.32) | collective-permute-done | bytes 131104 | tf_op jit(solution)/shard_map/ppermute | solution.py:365
  124.1 4.1 %collective-permute-done.33.l1 = bf16[72,1024]{1,0:T(8,128)(2,1)S(1)} collective-permute-done((bf16[72,1024]{1,0:T(8,128)(2,1)S(1)}, bf16[72,1024]{1,0:T(8,128)(2,1)S(1)}, u32[]{:S(2)}, u32[]{:S(2)}) %collective-permute-start.33) | collective-permute-done | bytes 147488 | tf_op jit(solution)/shard_map/ppermute | solution.py:365
  (81 shorter events, 32.0 us)
Async XLA Ops:
  2.9 17.1 %collective-permute-start = (bf16[128,1280]{1,0:T(8,128)(2,1)S(1)}, bf16[128,1280]{1,0:T(8,128)(2,1)S(1)}, u32[]{:S(2)}, u32[]{:S(2)}) collective-permute-start(bf16[128,1280]{1,0:T(8,128)(2,1)S(1)} %get-tuple-element.65), channel_id=1, source_target_pairs={{0,8},{8,0},{16,24},{24,16},{1,9},{9,1},{17,25},{25,17},{2,10},{10... | collective-permute-start | bytes 983048 | tf_op jit(solution)/shard_map/ppermute | solution.py:365
  6.0 35.1 %collective-permute-start.1 = (bf16[128,1280]{1,0:T(8,128)(2,1)S(1)}, bf16[128,1280]{1,0:T(8,128)(2,1)S(1)}, u32[]{:S(2)}, u32[]{:S(2)}) collective-permute-start(bf16[128,1280]{1,0:T(8,128)(2,1)S(1)} %get-tuple-element.66), channel_id=1, source_target_pairs={{0,16},{8,24},{16,0},{24,8},{1,17},{9,25},{17,1},{25,9},{2,18},{10... | collective-permute-start | bytes 983048 | tf_op jit(solution)/shard_map/ppermute | solution.py:365
  8.6 32.5 %collective-permute-start.2 = (bf16[128,1280]{1,0:T(8,128)(2,1)S(1)}, bf16[128,1280]{1,0:T(8,128)(2,1)S(1)}, u32[]{:S(2)}, u32[]{:S(2)}) collective-permute-start(bf16[128,1280]{1,0:T(8,128)(2,1)S(1)} %get-tuple-element.67), channel_id=1, source_target_pairs={{0,24},{8,16},{16,8},{24,0},{1,25},{9,17},{17,9},{25,1},{2,26},{10... | collective-permute-start | bytes 983048 | tf_op jit(solution)/shard_map/ppermute | solution.py:365
  29.2 9.3 %collective-permute-start.6 = (bf16[128,1024]{1,0:T(8,128)(2,1)S(1)}, bf16[128,1024]{1,0:T(8,128)(2,1)S(1)}, u32[]{:S(2)}, u32[]{:S(2)}) collective-permute-start(bf16[128,1024]{1,0:T(8,128)(2,1)S(1)} %get-tuple-element.126), channel_id=1, source_target_pairs={{0,8},{8,0},{16,24},{24,16},{1,9},{9,1},{17,25},{25,17},{2,10},{10... | collective-permute-start | bytes 786440 | tf_op jit(solution)/shard_map/ppermute | solution.py:365
  29.9 18.1 %collective-permute-start.3 = (bf16[272,128]{1,0:T(8,128)(2,1)S(1)}, bf16[272,128]{1,0:T(8,128)(2,1)S(1)}, u32[]{:S(2)}, u32[]{:S(2)}) collective-permute-start(bf16[272,128]{1,0:T(8,128)(2,1)S(1)} %get-tuple-element.72), channel_id=1, source_target_pairs={{0,8},{8,0},{16,24},{24,16},{1,9},{9,1},{17,25},{25,17},{2,10},{10... | collective-permute-start | bytes 208904 | tf_op jit(solution)/shard_map/ppermute | solution.py:365
  31.9 16.2 %collective-permute-start.4 = (bf16[272,128]{1,0:T(8,128)(2,1)S(1)}, bf16[272,128]{1,0:T(8,128)(2,1)S(1)}, u32[]{:S(2)}, u32[]{:S(2)}) collective-permute-start(bf16[272,128]{1,0:T(8,128)(2,1)S(1)} %get-tuple-element.73), channel_id=1, source_target_pairs={{0,16},{8,24},{16,0},{24,8},{1,17},{9,25},{17,1},{25,9},{2,18},{10... | collective-permute-start | bytes 208904 | tf_op jit(solution)/shard_map/ppermute | solution.py:365
  38.4 9.7 %collective-permute-start.5 = (bf16[272,128]{1,0:T(8,128)(2,1)S(1)}, bf16[272,128]{1,0:T(8,128)(2,1)S(1)}, u32[]{:S(2)}, u32[]{:S(2)}) collective-permute-start(bf16[272,128]{1,0:T(8,128)(2,1)S(1)} %get-tuple-element.74), channel_id=1, source_target_pairs={{0,24},{8,16},{16,8},{24,0},{1,25},{9,17},{17,9},{25,1},{2,26},{10... | collective-permute-start | bytes 208904 | tf_op jit(solution)/shard_map/ppermute | solution.py:365
  41.1 37.2 %collective-permute-start.10 = (bf16[128,1024]{1,0:T(8,128)(2,1)S(1)}, bf16[128,1024]{1,0:T(8,128)(2,1)S(1)}, u32[]{:S(2)}, u32[]{:S(2)}) collective-permute-start(bf16[128,1024]{1,0:T(8,128)(2,1)S(1)} %get-tuple-element.81), channel_id=1, source_target_pairs={{0,16},{8,24},{16,0},{24,8},{1,17},{9,25},{17,1},{25,9},{2,18},{10... | collective-permute-start | bytes 786440 | tf_op jit(solution)/shard_map/ppermute | solution.py:365
  41.1 37.2 %collective-permute-start.11 = (bf16[128,1024]{1,0:T(8,128)(2,1)S(1)}, bf16[128,1024]{1,0:T(8,128)(2,1)S(1)}, u32[]{:S(2)}, u32[]{:S(2)}) collective-permute-start(bf16[128,1024]{1,0:T(8,128)(2,1)S(1)} %get-tuple-element.82), channel_id=1, source_target_pairs={{0,24},{8,16},{16,8},{24,0},{1,25},{9,17},{17,9},{25,1},{2,26},{10... | collective-permute-start | bytes 786440 | tf_op jit(solution)/shard_map/ppermute | solution.py:365
  49.3 15.1 %collective-permute-start.9 = (bf16[144,512]{1,0:T(8,128)(2,1)S(1)}, bf16[144,512]{1,0:T(8,128)(2,1)S(1)}, u32[]{:S(2)}, u32[]{:S(2)}) collective-permute-start(bf16[144,512]{1,0:T(8,128)(2,1)S(1)} %get-tuple-element.86.m0.p0), channel_id=1, source_target_pairs={{0,24},{8,16},{16,8},{24,0},{1,25},{9,17},{17,9},{25,1},{2,26},{10... | collective-permute-start | bytes 442376 | tf_op jit(solution)/shard_map/ppermute | solution.py:365
  59.6 18.7 %collective-permute-start.8 = (bf16[144,512]{1,0:T(8,128)(2,1)S(1)}, bf16[144,512]{1,0:T(8,128)(2,1)S(1)}, u32[]{:S(2)}, u32[]{:S(2)}) collective-permute-start(bf16[144,512]{1,0:T(8,128)(2,1)S(1)} %get-tuple-element.86.m0.p0), channel_id=1, source_target_pairs={{0,16},{8,24},{16,0},{24,8},{1,17},{9,25},{17,1},{25,9},{2,18},{10... | collective-permute-start | bytes 442376 | tf_op jit(solution)/shard_map/ppermute | solution.py:365
  64.4 13.8 %collective-permute-start.7 = (bf16[144,512]{1,0:T(8,128)(2,1)S(1)}, bf16[144,512]{1,0:T(8,128)(2,1)S(1)}, u32[]{:S(2)}, u32[]{:S(2)}) collective-permute-start(bf16[144,512]{1,0:T(8,128)(2,1)S(1)} %get-tuple-element.86.m0.p0), channel_id=1, source_target_pairs={{0,8},{8,0},{16,24},{24,16},{1,9},{9,1},{17,25},{25,17},{2,10},{10... | collective-permute-start | bytes 442376 | tf_op jit(solution)/shard_map/ppermute | solution.py:365
  79.2 8.4 %collective-permute-start.18 = (bf16[128,512]{1,0:T(8,128)(2,1)S(1)}, bf16[128,512]{1,0:T(8,128)(2,1)S(1)}, u32[]{:S(2)}, u32[]{:S(2)}) collective-permute-start(bf16[128,512]{1,0:T(8,128)(2,1)S(1)} %get-tuple-element.98.p0), channel_id=1, source_target_pairs={{0,24},{8,16},{16,8},{24,0},{1,25},{9,17},{17,9},{25,1},{2,26},{10... | collective-permute-start | bytes 393224 | tf_op jit(solution)/shard_map/ppermute | solution.py:365
  81.7 11.0 %collective-permute-start.17 = (bf16[128,512]{1,0:T(8,128)(2,1)S(1)}, bf16[128,512]{1,0:T(8,128)(2,1)S(1)}, u32[]{:S(2)}, u32[]{:S(2)}) collective-permute-start(bf16[128,512]{1,0:T(8,128)(2,1)S(1)} %get-tuple-element.98.p0), channel_id=1, source_target_pairs={{0,16},{8,24},{16,0},{24,8},{1,17},{9,25},{17,1},{25,9},{2,18},{10... | collective-permute-start | bytes 393224 | tf_op jit(solution)/shard_map/ppermute | solution.py:365
  81.7 11.0 %collective-permute-start.16 = (bf16[128,512]{1,0:T(8,128)(2,1)S(1)}, bf16[128,512]{1,0:T(8,128)(2,1)S(1)}, u32[]{:S(2)}, u32[]{:S(2)}) collective-permute-start(bf16[128,512]{1,0:T(8,128)(2,1)S(1)} %get-tuple-element.98.p0), channel_id=1, source_target_pairs={{0,8},{8,0},{16,24},{24,16},{1,9},{9,1},{17,25},{25,17},{2,10},{10... | collective-permute-start | bytes 393224 | tf_op jit(solution)/shard_map/ppermute | solution.py:365
  85.0 14.2 %collective-permute-start.13 = (bf16[2,128,1024]{2,1,0:T(8,128)(2,1)S(1)}, bf16[2,128,1024]{2,1,0:T(8,128)(2,1)S(1)}, u32[]{:S(2)}, u32[]{:S(2)}) collective-permute-start(bf16[2,128,1024]{2,1,0:T(8,128)(2,1)S(1)} %get-tuple-element.91), channel_id=1, source_target_pairs={{0,2},{2,0},{4,6},{6,4},{1,3},{3,1},{5,7},{7,5},{8,10},{10,8},{12,... | collective-permute-start | bytes 1572872 | tf_op jit(solution)/shard_map/ppermute | solution.py:365
  85.1 7.5 %collective-permute-start.20 = (f32[16,1280]{1,0:T(8,128)S(1)}, f32[16,1280]{1,0:T(8,128)S(1)}, u32[]{:S(2)}, u32[]{:S(2)}) collective-permute-start(f32[16,1280]{1,0:T(8,128)S(1)} %get-tuple-element.93.l0), channel_id=1, source_target_pairs={{0,6},{2,4},{4,2},{6,0},{1,7},{3,5},{5,3},{7,1},{8,14},{10,12},{12... | collective-permute-start | bytes 245768 | tf_op jit(solution)/shard_map/ppermute | solution.py:365
  94.7 12.1 %collective-permute-start.21 = (bf16[2,128,1024]{2,1,0:T(8,128)(2,1)S(1)}, bf16[2,128,1024]{2,1,0:T(8,128)(2,1)S(1)}, u32[]{:S(2)}, u32[]{:S(2)}) collective-permute-start(bf16[2,128,1024]{2,1,0:T(8,128)(2,1)S(1)} %get-tuple-element.103), channel_id=1, source_target_pairs={{0,2},{2,0},{4,6},{6,4},{1,3},{3,1},{5,7},{7,5},{8,10},{10,8},{12,... | collective-permute-start | bytes 1572872 | tf_op jit(solution)/shard_map/ppermute | solution.py:365
  99.4 9.4 %collective-permute-start.14 = (bf16[128,1024]{1,0:T(8,128)(2,1)S(1)}, bf16[128,1024]{1,0:T(8,128)(2,1)S(1)}, u32[]{:S(2)}, u32[]{:S(2)}) collective-permute-start(bf16[128,1024]{1,0:T(8,128)(2,1)S(1)} %fusion.9), channel_id=1, source_target_pairs={{0,4},{2,6},{4,0},{6,2},{1,5},{3,7},{5,1},{7,3},{8,12},{10,14},{12... | collective-permute-start | bytes 786440 | tf_op jit(solution)/shard_map/ppermute | solution.py:365
  102.4 8.1 %collective-permute-start.29 = (bf16[80,512]{1,0:T(8,128)(2,1)S(1)}, bf16[80,512]{1,0:T(8,128)(2,1)S(1)}, u32[]{:S(2)}, u32[]{:S(2)}) collective-permute-start(bf16[80,512]{1,0:T(8,128)(2,1)S(1)} %step_pass.1.x0), channel_id=1, source_target_pairs={{0,24},{8,16},{16,8},{24,0},{1,25},{9,17},{17,9},{25,1},{2,26},{10... | collective-permute-start | bytes 245768 | tf_op jit(solution)/shard_map/ppermute | solution.py:365
  104.4 7.6 %collective-permute-start.28 = (bf16[80,512]{1,0:T(8,128)(2,1)S(1)}, bf16[80,512]{1,0:T(8,128)(2,1)S(1)}, u32[]{:S(2)}, u32[]{:S(2)}) collective-permute-start(bf16[80,512]{1,0:T(8,128)(2,1)S(1)} %step_pass.1.x0), channel_id=1, source_target_pairs={{0,16},{8,24},{16,0},{24,8},{1,17},{9,25},{17,1},{25,9},{2,18},{10... | collective-permute-start | bytes 245768 | tf_op jit(solution)/shard_map/ppermute | solution.py:365
  106.9 8.4 %collective-permute-start.22 = (bf16[128,1024]{1,0:T(8,128)(2,1)S(1)}, bf16[128,1024]{1,0:T(8,128)(2,1)S(1)}, u32[]{:S(2)}, u32[]{:S(2)}) collective-permute-start(bf16[128,1024]{1,0:T(8,128)(2,1)S(1)} %fusion.10), channel_id=1, source_target_pairs={{0,4},{2,6},{4,0},{6,2},{1,5},{3,7},{5,1},{7,3},{8,12},{10,14},{12... | collective-permute-start | bytes 786440 | tf_op jit(solution)/shard_map/ppermute | solution.py:365
  108.9 14.7 %collective-permute-start.15 = (bf16[128,1024]{1,0:T(8,128)(2,1)S(1)}, bf16[128,1024]{1,0:T(8,128)(2,1)S(1)}, u32[]{:S(2)}, u32[]{:S(2)}) collective-permute-start(bf16[128,1024]{1,0:T(8,128)(2,1)S(1)} %fusion.8.a0), channel_id=1, source_target_pairs={{0,1},{1,0},{2,3},{3,2},{4,5},{5,4},{6,7},{7,6},{8,9},{9,8},{10,11... | collective-permute-start | bytes 786440 | tf_op jit(solution)/shard_map/ppermute | solution.py:365
  115.4 8.7 %collective-permute-start.23 = (bf16[128,1024]{1,0:T(8,128)(2,1)S(1)}, bf16[128,1024]{1,0:T(8,128)(2,1)S(1)}, u32[]{:S(2)}, u32[]{:S(2)}) collective-permute-start(bf16[128,1024]{1,0:T(8,128)(2,1)S(1)} %fusion.4.b0), channel_id=1, source_target_pairs={{0,1},{1,0},{2,3},{3,2},{4,5},{5,4},{6,7},{7,6},{8,9},{9,8},{10,11... | collective-permute-start | bytes 786440 | tf_op jit(solution)/shard_map/ppermute | solution.py:365
  (16 other events, 181.8 us)
